TPU v7x, 256 devices: a whole 4x4x8 slice. The times are simulated.
256 devices in a mesh: rep: 16 (over y, x), fsdp: 16 (over z, core).
Axes of the slice: x: 4, y: 4, z: 8, core: 2. Of those that a mesh axis runs over, the one named last changes fastest.
Arguments:
- hidden_acts: bfloat16 [16, 8192, 512], P('rep', 'fsdp'), may hold values from -6 to 6
- out_grads: bfloat16 [16, 8192, 8192], P('rep', 'fsdp'), may hold values from -0.15625 to 0.15625
- anchor: float32 [512, 8192], P('fsdp'), may hold values from -6 to 6
- drift: float32 [16, 512, 8192], P('rep', 'fsdp'), may hold values from -120 to 120, as said below
- adam_first: float32 [16, 512, 8192], P('rep', 'fsdp'), may hold values from -6 to 6
- adam_second: float32 [16, 512, 8192], P('rep', 'fsdp'), may hold values from 0.3 to 3
- outer_momentum: float32 [512, 8192], P('fsdp'), may hold values from -6 to 6
Outputs:
- new_first: float32 [16, 512, 8192], P('rep', 'fsdp')
- new_second: float32 [16, 512, 8192], P('rep', 'fsdp')
- new_momentum: float32 [512, 8192], P('fsdp')
- new_anchor: float32 [512, 8192], P('fsdp')
Inputs may be any that keep to these rules, and one draw needn't show every extreme that they name: drift entries are finite reals.
All inputs are finite; a program needn't handle non-finite values.
Results may differ from a plain program's by a relative error of at most 0.0003.
Values sent between devices are 32-bit elements; how exact they have to be, the bound alone decides.
No kernel may reach another device: no remote copies, remote signals or barrier semaphores. Data moves between devices by JAX's collectives and lax.ppermute only.
A program may use at most 128 MiB of HBM per device.

v0:
```python
import math

import jax
import jax.numpy as jnp
from jax import lax
from jax.sharding import PartitionSpec as P

D = 8192
INNER_STEP = 100


beta_first = 0.9
beta_second = 0.95
inner_rate = 0.5
decay_weight = 0.1
outer_rate = 0.7
momentum_coef = 0.9


def outer_update(average, squares, ceiling, momentum_old, anchor_old):
    factor = ceiling / jnp.maximum(jnp.sqrt(squares), ceiling)
    momentum = momentum_coef * momentum_old + factor * average
    updated = anchor_old - outer_rate * (factor * average + momentum_coef * momentum)
    return (momentum, updated)


def per_device(hidden_acts, out_grads, anchor, drift, adam_first, adam_second, outer_momentum):
    activations = hidden_acts[0]
    cotangent = out_grads[0]
    rows_dev = anchor.shape[0]
    gradient = lax.psum_scatter(
        lax.dot_general(
            activations, cotangent, (((0,), (0,)), ((), ())), preferred_element_type=jnp.float32
        ),
        "fsdp",
        scatter_dimension=0,
        tiled=True,
    )
    correction_one = 1.0 - beta_first**INNER_STEP
    correction_two = 1.0 - beta_second**INNER_STEP
    own_drift = drift[0]
    moment_one = beta_first * adam_first[0] + (1.0 - beta_first) * gradient
    moment_two = beta_second * adam_second[0] + (1.0 - beta_second) * gradient * gradient
    update = moment_one / correction_one / (
        jnp.sqrt(moment_two / correction_two) + 1e-08
    ) + decay_weight * (anchor + own_drift)
    pseudo = inner_rate * update - own_drift
    replicas = lax.axis_size("rep")
    ceiling = 0.3 * math.sqrt(rows_dev * lax.axis_size("fsdp") * D)
    average = lax.psum(pseudo, "rep") / replicas
    squares = lax.psum(jnp.sum(average * average), "fsdp")
    momentum, updated = outer_update(average, squares, ceiling, outer_momentum, anchor)
    return (moment_one[None], moment_two[None], momentum, updated)


def solution(mesh):
    return jax.shard_map(
        per_device,
        mesh=mesh,
        in_specs=(
            P("rep", "fsdp", None),
            P("rep", "fsdp", None),
            P("fsdp", None),
            P("rep", "fsdp", None),
            P("rep", "fsdp", None),
            P("rep", "fsdp", None),
            P("fsdp", None),
        ),
        out_specs=(
            P("rep", "fsdp", None),
            P("rep", "fsdp", None),
            P("fsdp", None),
            P("fsdp", None),
        ),
        check_vma=False,
    )
```

profile of v0, /device:TPU:1, one launch (start us, length us, event | category | flops | bytes accessed | tf_op | source)
XLA Modules:
  0.0 261.7 jit_solution(1608500180151418882)
XLA Ops:
  7.2 0.0 copy-start
  7.2 0.0 reduce-scatter.2.cloned.1.call-start
  7.2 1.0 copy-done
  8.2 11.5 %fusion = f32[512,8192]{1,0:T(8,128)} fusion(bf16[1,512,8192]{2,1,0:T(8,128)(2,1)} %param.8, bf16[1,512,512]{2,1,0:T(8,128)(2,1)S(1)} %copy-done), kind=kOutput, calls=%fused_computation | convolution fusion | flops 4294967296 | bytes 25690112 | tf_op jit(solution)/shard_map/dot_general | solution.py:32
  19.7 0.0 copy-start.1
  19.7 0.0 reduce-scatter.2.cloned.1.call-update
  19.7 0.0 copy-start.2
  19.7 0.0 all-reduce.2.cloned.1.call-start
  19.8 103.3 %reduce-scatter.2.cloned.1.call-done = f32[32,8192]{1,0:T(8,128)} async-done(((f32[512,8192]{1,0:T(8,128)}), f32[32,8192]{1,0:T(8,128)}) %reduce-scatter.2.cloned.1.call-update) | async-done | bytes 1048592 | tf_op jit(solution)/shard_map/reduce_scatter | solution.py:31
  123.1 0.0 copy-done.1
  123.1 4.3 %bitcast_subtract_fusion = (f32[32,8192]{1,0:T(8,128)}, f32[1,32,8192]{2,1,0:T(8,128)}, f32[1,32,8192]{2,1,0:T(8,128)}) fusion(f32[1,32,8192]{2,1,0:T(8,128)} %param.10, f32[32,8192]{1,0:T(8,128)S(1)} %copy-done.1, f32[32,8192]{1,0:T(8,128)} %reduce-scatter.2.cloned.1.call-done, f32[1,32,8192]{2,1,0:T(8,128)} %param.11, f32[1,32,8192]{2,1,0:T(8,128)} %param.12), kind=kLoop, calls=%fused_computation.4 | loop fusion | flops 4194304 | bytes 8388608 | tf_op jit(solution)/shard_map/sub | solution.py:47
  127.5 0.0 all-reduce.2.cloned.1.call-update
  127.5 95.5 %all-reduce.2.cloned.1.call-done = f32[32,8192]{1,0:T(8,128)} async-done(((f32[32,8192]{1,0:T(8,128)}), f32[32,8192]{1,0:T(8,128)}) %all-reduce.2.cloned.1.call-update) | async-done | bytes 1048592 | tf_op jit(solution)/shard_map/psum | solution.py:50
  223.0 2.1 multiply_reduce_fusion
  225.1 26.2 %psum.15 = f32[]{:T(128)} all-reduce(f32[]{:T(128)} %multiply_reduce_fusion), channel_id=1, replica_groups=mesh['rep'=16,'fsdp'=16] {'fsdp'}, use_global_device_ids=true, to_apply=%region_3.0 | all-reduce | flops 1 | bytes 8 | tf_op jit(solution)/shard_map/psum | solution.py:51
  252.0 0.0 copy-done.2
  252.0 2.8 %multiply_subtract_fusion = (f32[32,8192]{1,0:T(8,128)}, f32[32,8192]{1,0:T(8,128)}) fusion(f32[32,8192]{1,0:T(8,128)S(1)} %copy-done.1, f32[32,8192]{1,0:T(8,128)} %all-reduce.2.cloned.1.call-done, f32[]{:T(128)S(6)} %mul.75, f32[32,8192]{1,0:T(8,128)S(1)} %copy-done.2), kind=kLoop, calls=%fused_computation.10 | loop fusion | flops 1835008 | bytes 5242884 | tf_op jit(solution)/shard_map/sub | solution.py:23
Async XLA Ops:
  7.2 1.0 copy-start
  7.2 115.9 %reduce-scatter.2.cloned.1.call-start = ((), (), s32[]{:S(2)}) async-start(), calls=%async_computation.1 | async-start | bytes 17825792 | tf_op jit(solution)/shard_map/reduce_scatter | solution.py:31
  19.7 103.4 %copy-start.1 = (f32[32,8192]{1,0:T(8,128)S(1)}, f32[32,8192]{1,0:T(8,128)}, u32[]{:S(2)}) copy-start(f32[32,8192]{1,0:T(8,128)} %param.9) | copy-start | bytes 3145732
  19.7 232.3 %copy-start.2 = (f32[32,8192]{1,0:T(8,128)S(1)}, f32[32,8192]{1,0:T(8,128)}, u32[]{:S(2)}) copy-start(f32[32,8192]{1,0:T(8,128)} %param.13) | copy-start | bytes 3145732
  19.7 203.3 %all-reduce.2.cloned.1.call-start = ((), (), s32[]{:S(2)}) async-start(), calls=%async_computation.2 | async-start | bytes 2097152 | tf_op jit(solution)/shard_map/psum | solution.py:50
Sparse Core Ops, SparseCore 0:
  19.8 103.2 reduce-scatter.1
  127.6 95.3 all-reduce.1
where the time goes:
time: 262 us
  waiting for transfers between devices  199 us (76%)
  blocking collectives  26.2 us (10%)
  between operations  14.8 us (6%)
  matrix products  11.5 us (4%)
  other arithmetic  9.23 us (4%)
    reduce_scatter x1, waiting for transfers between devices, per_device(): lax.psum_scatter(lax.dot_general(activations, cotangent, (((0,), (0,)), (...  103 us
    psum x1, waiting for transfers between devices, per_device(): average = lax.psum(pseudo, 'rep') / replicas  95.5 us
    psum x1, blocking collectives, per_device(): squares = lax.psum(jnp.sum(average * average), 'fsdp')  26.2 us
    dot_general x1, matrix products, per_device(): lax.dot_general(activations, cotangent, (((0,), (0,)), ((), ())), preferr...  11.5 us
  transfers between devices with their start and end apart: 2, of which 2 were waited for; matrix products, arithmetic and copies ran while one was open for 0% of the time, Pallas kernels for 0%

commit v1 on v0

v1 whole, which is shorter than its diff:
```python
import math

import jax
import jax.numpy as jnp
from jax import lax
from jax.sharding import Mesh, PartitionSpec as P

D = 8192
INNER_STEP = 100

beta_first = 0.9
beta_second = 0.95
inner_rate = 0.5
decay_weight = 0.1
outer_rate = 0.7
momentum_coef = 0.9

Y, X, Z, C = 4, 4, 8, 2
ROWS_DEV = 32
PARTS = Z * C
CHUNKS = 4
WIDTH = D // CHUNKS
HALF = WIDTH // 2
UP = [(i, (i + 1) % Z) for i in range(Z)]
DOWN = [(i, (i - 1) % Z) for i in range(Z)]
SWAP = [(0, 1), (1, 0)]


def reorder_rows(activations, z, c):
    rows = Z * C * ROWS_DEV
    place = lax.broadcasted_iota(jnp.int32, (rows, rows), 1)
    source = lax.broadcasted_iota(jnp.int32, (rows, rows), 0)
    mine = place // (Z * ROWS_DEV)
    core = jnp.where(mine == 1, c, 1 - c)
    step = (place // ROWS_DEV) % Z
    wanted = (((z + step) % Z) * C + core) * ROWS_DEV + place % ROWS_DEV
    pick = (wanted == source).astype(activations.dtype)
    return lax.dot_general(
        pick, activations, (((0,), (1,)), ((), ())), preferred_element_type=jnp.float32
    ).astype(activations.dtype)


def per_device(hidden_acts, out_grads, anchor, drift, adam_first, adam_second, outer_momentum):
    z = lax.axis_index("z")
    c = lax.axis_index("c")
    ordered = reorder_rows(hidden_acts[0], z, c)
    cotangent = out_grads[0]
    half_rows = Z * ROWS_DEV
    theirs, mine = ordered[:half_rows], ordered[half_rows:]

    def product(lhs, rhs):
        return lax.dot_general(lhs, rhs, (((1,), (0,)), ((), ())), preferred_element_type=jnp.float32)

    def ring(k, gate):
        cols = lax.slice_in_dim(cotangent, k * WIDTH, (k + 1) * WIDTH, axis=1)
        sent = product(theirs, cols)
        got = lax.ppermute(sent, "c", SWAP)
        kept = product(mine, cols)
        if gate is not None:
            got, _ = lax.optimization_barrier((got, gate))

        def own(j, lo=0, hi=WIDTH):
            j = j % Z
            r = slice(j * ROWS_DEV, (j + 1) * ROWS_DEV)
            return kept[r, lo:hi] + got[r, lo:hi]

        up = own(4, HALF, WIDTH)
        down = own(4, 0, HALF)
        for t in range(4):
            up = lax.ppermute(up, "z", UP)
            down = lax.ppermute(down, "z", DOWN)
            if t == 0:
                up = jnp.concatenate([own(3, 0, HALF), own(3, HALF, WIDTH) + up], axis=1)
                down = jnp.concatenate([own(5, 0, HALF) + down, own(5, HALF, WIDTH)], axis=1)
            elif t < 3:
                up = own(3 - t) + up
                down = own(5 + t) + down
            yield None
        yield own(0) + up + down

    done = [None] * CHUNKS
    for first in range(0, CHUNKS, 2):
        gate = None if first == 0 else done[first - 2][:8, :128]
        rings = [ring(k, gate) for k in (first, first + 1)]
        for t in range(5):
            for i in range(2):
                done[first + i] = next(rings[i])

    gradient = jnp.concatenate(done, axis=1)
    correction_one = 1.0 - beta_first**INNER_STEP
    correction_two = 1.0 - beta_second**INNER_STEP
    own_drift = drift[0]
    moment_one = beta_first * adam_first[0] + (1.0 - beta_first) * gradient
    moment_two = beta_second * adam_second[0] + (1.0 - beta_second) * gradient * gradient
    update = moment_one / correction_one / (
        jnp.sqrt(moment_two / correction_two) + 1e-08
    ) + decay_weight * (anchor + own_drift)
    pseudo = inner_rate * update - own_drift

    replicas = Y * X
    piece = D // replicas
    spread = pseudo.reshape(ROWS_DEV, replicas, piece).transpose(1, 0, 2)
    met = lax.all_to_all(spread, ("y", "x"), split_axis=0, concat_axis=0, tiled=True)
    part = jnp.sum(met, axis=0) / replicas
    copies = jnp.broadcast_to(part[None], (replicas, ROWS_DEV, piece))
    pieces = lax.all_to_all(copies, ("y", "x"), split_axis=0, concat_axis=0, tiled=True)
    average = pieces.transpose(1, 0, 2).reshape(ROWS_DEV, D)
    squares = jnp.broadcast_to(jnp.sum(pieces * pieces), (PARTS, 1, 128))
    squares = lax.all_to_all(squares, ("z", "c"), split_axis=0, concat_axis=0, tiled=True)
    squares = jnp.sum(squares[:, 0, 0])
    ceiling = 0.3 * math.sqrt(ROWS_DEV * PARTS * D)
    factor = ceiling / jnp.maximum(jnp.sqrt(squares), ceiling)
    momentum = momentum_coef * outer_momentum + factor * average
    updated = anchor - outer_rate * (factor * average + momentum_coef * momentum)
    return (moment_one[None], moment_two[None], momentum, updated)


def solution(mesh):
    devices = mesh.devices.reshape(Y, X, Z, C)
    grid = Mesh(devices, ("y", "x", "z", "c"))
    rep, fsdp = ("y", "x"), ("z", "c")
    return jax.shard_map(
        per_device,
        mesh=grid,
        in_specs=(
            P(rep, fsdp, None),
            P(rep, fsdp, None),
            P(fsdp, None),
            P(rep, fsdp, None),
            P(rep, fsdp, None),
            P(rep, fsdp, None),
            P(fsdp, None),
        ),
        out_specs=(
            P(rep, fsdp, None),
            P(rep, fsdp, None),
            P(fsdp, None),
            P(fsdp, None),
        ),
        check_vma=False,
    )
```

time: 262 us -> 181 us (0.69)
  waiting for transfers between devices: 199 us -> 62.8 us
  starting transfers between devices: 0.08 us -> 56.9 us
  between operations: 14.8 us -> 1.96 us
  blocking collectives: 26.2 us -> 37.4 us
  local copies, waits for them, and re-layouts: 1 us -> 6.7 us
  matrix products: 11.5 us -> 6.17 us
    reduce_scatter x1 -> x0, waiting for transfers between devices: 103 us -> none  [per_device(): lax.psum_scatter(lax.dot_general(activations, cotangent, (((0,), (0,)), (...]
    psum x1 -> x0, waiting for transfers between devices: 95.5 us -> none  [per_device(): average = lax.psum(pseudo, 'rep') / replicas]
    ppermute x0 -> x36, waiting for transfers between devices: none -> 58.4 us  [the longest x16 39.4 us: ring(): up = lax.ppermute(up, 'z', UP)]
    all_to_all x0 -> x2, blocking collectives: none -> 37.4 us  [the longest x1 19.1 us: per_device(): lax.all_to_all(copies, ('y', 'x'), split_axis=0, concat_axis=0, tiled=True)]
    ppermute x0 -> x36, starting transfers between devices: none -> 37.4 us  [the longest x16 28.8 us: ring(): down = lax.ppermute(down, 'z', DOWN)]
    psum x1 -> x0, blocking collectives: 26.2 us -> none  [per_device(): squares = lax.psum(jnp.sum(average * average), 'fsdp')]
    all_to_all x0 -> x1, starting transfers between devices: none -> 19.5 us  [per_device(): lax.all_to_all(squares, ('z', 'c'), split_axis=0, concat_axis=0, tiled=True)]
    dot_general x1 -> x9, matrix products: 11.5 us -> 6.17 us  [the longest x8 5.66 us: product(): lax.dot_general(lhs, rhs, (((1,), (0,)), ((), ())), preferred_element_typ...]
  transfers between devices with their start and end apart: 2 -> 37, of which waited for: 2 -> 20; matrix products, arithmetic and copies ran while one was open for 0% -> 5% of each run, Pallas kernels for 0% -> 0%
where the time goes in v1:
time: 181 us; the launch traced here: 180 us
  waiting for transfers between devices  62.8 us (35%)
  starting transfers between devices  56.9 us (31%)
  blocking collectives  37.4 us (21%)
  other arithmetic  8.47 us (5%)
  local copies, waits for them, and re-layouts  6.7 us (4%)
  matrix products  6.17 us (3%)
  between operations  1.96 us (1%)
    ppermute x16, waiting for transfers between devices, ring(): up = lax.ppermute(up, 'z', UP)  39.4 us
    ppermute x16, starting transfers between devices, ring(): down = lax.ppermute(down, 'z', DOWN)  28.8 us
    all_to_all x1, starting transfers between devices, per_device(): lax.all_to_all(squares, ('z', 'c'), split_axis=0, concat_axis=0, tiled=True)  19.5 us
    all_to_all x1, blocking collectives, per_device(): lax.all_to_all(copies, ('y', 'x'), split_axis=0, concat_axis=0, tiled=True)  19.1 us
    ppermute x16, waiting for transfers between devices, ring(): down = lax.ppermute(down, 'z', DOWN)  19 us
    all_to_all x1, blocking collectives, per_device(): lax.all_to_all(spread, ('y', 'x'), split_axis=0, concat_axis=0, tiled=True)  18.3 us
    dot_general x8, matrix products, product(): lax.dot_general(lhs, rhs, (((1,), (0,)), ((), ())), preferred_element_typ...  5.66 us
    unnamed x24, local copies, waits for them, and re-layouts  5.19 us
  transfers between devices with their start and end apart: 37, of which 20 were waited for; matrix products, arithmetic and copies ran while one was open for 5% of the time, Pallas kernels for 0%

profile of v1, /device:TPU:1, one launch (start us, length us, event | category | flops | bytes accessed | tf_op | source)
XLA Modules:
  0.0 180.4 jit_solution(4632644822618032646)
XLA Ops:
  0.7 1.0 copy-done
  2.2 2.9 %copy-done.2 = bf16[1,512,8192]{2,1,0:T(8,128)(2,1)S(1)} copy-done((bf16[1,512,8192]{2,1,0:T(8,128)(2,1)S(1)}, bf16[1,512,8192]{2,1,0:T(8,128)(2,1)}, u32[]{:S(2)}) %copy-start.2) | copy-done | bytes 8388632
  5.8 3.3 %collective-permute-start.9 = (f32[256,2048]{1,0:T(8,128)S(1)}, f32[256,2048]{1,0:T(8,128)S(1)}, u32[]{:S(2)}, u32[]{:S(2)}) collective-permute-start(f32[256,2048]{1,0:T(8,128)S(1)} %fusion.8), channel_id=1, source_target_pairs={{0,1},{1,0},{2,3},{3,2},{4,5},{5,4},{6,7},{7,6},{8,9},{9,8},{10,11... | collective-permute-start | bytes 6291464 | tf_op jit(solution)/shard_map/ppermute | solution.py:57
  12.7 0.7 fusion.14
  13.5 0.7 fusion.6
  15.1 3.9 %collective-permute-start.14 = (f32[32,1024]{1,0:T(8,128)S(1)}, f32[32,1024]{1,0:T(8,128)S(1)}, u32[]{:S(2)}, u32[]{:S(2)}) collective-permute-start(f32[32,1024]{1,0:T(8,128)S(1)} %get-tuple-element.14), channel_id=1, source_target_pairs={{0,14},{2,0},{4,2},{6,4},{8,6},{10,8},{12,10},{14,12},{1,15},{3,1}... | collective-permute-start | bytes 393224 | tf_op jit(solution)/shard_map/ppermute | solution.py:71
  19.1 3.2 %collective-permute-done.10 = f32[32,1024]{1,0:T(8,128)S(1)} collective-permute-done((f32[32,1024]{1,0:T(8,128)S(1)}, f32[32,1024]{1,0:T(8,128)S(1)}, u32[]{:S(2)}, u32[]{:S(2)}) %collective-permute-start.10) | collective-permute-done | bytes 131104 | tf_op jit(solution)/shard_map/ppermute | solution.py:70
  22.3 1.1 collective-permute-start.5
  24.6 1.6 collective-permute-done.5
  26.3 2.9 %collective-permute-start.15 = (f32[32,2048]{1,0:T(8,128)S(1)}, f32[32,2048]{1,0:T(8,128)S(1)}, u32[]{:S(2)}, u32[]{:S(2)}) collective-permute-start(f32[32,2048]{1,0:T(8,128)S(1)} %pad_maximum_fusion.5), channel_id=1, source_target_pairs={{0,14},{2,0},{4,2},{6,4},{8,6},{10,8},{12,10},{14,12},{1,15},{3,1}... | collective-permute-start | bytes 786440 | tf_op jit(solution)/shard_map/ppermute | solution.py:71
  29.3 6.4 %collective-permute-done.2 = f32[32,2048]{1,0:T(8,128)S(1)} collective-permute-done((f32[32,2048]{1,0:T(8,128)S(1)}, f32[32,2048]{1,0:T(8,128)S(1)}, u32[]{:S(2)}, u32[]{:S(2)}) %collective-permute-start.2) | collective-permute-done | bytes 262176 | tf_op jit(solution)/shard_map/ppermute | solution.py:70
  35.7 1.1 collective-permute-start.6
  37.4 3.6 %collective-permute-done.6 = f32[32,2048]{1,0:T(8,128)S(1)} collective-permute-done((f32[32,2048]{1,0:T(8,128)S(1)}, f32[32,2048]{1,0:T(8,128)S(1)}, u32[]{:S(2)}, u32[]{:S(2)}) %collective-permute-start.6) | collective-permute-done | bytes 262176 | tf_op jit(solution)/shard_map/ppermute | solution.py:71
  40.9 2.4 %collective-permute-done.3 = f32[32,2048]{1,0:T(8,128)S(1)} collective-permute-done((f32[32,2048]{1,0:T(8,128)S(1)}, f32[32,2048]{1,0:T(8,128)S(1)}, u32[]{:S(2)}, u32[]{:S(2)}) %collective-permute-start.3) | collective-permute-done | bytes 262176 | tf_op jit(solution)/shard_map/ppermute | solution.py:70
  43.8 5.6 %collective-permute-done.12 = f32[32,2048]{1,0:T(8,128)S(1)} collective-permute-done((f32[32,2048]{1,0:T(8,128)S(1)}, f32[32,2048]{1,0:T(8,128)S(1)}, u32[]{:S(2)}, u32[]{:S(2)}) %collective-permute-start.12) | collective-permute-done | bytes 262176 | tf_op jit(solution)/shard_map/ppermute | solution.py:70
  49.6 1.5 collective-permute-start.13
  51.1 6.5 %collective-permute-done.16 = f32[32,2048]{1,0:T(8,128)S(1)} collective-permute-done((f32[32,2048]{1,0:T(8,128)S(1)}, f32[32,2048]{1,0:T(8,128)S(1)}, u32[]{:S(2)}, u32[]{:S(2)}) %collective-permute-start.16) | collective-permute-done | bytes 262176 | tf_op jit(solution)/shard_map/ppermute | solution.py:71
  57.6 1.4 collective-permute-start.8
  59.1 1.2 collective-permute-done.4
  60.3 1.5 collective-permute-start.17
  61.8 1.7 collective-permute-done.8
  63.8 2.7 %collective-permute-start.23 = (f32[32,1024]{1,0:T(8,128)S(1)}, f32[32,1024]{1,0:T(8,128)S(1)}, u32[]{:S(2)}, u32[]{:S(2)}) collective-permute-start(f32[32,1024]{1,0:T(8,128)S(1)} %get-tuple-element.22), channel_id=1, source_target_pairs={{0,14},{2,0},{4,2},{6,4},{8,6},{10,8},{12,10},{14,12},{1,15},{3,1}... | collective-permute-start | bytes 393224 | tf_op jit(solution)/shard_map/ppermute | solution.py:71
  66.6 2.7 %collective-permute-start.32 = (f32[32,1024]{1,0:T(8,128)S(1)}, f32[32,1024]{1,0:T(8,128)S(1)}, u32[]{:S(2)}, u32[]{:S(2)}) collective-permute-start(f32[32,1024]{1,0:T(8,128)S(1)} %get-tuple-element.30), channel_id=1, source_target_pairs={{0,14},{2,0},{4,2},{6,4},{8,6},{10,8},{12,10},{14,12},{1,15},{3,1}... | collective-permute-start | bytes 393224 | tf_op jit(solution)/shard_map/ppermute | solution.py:71
  69.4 1.4 collective-permute-done.23
  70.9 2.5 %collective-permute-start.24 = (f32[32,2048]{1,0:T(8,128)S(1)}, f32[32,2048]{1,0:T(8,128)S(1)}, u32[]{:S(2)}, u32[]{:S(2)}) collective-permute-start(f32[32,2048]{1,0:T(8,128)S(1)} %pad_maximum_fusion.7), channel_id=1, source_target_pairs={{0,14},{2,0},{4,2},{6,4},{8,6},{10,8},{12,10},{14,12},{1,15},{3,1}... | collective-permute-start | bytes 786440 | tf_op jit(solution)/shard_map/ppermute | solution.py:71
  73.8 2.7 %collective-permute-start.33 = (f32[32,2048]{1,0:T(8,128)S(1)}, f32[32,2048]{1,0:T(8,128)S(1)}, u32[]{:S(2)}, u32[]{:S(2)}) collective-permute-start(f32[32,2048]{1,0:T(8,128)S(1)} %pad_maximum_fusion.9), channel_id=1, source_target_pairs={{0,14},{2,0},{4,2},{6,4},{8,6},{10,8},{12,10},{14,12},{1,15},{3,1}... | collective-permute-start | bytes 786440 | tf_op jit(solution)/shard_map/ppermute | solution.py:71
  76.6 4.9 %collective-permute-done.20 = f32[32,2048]{1,0:T(8,128)S(1)} collective-permute-done((f32[32,2048]{1,0:T(8,128)S(1)}, f32[32,2048]{1,0:T(8,128)S(1)}, u32[]{:S(2)}, u32[]{:S(2)}) %collective-permute-start.20) | collective-permute-done | bytes 262176 | tf_op jit(solution)/shard_map/ppermute | solution.py:70
  81.7 2.7 %collective-permute-done.29 = f32[32,2048]{1,0:T(8,128)S(1)} collective-permute-done((f32[32,2048]{1,0:T(8,128)S(1)}, f32[32,2048]{1,0:T(8,128)S(1)}, u32[]{:S(2)}, u32[]{:S(2)}) %collective-permute-start.29) | collective-permute-done | bytes 262176 | tf_op jit(solution)/shard_map/ppermute | solution.py:70
  84.5 5.6 %collective-permute-done.21 = f32[32,2048]{1,0:T(8,128)S(1)} collective-permute-done((f32[32,2048]{1,0:T(8,128)S(1)}, f32[32,2048]{1,0:T(8,128)S(1)}, u32[]{:S(2)}, u32[]{:S(2)}) %collective-permute-start.21) | collective-permute-done | bytes 262176 | tf_op jit(solution)/shard_map/ppermute | solution.py:70
  90.2 0.9 collective-permute-start.25
  91.8 4.0 %collective-permute-done.30 = f32[32,2048]{1,0:T(8,128)S(1)} collective-permute-done((f32[32,2048]{1,0:T(8,128)S(1)}, f32[32,2048]{1,0:T(8,128)S(1)}, u32[]{:S(2)}, u32[]{:S(2)}) %collective-permute-start.30) | collective-permute-done | bytes 262176 | tf_op jit(solution)/shard_map/ppermute | solution.py:70
  95.8 0.9 collective-permute-start.34
  97.5 2.1 %collective-permute-start.26 = (f32[32,2048]{1,0:T(8,128)S(1)}, f32[32,2048]{1,0:T(8,128)S(1)}, u32[]{:S(2)}, u32[]{:S(2)}) collective-permute-start(f32[32,2048]{1,0:T(8,128)S(1)} %fusion.61), channel_id=1, source_target_pairs={{0,14},{2,0},{4,2},{6,4},{8,6},{10,8},{12,10},{14,12},{1,15},{3,1}... | collective-permute-start | bytes 786440 | tf_op jit(solution)/shard_map/ppermute | solution.py:71
  99.6 1.8 %collective-permute-done.34 = f32[32,2048]{1,0:T(8,128)S(1)} collective-permute-done((f32[32,2048]{1,0:T(8,128)S(1)}, f32[32,2048]{1,0:T(8,128)S(1)}, u32[]{:S(2)}, u32[]{:S(2)}) %collective-permute-start.34) | collective-permute-done | bytes 262176 | tf_op jit(solution)/shard_map/ppermute | solution.py:71
  101.5 1.8 %collective-permute-start.35 = (f32[32,2048]{1,0:T(8,128)S(1)}, f32[32,2048]{1,0:T(8,128)S(1)}, u32[]{:S(2)}, u32[]{:S(2)}) collective-permute-start(f32[32,2048]{1,0:T(8,128)S(1)} %fusion.55), channel_id=1, source_target_pairs={{0,14},{2,0},{4,2},{6,4},{8,6},{10,8},{12,10},{14,12},{1,15},{3,1}... | collective-permute-start | bytes 786440 | tf_op jit(solution)/shard_map/ppermute | solution.py:71
  103.3 0.9 collective-permute-done.26
  104.3 2.7 %collective-permute-done.31 = f32[32,2048]{1,0:T(8,128)S(1)} collective-permute-done((f32[32,2048]{1,0:T(8,128)S(1)}, f32[32,2048]{1,0:T(8,128)S(1)}, u32[]{:S(2)}, u32[]{:S(2)}) %collective-permute-start.31) | collective-permute-done | bytes 262176 | tf_op jit(solution)/shard_map/ppermute | solution.py:70
  107.0 1.6 collective-permute-done.35
  108.7 0.8 bitcast_subtract_fusion
  109.6 18.3 %all_to_all.15 = f32[16,32,512]{2,1,0:T(8,128)S(1)} all-to-all(f32[16,32,512]{2,1,0:T(8,128)S(1)} %bitcast.49), channel_id=1, replica_groups=mesh['y'=4,'x'=4,'z'=8,'c'=2] {'y','x'}, dimensions={0} | all-to-all | bytes 2097152 | tf_op jit(solution)/shard_map/all_to_all | solution.py:103
  128.2 19.1 %all_to_all.16 = f32[16,32,512]{2,1,0:T(8,128)S(1)} all-to-all(f32[16,32,512]{2,1,0:T(8,128)S(1)} %broadcast_in_dim.21), channel_id=1, replica_groups=mesh['y'=4,'x'=4,'z'=8,'c'=2] {'y','x'}, dimensions={0} | all-to-all | bytes 2097152 | tf_op jit(solution)/shard_map/all_to_all | solution.py:106
  147.3 0.9 multiply_reduce_fusion
  148.1 1.2 broadcast_in_dim.22
  149.4 19.5 %all-to-all-start.2 = ((f32[16,1,128]{2,1,0:T(1,128)}), f32[16,1,128]{2,1,0:T(1,128)S(1)}, u32[]{:S(2)}, u32[]{:S(2)}) async-start(f32[16,1,128]{2,1,0:T(1,128)} %broadcast_in_dim.22), calls=%async_computation.2 | async-start | bytes 16384 | tf_op jit(solution)/shard_map/all_to_all | solution.py:109
  168.8 2.7 %fusion.23 = (f32[1,32,8192]{2,1,0:T(8,128)}, f32[1,32,8192]{2,1,0:T(8,128)}) fusion(f32[1,32,8192]{2,1,0:T(8,128)S(1)} %copy-done.3, f32[1,32,2048]{2,1,0:T(8,128)} %bitcast.54, f32[1,32,2048]{2,1,0:T(8,128)} %bitcast.53, f32[1,32,2048]{2,1,0:T(8,128)} %bitcast.52, f32[1,32,2048]{2,1,0:T(8,128)S(1)} %bitcast.51, f32[1,32,8192]{2,1,0:T(8,128)S(1)} %copy-done.4), kind=kLoop, calls=%fused_computation.34 | loop fusion | flops 2621440 | bytes 5242880 | tf_op jit(solution)/shard_map/add | solution.py:94
  171.6 4.3 %all-to-all-done.2 = f32[16,1,128]{2,1,0:T(1,128)S(1)} async-done(((f32[16,1,128]{2,1,0:T(1,128)}), f32[16,1,128]{2,1,0:T(1,128)S(1)}, u32[]{:S(2)}, u32[]{:S(2)}) %all-to-all-start.2) | async-done | bytes 8224 | tf_op jit(solution)/shard_map/all_to_all | solution.py:109
  177.5 1.0 copy-done.6
  178.8 1.6 multiply_subtract_fusion
  (110 shorter events, 12.8 us)
Async XLA Ops:
  0.6 1.1 copy-start
  1.7 3.4 %copy-start.2 = (bf16[1,512,8192]{2,1,0:T(8,128)(2,1)S(1)}, bf16[1,512,8192]{2,1,0:T(8,128)(2,1)}, u32[]{:S(2)}) copy-start(bf16[1,512,8192]{2,1,0:T(8,128)(2,1)} %param.8) | copy-start | bytes 25165828
  5.8 9.1 %collective-permute-start.9 = (f32[256,2048]{1,0:T(8,128)S(1)}, f32[256,2048]{1,0:T(8,128)S(1)}, u32[]{:S(2)}, u32[]{:S(2)}) collective-permute-start(f32[256,2048]{1,0:T(8,128)S(1)} %fusion.8), channel_id=1, source_target_pairs={{0,1},{1,0},{2,3},{3,2},{4,5},{5,4},{6,7},{7,6},{8,9},{9,8},{10,11... | collective-permute-start | bytes 6291464 | tf_op jit(solution)/shard_map/ppermute | solution.py:57
  9.8 9.2 %collective-permute-start = (f32[256,2048]{1,0:T(8,128)S(1)}, f32[256,2048]{1,0:T(8,128)S(1)}, u32[]{:S(2)}, u32[]{:S(2)}) collective-permute-start(f32[256,2048]{1,0:T(8,128)S(1)} %fusion.12), channel_id=1, source_target_pairs={{0,1},{1,0},{2,3},{3,2},{4,5},{5,4},{6,7},{7,6},{8,9},{9,8},{10,11... | collective-permute-start | bytes 6291464 | tf_op jit(solution)/shard_map/ppermute | solution.py:57
  10.6 53.0 %collective-permute-start.18 = (f32[256,2048]{1,0:T(8,128)S(1)}, f32[256,2048]{1,0:T(8,128)S(1)}, u32[]{:S(2)}, u32[]{:S(2)}) collective-permute-start(f32[256,2048]{1,0:T(8,128)S(1)} %fusion.4), channel_id=1, source_target_pairs={{0,1},{1,0},{2,3},{3,2},{4,5},{5,4},{6,7},{7,6},{8,9},{9,8},{10,11... | collective-permute-start | bytes 6291464 | tf_op jit(solution)/shard_map/ppermute | solution.py:57
  11.9 54.5 %collective-permute-start.27 = (f32[256,2048]{1,0:T(8,128)S(1)}, f32[256,2048]{1,0:T(8,128)S(1)}, u32[]{:S(2)}, u32[]{:S(2)}) collective-permute-start(f32[256,2048]{1,0:T(8,128)S(1)} %fusion), channel_id=1, source_target_pairs={{0,1},{1,0},{2,3},{3,2},{4,5},{5,4},{6,7},{7,6},{8,9},{9,8},{10,11... | collective-permute-start | bytes 6291464 | tf_op jit(solution)/shard_map/ppermute | solution.py:57
  15.0 7.3 %collective-permute-start.10 = (f32[32,1024]{1,0:T(8,128)S(1)}, f32[32,1024]{1,0:T(8,128)S(1)}, u32[]{:S(2)}, u32[]{:S(2)}) collective-permute-start(f32[32,1024]{1,0:T(8,128)S(1)} %get-tuple-element.15), channel_id=1, source_target_pairs={{0,2},{2,4},{4,6},{6,8},{8,10},{10,12},{12,14},{14,0},{1,3},{3,5},... | collective-permute-start | bytes 393224 | tf_op jit(solution)/shard_map/ppermute | solution.py:70
  15.1 8.4 %collective-permute-start.14 = (f32[32,1024]{1,0:T(8,128)S(1)}, f32[32,1024]{1,0:T(8,128)S(1)}, u32[]{:S(2)}, u32[]{:S(2)}) collective-permute-start(f32[32,1024]{1,0:T(8,128)S(1)} %get-tuple-element.14), channel_id=1, source_target_pairs={{0,14},{2,0},{4,2},{6,4},{8,6},{10,8},{12,10},{14,12},{1,15},{3,1}... | collective-permute-start | bytes 393224 | tf_op jit(solution)/shard_map/ppermute | solution.py:71
  19.0 5.5 %collective-permute-start.1 = (f32[32,1024]{1,0:T(8,128)S(1)}, f32[32,1024]{1,0:T(8,128)S(1)}, u32[]{:S(2)}, u32[]{:S(2)}) collective-permute-start(f32[32,1024]{1,0:T(8,128)S(1)} %get-tuple-element.39), channel_id=1, source_target_pairs={{0,2},{2,4},{4,6},{6,8},{8,10},{10,12},{12,14},{14,0},{1,3},{3,5},... | collective-permute-start | bytes 393224 | tf_op jit(solution)/shard_map/ppermute | solution.py:70
  22.3 3.8 %collective-permute-start.5 = (f32[32,1024]{1,0:T(8,128)S(1)}, f32[32,1024]{1,0:T(8,128)S(1)}, u32[]{:S(2)}, u32[]{:S(2)}) collective-permute-start(f32[32,1024]{1,0:T(8,128)S(1)} %get-tuple-element.38), channel_id=1, source_target_pairs={{0,14},{2,0},{4,2},{6,4},{8,6},{10,8},{12,10},{14,12},{1,15},{3,1}... | collective-permute-start | bytes 393224 | tf_op jit(solution)/shard_map/ppermute | solution.py:71
  23.6 13.3 %collective-permute-start.11 = (f32[32,2048]{1,0:T(8,128)S(1)}, f32[32,2048]{1,0:T(8,128)S(1)}, u32[]{:S(2)}, u32[]{:S(2)}) collective-permute-start(f32[32,2048]{1,0:T(8,128)S(1)} %pad_maximum_fusion.4), channel_id=1, source_target_pairs={{0,2},{2,4},{4,6},{6,8},{8,10},{10,12},{12,14},{14,0},{1,3},{3,5},... | collective-permute-start | bytes 786440 | tf_op jit(solution)/shard_map/ppermute | solution.py:70
  26.2 9.5 %collective-permute-start.2 = (f32[32,2048]{1,0:T(8,128)S(1)}, f32[32,2048]{1,0:T(8,128)S(1)}, u32[]{:S(2)}, u32[]{:S(2)}) collective-permute-start(f32[32,2048]{1,0:T(8,128)S(1)} %pad_maximum_fusion.2), channel_id=1, source_target_pairs={{0,2},{2,4},{4,6},{6,8},{8,10},{10,12},{12,14},{14,0},{1,3},{3,5},... | collective-permute-start | bytes 786440 | tf_op jit(solution)/shard_map/ppermute | solution.py:70
  26.3 17.5 %collective-permute-start.15 = (f32[32,2048]{1,0:T(8,128)S(1)}, f32[32,2048]{1,0:T(8,128)S(1)}, u32[]{:S(2)}, u32[]{:S(2)}) collective-permute-start(f32[32,2048]{1,0:T(8,128)S(1)} %pad_maximum_fusion.5), channel_id=1, source_target_pairs={{0,14},{2,0},{4,2},{6,4},{8,6},{10,8},{12,10},{14,12},{1,15},{3,1}... | collective-permute-start | bytes 786440 | tf_op jit(solution)/shard_map/ppermute | solution.py:71
  35.7 5.2 %collective-permute-start.6 = (f32[32,2048]{1,0:T(8,128)S(1)}, f32[32,2048]{1,0:T(8,128)S(1)}, u32[]{:S(2)}, u32[]{:S(2)}) collective-permute-start(f32[32,2048]{1,0:T(8,128)S(1)} %pad_maximum_fusion.3), channel_id=1, source_target_pairs={{0,14},{2,0},{4,2},{6,4},{8,6},{10,8},{12,10},{14,12},{1,15},{3,1}... | collective-permute-start | bytes 786440 | tf_op jit(solution)/shard_map/ppermute | solution.py:71
  36.9 6.5 %collective-permute-start.3 = (f32[32,2048]{1,0:T(8,128)S(1)}, f32[32,2048]{1,0:T(8,128)S(1)}, u32[]{:S(2)}, u32[]{:S(2)}) collective-permute-start(f32[32,2048]{1,0:T(8,128)S(1)} %fusion.74), channel_id=1, source_target_pairs={{0,2},{2,4},{4,6},{6,8},{8,10},{10,12},{12,14},{14,0},{1,3},{3,5},... | collective-permute-start | bytes 786440 | tf_op jit(solution)/shard_map/ppermute | solution.py:70
  40.9 8.5 %collective-permute-start.12 = (f32[32,2048]{1,0:T(8,128)S(1)}, f32[32,2048]{1,0:T(8,128)S(1)}, u32[]{:S(2)}, u32[]{:S(2)}) collective-permute-start(f32[32,2048]{1,0:T(8,128)S(1)} %fusion.68), channel_id=1, source_target_pairs={{0,2},{2,4},{4,6},{6,8},{8,10},{10,12},{12,14},{14,0},{1,3},{3,5},... | collective-permute-start | bytes 786440 | tf_op jit(solution)/shard_map/ppermute | solution.py:70
  43.5 7.6 %collective-permute-start.7 = (f32[32,2048]{1,0:T(8,128)S(1)}, f32[32,2048]{1,0:T(8,128)S(1)}, u32[]{:S(2)}, u32[]{:S(2)}) collective-permute-start(f32[32,2048]{1,0:T(8,128)S(1)} %get-tuple-element.35), channel_id=1, source_target_pairs={{0,14},{2,0},{4,2},{6,4},{8,6},{10,8},{12,10},{14,12},{1,15},{3,1}... | collective-permute-start | bytes 786440 | tf_op jit(solution)/shard_map/ppermute | solution.py:71
  49.5 8.1 %collective-permute-start.16 = (f32[32,2048]{1,0:T(8,128)S(1)}, f32[32,2048]{1,0:T(8,128)S(1)}, u32[]{:S(2)}, u32[]{:S(2)}) collective-permute-start(f32[32,2048]{1,0:T(8,128)S(1)} %get-tuple-element.11), channel_id=1, source_target_pairs={{0,14},{2,0},{4,2},{6,4},{8,6},{10,8},{12,10},{14,12},{1,15},{3,1}... | collective-permute-start | bytes 786440 | tf_op jit(solution)/shard_map/ppermute | solution.py:71
  49.6 17.0 %collective-permute-start.13 = (f32[32,2048]{1,0:T(8,128)S(1)}, f32[32,2048]{1,0:T(8,128)S(1)}, u32[]{:S(2)}, u32[]{:S(2)}) collective-permute-start(f32[32,2048]{1,0:T(8,128)S(1)} %get-tuple-element.10), channel_id=1, source_target_pairs={{0,2},{2,4},{4,6},{6,8},{8,10},{10,12},{12,14},{14,0},{1,3},{3,5},... | collective-permute-start | bytes 786440 | tf_op jit(solution)/shard_map/ppermute | solution.py:70
  51.1 9.2 %collective-permute-start.4 = (f32[32,2048]{1,0:T(8,128)S(1)}, f32[32,2048]{1,0:T(8,128)S(1)}, u32[]{:S(2)}, u32[]{:S(2)}) collective-permute-start(f32[32,2048]{1,0:T(8,128)S(1)} %get-tuple-element.34), channel_id=1, source_target_pairs={{0,2},{2,4},{4,6},{6,8},{8,10},{10,12},{12,14},{14,0},{1,3},{3,5},... | collective-permute-start | bytes 786440 | tf_op jit(solution)/shard_map/ppermute | solution.py:70
  57.6 5.9 %collective-permute-start.8 = (f32[32,2048]{1,0:T(8,128)S(1)}, f32[32,2048]{1,0:T(8,128)S(1)}, u32[]{:S(2)}, u32[]{:S(2)}) collective-permute-start(f32[32,2048]{1,0:T(8,128)S(1)} %fusion.73), channel_id=1, source_target_pairs={{0,14},{2,0},{4,2},{6,4},{8,6},{10,8},{12,10},{14,12},{1,15},{3,1}... | collective-permute-start | bytes 786440 | tf_op jit(solution)/shard_map/ppermute | solution.py:71
  60.3 9.0 %collective-permute-start.17 = (f32[32,2048]{1,0:T(8,128)S(1)}, f32[32,2048]{1,0:T(8,128)S(1)}, u32[]{:S(2)}, u32[]{:S(2)}) collective-permute-start(f32[32,2048]{1,0:T(8,128)S(1)} %fusion.67), channel_id=1, source_target_pairs={{0,14},{2,0},{4,2},{6,4},{8,6},{10,8},{12,10},{14,12},{1,15},{3,1}... | collective-permute-start | bytes 786440 | tf_op jit(solution)/shard_map/ppermute | solution.py:71
  63.7 5.7 %collective-permute-start.19 = (f32[32,1024]{1,0:T(8,128)S(1)}, f32[32,1024]{1,0:T(8,128)S(1)}, u32[]{:S(2)}, u32[]{:S(2)}) collective-permute-start(f32[32,1024]{1,0:T(8,128)S(1)} %get-tuple-element.23), channel_id=1, source_target_pairs={{0,2},{2,4},{4,6},{6,8},{8,10},{10,12},{12,14},{14,0},{1,3},{3,5},... | collective-permute-start | bytes 393224 | tf_op jit(solution)/shard_map/ppermute | solution.py:70
  63.8 7.0 %collective-permute-start.23 = (f32[32,1024]{1,0:T(8,128)S(1)}, f32[32,1024]{1,0:T(8,128)S(1)}, u32[]{:S(2)}, u32[]{:S(2)}) collective-permute-start(f32[32,1024]{1,0:T(8,128)S(1)} %get-tuple-element.22), channel_id=1, source_target_pairs={{0,14},{2,0},{4,2},{6,4},{8,6},{10,8},{12,10},{14,12},{1,15},{3,1}... | collective-permute-start | bytes 393224 | tf_op jit(solution)/shard_map/ppermute | solution.py:71
  66.5 7.2 %collective-permute-start.28 = (f32[32,1024]{1,0:T(8,128)S(1)}, f32[32,1024]{1,0:T(8,128)S(1)}, u32[]{:S(2)}, u32[]{:S(2)}) collective-permute-start(f32[32,1024]{1,0:T(8,128)S(1)} %get-tuple-element.31), channel_id=1, source_target_pairs={{0,2},{2,4},{4,6},{6,8},{8,10},{10,12},{12,14},{14,0},{1,3},{3,5},... | collective-permute-start | bytes 393224 | tf_op jit(solution)/shard_map/ppermute | solution.py:70
  66.6 7.1 %collective-permute-start.32 = (f32[32,1024]{1,0:T(8,128)S(1)}, f32[32,1024]{1,0:T(8,128)S(1)}, u32[]{:S(2)}, u32[]{:S(2)}) collective-permute-start(f32[32,1024]{1,0:T(8,128)S(1)} %get-tuple-element.30), channel_id=1, source_target_pairs={{0,14},{2,0},{4,2},{6,4},{8,6},{10,8},{12,10},{14,12},{1,15},{3,1}... | collective-permute-start | bytes 393224 | tf_op jit(solution)/shard_map/ppermute | solution.py:71
  69.4 39.3 %copy-start.7 = (f32[32,2048]{1,0:T(8,128)}, f32[32,2048]{1,0:T(8,128)S(1)}, u32[]{:S(2)}) copy-start(f32[32,2048]{1,0:T(8,128)S(1)} %fusion.71) | copy-start | bytes 786436
  70.9 13.6 %collective-permute-start.24 = (f32[32,2048]{1,0:T(8,128)S(1)}, f32[32,2048]{1,0:T(8,128)S(1)}, u32[]{:S(2)}, u32[]{:S(2)}) collective-permute-start(f32[32,2048]{1,0:T(8,128)S(1)} %pad_maximum_fusion.7), channel_id=1, source_target_pairs={{0,14},{2,0},{4,2},{6,4},{8,6},{10,8},{12,10},{14,12},{1,15},{3,1}... | collective-permute-start | bytes 786440 | tf_op jit(solution)/shard_map/ppermute | solution.py:71
  73.4 8.1 %collective-permute-start.20 = (f32[32,2048]{1,0:T(8,128)S(1)}, f32[32,2048]{1,0:T(8,128)S(1)}, u32[]{:S(2)}, u32[]{:S(2)}) collective-permute-start(f32[32,2048]{1,0:T(8,128)S(1)} %pad_maximum_fusion.6), channel_id=1, source_target_pairs={{0,2},{2,4},{4,6},{6,8},{8,10},{10,12},{12,14},{14,0},{1,3},{3,5},... | collective-permute-start | bytes 786440 | tf_op jit(solution)/shard_map/ppermute | solution.py:70
  73.8 18.0 %collective-permute-start.33 = (f32[32,2048]{1,0:T(8,128)S(1)}, f32[32,2048]{1,0:T(8,128)S(1)}, u32[]{:S(2)}, u32[]{:S(2)}) collective-permute-start(f32[32,2048]{1,0:T(8,128)S(1)} %pad_maximum_fusion.9), channel_id=1, source_target_pairs={{0,14},{2,0},{4,2},{6,4},{8,6},{10,8},{12,10},{14,12},{1,15},{3,1}... | collective-permute-start | bytes 786440 | tf_op jit(solution)/shard_map/ppermute | solution.py:71
  76.6 7.8 %collective-permute-start.29 = (f32[32,2048]{1,0:T(8,128)S(1)}, f32[32,2048]{1,0:T(8,128)S(1)}, u32[]{:S(2)}, u32[]{:S(2)}) collective-permute-start(f32[32,2048]{1,0:T(8,128)S(1)} %pad_maximum_fusion.8), channel_id=1, source_target_pairs={{0,2},{2,4},{4,6},{6,8},{8,10},{10,12},{12,14},{14,0},{1,3},{3,5},... | collective-permute-start | bytes 786440 | tf_op jit(solution)/shard_map/ppermute | solution.py:70
  81.6 8.6 %collective-permute-start.21 = (f32[32,2048]{1,0:T(8,128)S(1)}, f32[32,2048]{1,0:T(8,128)S(1)}, u32[]{:S(2)}, u32[]{:S(2)}) collective-permute-start(f32[32,2048]{1,0:T(8,128)S(1)} %fusion.62), channel_id=1, source_target_pairs={{0,2},{2,4},{4,6},{6,8},{8,10},{10,12},{12,14},{14,0},{1,3},{3,5},... | collective-permute-start | bytes 786440 | tf_op jit(solution)/shard_map/ppermute | solution.py:70
  84.4 11.4 %collective-permute-start.30 = (f32[32,2048]{1,0:T(8,128)S(1)}, f32[32,2048]{1,0:T(8,128)S(1)}, u32[]{:S(2)}, u32[]{:S(2)}) collective-permute-start(f32[32,2048]{1,0:T(8,128)S(1)} %fusion.56), channel_id=1, source_target_pairs={{0,2},{2,4},{4,6},{6,8},{8,10},{10,12},{12,14},{14,0},{1,3},{3,5},... | collective-permute-start | bytes 786440 | tf_op jit(solution)/shard_map/ppermute | solution.py:70
  90.2 7.2 %collective-permute-start.25 = (f32[32,2048]{1,0:T(8,128)S(1)}, f32[32,2048]{1,0:T(8,128)S(1)}, u32[]{:S(2)}, u32[]{:S(2)}) collective-permute-start(f32[32,2048]{1,0:T(8,128)S(1)} %get-tuple-element.19), channel_id=1, source_target_pairs={{0,14},{2,0},{4,2},{6,4},{8,6},{10,8},{12,10},{14,12},{1,15},{3,1}... | collective-permute-start | bytes 786440 | tf_op jit(solution)/shard_map/ppermute | solution.py:71
  91.1 12.2 %collective-permute-start.22 = (f32[32,2048]{1,0:T(8,128)S(1)}, f32[32,2048]{1,0:T(8,128)S(1)}, u32[]{:S(2)}, u32[]{:S(2)}) collective-permute-start(f32[32,2048]{1,0:T(8,128)S(1)} %get-tuple-element.18), channel_id=1, source_target_pairs={{0,2},{2,4},{4,6},{6,8},{8,10},{10,12},{12,14},{14,0},{1,3},{3,5},... | collective-permute-start | bytes 786440 | tf_op jit(solution)/shard_map/ppermute | solution.py:70
  95.8 5.6 %collective-permute-start.34 = (f32[32,2048]{1,0:T(8,128)S(1)}, f32[32,2048]{1,0:T(8,128)S(1)}, u32[]{:S(2)}, u32[]{:S(2)}) collective-permute-start(f32[32,2048]{1,0:T(8,128)S(1)} %get-tuple-element.27), channel_id=1, source_target_pairs={{0,14},{2,0},{4,2},{6,4},{8,6},{10,8},{12,10},{14,12},{1,15},{3,1}... | collective-permute-start | bytes 786440 | tf_op jit(solution)/shard_map/ppermute | solution.py:71
  96.8 10.2 %collective-permute-start.31 = (f32[32,2048]{1,0:T(8,128)S(1)}, f32[32,2048]{1,0:T(8,128)S(1)}, u32[]{:S(2)}, u32[]{:S(2)}) collective-permute-start(f32[32,2048]{1,0:T(8,128)S(1)} %get-tuple-element.26), channel_id=1, source_target_pairs={{0,2},{2,4},{4,6},{6,8},{8,10},{10,12},{12,14},{14,0},{1,3},{3,5},... | collective-permute-start | bytes 786440 | tf_op jit(solution)/shard_map/ppermute | solution.py:70
  97.4 11.2 %copy-start.11 = (f32[1,32,8192]{2,1,0:T(8,128)S(1)}, f32[1,32,8192]{2,1,0:T(8,128)}, u32[]{:S(2)}) copy-start(f32[1,32,8192]{2,1,0:T(8,128)} %param.10) | copy-start | bytes 3145732
  97.4 11.2 %copy-start.3 = (f32[1,32,8192]{2,1,0:T(8,128)S(1)}, f32[1,32,8192]{2,1,0:T(8,128)}, u32[]{:S(2)}) copy-start(f32[1,32,8192]{2,1,0:T(8,128)} %param.12) | copy-start | bytes 3145732
  97.4 11.2 %copy-start.4 = (f32[1,32,8192]{2,1,0:T(8,128)S(1)}, f32[1,32,8192]{2,1,0:T(8,128)}, u32[]{:S(2)}) copy-start(f32[1,32,8192]{2,1,0:T(8,128)} %param.11) | copy-start | bytes 3145732
  97.5 11.2 %copy-start.5 = (f32[32,8192]{1,0:T(8,128)S(1)}, f32[32,8192]{1,0:T(8,128)}, u32[]{:S(2)}) copy-start(f32[32,8192]{1,0:T(8,128)} %param.9) | copy-start | bytes 3145732
  97.5 6.8 %collective-permute-start.26 = (f32[32,2048]{1,0:T(8,128)S(1)}, f32[32,2048]{1,0:T(8,128)S(1)}, u32[]{:S(2)}, u32[]{:S(2)}) collective-permute-start(f32[32,2048]{1,0:T(8,128)S(1)} %fusion.61), channel_id=1, source_target_pairs={{0,14},{2,0},{4,2},{6,4},{8,6},{10,8},{12,10},{14,12},{1,15},{3,1}... | collective-permute-start | bytes 786440 | tf_op jit(solution)/shard_map/ppermute | solution.py:71
  101.5 7.1 %collective-permute-start.35 = (f32[32,2048]{1,0:T(8,128)S(1)}, f32[32,2048]{1,0:T(8,128)S(1)}, u32[]{:S(2)}, u32[]{:S(2)}) collective-permute-start(f32[32,2048]{1,0:T(8,128)S(1)} %fusion.55), channel_id=1, source_target_pairs={{0,14},{2,0},{4,2},{6,4},{8,6},{10,8},{12,10},{14,12},{1,15},{3,1}... | collective-permute-start | bytes 786440 | tf_op jit(solution)/shard_map/ppermute | solution.py:71
  104.3 5.3 %copy-start.8 = (f32[32,2048]{1,0:T(8,128)}, f32[32,2048]{1,0:T(8,128)S(1)}, u32[]{:S(2)}) copy-start(f32[32,2048]{1,0:T(8,128)S(1)} %fusion.65) | copy-start | bytes 786436
  149.4 26.5 %all-to-all-start.2 = ((f32[16,1,128]{2,1,0:T(1,128)}), f32[16,1,128]{2,1,0:T(1,128)S(1)}, u32[]{:S(2)}, u32[]{:S(2)}) async-start(f32[16,1,128]{2,1,0:T(1,128)} %broadcast_in_dim.22), calls=%async_computation.2 | async-start | bytes 16384 | tf_op jit(solution)/shard_map/all_to_all | solution.py:109
  177.3 1.2 copy-start.6
  177.3 1.5 copy-start.10
  177.5 2.9 %copy-start.1 = (bf16[1,512,512]{2,1,0:T(8,128)(2,1)S(1)}, bf16[1,512,512]{2,1,0:T(8,128)(2,1)}, u32[]{:S(2)}) copy-start(bf16[1,512,512]{2,1,0:T(8,128)(2,1)} %param.7) | copy-start | bytes 1572868
  (1 other events, 1.0 us)

commit v2 on v1

--- a/solution.py
+++ b/solution.py
@@ -18,9 +18,10 @@
 Y, X, Z, C = 4, 4, 8, 2
 ROWS_DEV = 32
 PARTS = Z * C
-CHUNKS = 4
+CHUNKS = 2
 WIDTH = D // CHUNKS
 HALF = WIDTH // 2
+STEPS = (4, 3, 5, 2, 6, 1, 7, 0)
 UP = [(i, (i + 1) % Z) for i in range(Z)]
 DOWN = [(i, (i - 1) % Z) for i in range(Z)]
 SWAP = [(0, 1), (1, 0)]
@@ -32,7 +33,10 @@
     source = lax.broadcasted_iota(jnp.int32, (rows, rows), 0)
     mine = place // (Z * ROWS_DEV)
     core = jnp.where(mine == 1, c, 1 - c)
-    step = (place // ROWS_DEV) % Z
+    slot = (place // ROWS_DEV) % Z
+    step = jnp.zeros_like(slot)
+    for at, distance in enumerate(STEPS):
+        step = jnp.where(slot == at, distance, step)
     wanted = (((z + step) % Z) * C + core) * ROWS_DEV + place % ROWS_DEV
     pick = (wanted == source).astype(activations.dtype)
     return lax.dot_general(
@@ -51,42 +55,51 @@
     def product(lhs, rhs):
         return lax.dot_general(lhs, rhs, (((1,), (0,)), ((), ())), preferred_element_type=jnp.float32)
 
-    def ring(k, gate):
-        cols = lax.slice_in_dim(cotangent, k * WIDTH, (k + 1) * WIDTH, axis=1)
-        sent = product(theirs, cols)
-        got = lax.ppermute(sent, "c", SWAP)
-        kept = product(mine, cols)
-        if gate is not None:
-            got, _ = lax.optimization_barrier((got, gate))
+    def after(values, *tokens):
+        return lax.optimization_barrier((values, tokens))[0]
 
-        def own(j, lo=0, hi=WIDTH):
-            j = j % Z
-            r = slice(j * ROWS_DEV, (j + 1) * ROWS_DEV)
-            return kept[r, lo:hi] + got[r, lo:hi]
+    chunks = range(CHUNKS)
+    cols = [lax.slice_in_dim(cotangent, k * WIDTH, (k + 1) * WIDTH, axis=1) for k in chunks]
+    first = [lax.ppermute(product(theirs[:ROWS_DEV], cols[k]), "c", SWAP) for k in chunks]
+    kept = [None] * CHUNKS
+    rest = [None] * CHUNKS
+    up = [None] * CHUNKS
+    down = [None] * CHUNKS
 
-        up = own(4, HALF, WIDTH)
-        down = own(4, 0, HALF)
-        for t in range(4):
-            up = lax.ppermute(up, "z", UP)
-            down = lax.ppermute(down, "z", DOWN)
-            if t == 0:
-                up = jnp.concatenate([own(3, 0, HALF), own(3, HALF, WIDTH) + up], axis=1)
-                down = jnp.concatenate([own(5, 0, HALF) + down, own(5, HALF, WIDTH)], axis=1)
-            elif t < 3:
-                up = own(3 - t) + up
-                down = own(5 + t) + down
-            yield None
-        yield own(0) + up + down
+    def own(k, distance, lo=0, hi=WIDTH):
+        at = STEPS.index(distance) * ROWS_DEV
+        local = kept[k][at : at + ROWS_DEV, lo:hi]
+        if at == 0:
+            return local + first[k][:, lo:hi]
+        return local + rest[k][at - ROWS_DEV : at, lo:hi]
 
-    done = [None] * CHUNKS
-    for first in range(0, CHUNKS, 2):
-        gate = None if first == 0 else done[first - 2][:8, :128]
-        rings = [ring(k, gate) for k in (first, first + 1)]
-        for t in range(5):
-            for i in range(2):
-                done[first + i] = next(rings[i])
+    lhs = mine
+    for k in chunks:
+        kept[k] = product(lhs, cols[k])
+        up[k] = own(k, 4, HALF, WIDTH)
+        down[k] = own(k, 4, 0, HALF)
+        lhs = after(mine, up[k], down[k])
+    lhs = after(theirs[ROWS_DEV:], up[-1], down[-1])
+    for k in chunks:
+        sent = product(lhs, cols[k])
+        rest[k] = lax.ppermute(sent, "c", SWAP)
+        lhs = after(theirs[ROWS_DEV:], sent)
+    last = (up[-1], down[-1])
+    for t in range(1, 5):
+        for k in chunks:
+            moved = (lax.ppermute(up[k], "z", UP), lax.ppermute(down[k], "z", DOWN))
+            u, d = after(moved, last)
+            if t == 1:
+                up[k] = jnp.concatenate([own(k, 3, 0, HALF), own(k, 3, HALF, WIDTH) + u], axis=1)
+                down[k] = jnp.concatenate([own(k, 5, 0, HALF) + d, own(k, 5, HALF, WIDTH)], axis=1)
+            elif t < 4:
+                up[k] = own(k, 4 - t) + u
+                down[k] = own(k, 4 + t) + d
+            else:
+                up[k] = down[k] = own(k, 0) + u + d
+            last = (up[k], down[k])
 
-    gradient = jnp.concatenate(done, axis=1)
+    gradient = jnp.concatenate(up, axis=1)
     correction_one = 1.0 - beta_first**INNER_STEP
     correction_two = 1.0 - beta_second**INNER_STEP
     own_drift = drift[0]

time: 181 us -> 161 us (0.89)
  starting transfers between devices: 56.9 us -> 31.5 us
  waiting for transfers between devices: 62.8 us -> 68.5 us
    ppermute x36 -> x20, starting transfers between devices: 37.4 us -> 22.6 us  [the longest x16 18.6 us: per_device(): moved = (lax.ppermute(up[k], 'z', UP), lax.ppermute(down[k], 'z', DOWN))]
    all_to_all x1, starting transfers between devices: 19.5 us -> 8.85 us  [per_device(): lax.all_to_all(squares, ('z', 'c'), split_axis=0, concat_axis=0, tiled=True)]
    ppermute x36 -> x20, waiting for transfers between devices: 58.4 us -> 64.4 us  [the longest x16 64.4 us: per_device(): moved = (lax.ppermute(up[k], 'z', UP), lax.ppermute(down[k], 'z', DOWN))]
    all_to_all x1, blocking collectives: 19.1 us -> 16.2 us  [per_device(): lax.all_to_all(copies, ('y', 'x'), split_axis=0, concat_axis=0, tiled=True)]
    all_to_all x1, blocking collectives: 18.3 us -> 20.5 us  [per_device(): lax.all_to_all(spread, ('y', 'x'), split_axis=0, concat_axis=0, tiled=True)]
    unnamed x24 -> x16, local copies, waits for them, and re-layouts: 5.19 us -> 3.86 us
    dot_general x8 -> x6, matrix products: 5.66 us -> 6.54 us  [product(): lax.dot_general(lhs, rhs, (((1,), (0,)), ((), ())), preferred_element_typ...]
  transfers between devices with their start and end apart: 37 -> 21, of which waited for: 20 -> 14; matrix products, arithmetic and copies ran while one was open for 5% -> 5% of each run, Pallas kernels for 0% -> 0%
where the time goes in v2:
time: 161 us
  waiting for transfers between devices  68.5 us (43%)
  blocking collectives  36.7 us (23%)
  starting transfers between devices  31.5 us (20%)
  other arithmetic  9.82 us (6%)
  matrix products  7.05 us (4%)
  local copies, waits for them, and re-layouts  5.41 us (3%)
  between operations  1.7 us (1%)
    ppermute x16, waiting for transfers between devices, per_device(): moved = (lax.ppermute(up[k], 'z', UP), lax.ppermute(down[k], 'z', DOWN))  64.4 us
    all_to_all x1, blocking collectives, per_device(): lax.all_to_all(spread, ('y', 'x'), split_axis=0, concat_axis=0, tiled=True)  20.5 us
    ppermute x16, starting transfers between devices, per_device(): moved = (lax.ppermute(up[k], 'z', UP), lax.ppermute(down[k], 'z', DOWN))  18.6 us
    all_to_all x1, blocking collectives, per_device(): lax.all_to_all(copies, ('y', 'x'), split_axis=0, concat_axis=0, tiled=True)  16.2 us
    all_to_all x1, starting transfers between devices, per_device(): lax.all_to_all(squares, ('z', 'c'), split_axis=0, concat_axis=0, tiled=True)  8.85 us
    dot_general x6, matrix products, product(): lax.dot_general(lhs, rhs, (((1,), (0,)), ((), ())), preferred_element_typ...  6.54 us
    all_to_all x1, waiting for transfers between devices, per_device(): lax.all_to_all(squares, ('z', 'c'), split_axis=0, concat_axis=0, tiled=True)  4.1 us
    unnamed x16, local copies, waits for them, and re-layouts  3.86 us
  transfers between devices with their start and end apart: 21, of which 14 were waited for; matrix products, arithmetic and copies ran while one was open for 5% of the time, Pallas kernels for 0%

profile of v2, /device:TPU:1, one launch (start us, length us, event | category | flops | bytes accessed | tf_op | source)
XLA Modules:
  0.0 160.6 jit_solution(4007967948049819989)
XLA Ops:
  0.7 1.0 copy-done
  1.7 0.5 convolution_convert_fusion
  2.2 2.9 %copy-done.2 = bf16[1,512,8192]{2,1,0:T(8,128)(2,1)S(1)} copy-done((bf16[1,512,8192]{2,1,0:T(8,128)(2,1)S(1)}, bf16[1,512,8192]{2,1,0:T(8,128)(2,1)}, u32[]{:S(2)}) %copy-start.2) | copy-done | bytes 8388632
  5.1 0.8 fusion.8
  5.9 3.3 %collective-permute-start = (f32[32,4096]{1,0:T(8,128)S(1)}, f32[32,4096]{1,0:T(8,128)S(1)}, u32[]{:S(2)}, u32[]{:S(2)}) collective-permute-start(f32[32,4096]{1,0:T(8,128)S(1)} %fusion.8), channel_id=1, source_target_pairs={{0,1},{1,0},{2,3},{3,2},{4,5},{5,4},{6,7},{7,6},{8,9},{9,8},{10,11... | collective-permute-start | bytes 1572872 | tf_op jit(solution)/shard_map/ppermute | solution.py:63
  9.1 0.8 fusion.2
  10.0 1.3 fusion.10
  11.4 1.3 fusion.4
  12.8 1.2 fusion.6
  13.9 0.6 collective-permute-start.2
  14.5 1.2 fusion
  15.8 3.9 %collective-permute-start.4 = (f32[32,2048]{1,0:T(8,128)S(1)}, f32[32,2048]{1,0:T(8,128)S(1)}, u32[]{:S(2)}, u32[]{:S(2)}) collective-permute-start(f32[32,2048]{1,0:T(8,128)S(1)} %get-tuple-element.62), channel_id=1, source_target_pairs={{0,14},{2,0},{4,2},{6,4},{8,6},{10,8},{12,10},{14,12},{1,15},{3,1}... | collective-permute-start | bytes 786440 | tf_op jit(solution)/shard_map/ppermute | solution.py:90
  19.7 2.7 %collective-permute-start.9 = (f32[32,2048]{1,0:T(8,128)S(1)}, f32[32,2048]{1,0:T(8,128)S(1)}, u32[]{:S(2)}, u32[]{:S(2)}) collective-permute-start(f32[32,2048]{1,0:T(8,128)S(1)} %get-tuple-element.60), channel_id=1, source_target_pairs={{0,14},{2,0},{4,2},{6,4},{8,6},{10,8},{12,10},{14,12},{1,15},{3,1}... | collective-permute-start | bytes 786440 | tf_op jit(solution)/shard_map/ppermute | solution.py:90
  22.4 2.6 %collective-permute-done.4 = f32[32,2048]{1,0:T(8,128)S(1)} collective-permute-done((f32[32,2048]{1,0:T(8,128)S(1)}, f32[32,2048]{1,0:T(8,128)S(1)}, u32[]{:S(2)}, u32[]{:S(2)}) %collective-permute-start.4) | collective-permute-done | bytes 262176 | tf_op jit(solution)/shard_map/ppermute | solution.py:90
  25.0 3.1 %collective-permute-done.3 = f32[32,2048]{1,0:T(8,128)S(1)} collective-permute-done((f32[32,2048]{1,0:T(8,128)S(1)}, f32[32,2048]{1,0:T(8,128)S(1)}, u32[]{:S(2)}, u32[]{:S(2)}) %collective-permute-start.3) | collective-permute-done | bytes 262176 | tf_op jit(solution)/shard_map/ppermute | solution.py:90
  28.3 0.3 collective-permute-start.5
  28.6 2.7 %collective-permute-start.6 = (f32[32,4096]{1,0:T(8,128)S(1)}, f32[32,4096]{1,0:T(8,128)S(1)}, u32[]{:S(2)}, u32[]{:S(2)}) collective-permute-start(f32[32,4096]{1,0:T(8,128)S(1)} %pad_maximum_fusion.3), channel_id=1, source_target_pairs={{0,14},{2,0},{4,2},{6,4},{8,6},{10,8},{12,10},{14,12},{1,15},{3,1}... | collective-permute-start | bytes 1572872 | tf_op jit(solution)/shard_map/ppermute | solution.py:90
  31.3 1.5 collective-permute-done.8
  33.2 2.7 %collective-permute-start.13 = (f32[32,4096]{1,0:T(8,128)S(1)}, f32[32,4096]{1,0:T(8,128)S(1)}, u32[]{:S(2)}, u32[]{:S(2)}) collective-permute-start(f32[32,4096]{1,0:T(8,128)S(1)} %pad_maximum_fusion.5), channel_id=1, source_target_pairs={{0,14},{2,0},{4,2},{6,4},{8,6},{10,8},{12,10},{14,12},{1,15},{3,1}... | collective-permute-start | bytes 1572872 | tf_op jit(solution)/shard_map/ppermute | solution.py:90
  36.0 8.1 %collective-permute-done.5 = f32[32,4096]{1,0:T(8,128)S(1)} collective-permute-done((f32[32,4096]{1,0:T(8,128)S(1)}, f32[32,4096]{1,0:T(8,128)S(1)}, u32[]{:S(2)}, u32[]{:S(2)}) %collective-permute-start.5) | collective-permute-done | bytes 524320 | tf_op jit(solution)/shard_map/ppermute | solution.py:90
  44.3 1.3 collective-permute-start.11
  45.5 0.3 collective-permute-start.10
  45.8 9.5 %collective-permute-done.12 = f32[32,4096]{1,0:T(8,128)S(1)} collective-permute-done((f32[32,4096]{1,0:T(8,128)S(1)}, f32[32,4096]{1,0:T(8,128)S(1)}, u32[]{:S(2)}, u32[]{:S(2)}) %collective-permute-start.12) | collective-permute-done | bytes 524320 | tf_op jit(solution)/shard_map/ppermute | solution.py:90
  55.3 0.2 fusion.35
  55.6 1.3 collective-permute-start.17
  56.8 0.3 collective-permute-start.16
  57.1 6.0 %collective-permute-done.11 = f32[32,4096]{1,0:T(8,128)S(1)} collective-permute-done((f32[32,4096]{1,0:T(8,128)S(1)}, f32[32,4096]{1,0:T(8,128)S(1)}, u32[]{:S(2)}, u32[]{:S(2)}) %collective-permute-start.11) | collective-permute-done | bytes 524320 | tf_op jit(solution)/shard_map/ppermute | solution.py:90
  63.1 3.4 %collective-permute-done.10 = f32[32,4096]{1,0:T(8,128)S(1)} collective-permute-done((f32[32,4096]{1,0:T(8,128)S(1)}, f32[32,4096]{1,0:T(8,128)S(1)}, u32[]{:S(2)}, u32[]{:S(2)}) %collective-permute-start.10) | collective-permute-done | bytes 524320 | tf_op jit(solution)/shard_map/ppermute | solution.py:90
  66.8 1.3 collective-permute-start.15
  68.0 0.4 collective-permute-start.14
  68.4 6.0 %collective-permute-done.17 = f32[32,4096]{1,0:T(8,128)S(1)} collective-permute-done((f32[32,4096]{1,0:T(8,128)S(1)}, f32[32,4096]{1,0:T(8,128)S(1)}, u32[]{:S(2)}, u32[]{:S(2)}) %collective-permute-start.17) | collective-permute-done | bytes 524320 | tf_op jit(solution)/shard_map/ppermute | solution.py:90
  74.4 3.4 %collective-permute-done.16 = f32[32,4096]{1,0:T(8,128)S(1)} collective-permute-done((f32[32,4096]{1,0:T(8,128)S(1)}, f32[32,4096]{1,0:T(8,128)S(1)}, u32[]{:S(2)}, u32[]{:S(2)}) %collective-permute-start.16) | collective-permute-done | bytes 524320 | tf_op jit(solution)/shard_map/ppermute | solution.py:90
  78.0 1.3 collective-permute-start.19
  79.3 0.3 collective-permute-start.18
  79.6 6.1 %collective-permute-done.15 = f32[32,4096]{1,0:T(8,128)S(1)} collective-permute-done((f32[32,4096]{1,0:T(8,128)S(1)}, f32[32,4096]{1,0:T(8,128)S(1)}, u32[]{:S(2)}, u32[]{:S(2)}) %collective-permute-start.15) | collective-permute-done | bytes 524320 | tf_op jit(solution)/shard_map/ppermute | solution.py:90
  85.6 3.4 %collective-permute-done.14 = f32[32,4096]{1,0:T(8,128)S(1)} collective-permute-done((f32[32,4096]{1,0:T(8,128)S(1)}, f32[32,4096]{1,0:T(8,128)S(1)}, u32[]{:S(2)}, u32[]{:S(2)}) %collective-permute-start.14) | collective-permute-done | bytes 524320 | tf_op jit(solution)/shard_map/ppermute | solution.py:90
  89.2 7.7 %collective-permute-done.19 = f32[32,4096]{1,0:T(8,128)S(1)} collective-permute-done((f32[32,4096]{1,0:T(8,128)S(1)}, f32[32,4096]{1,0:T(8,128)S(1)}, u32[]{:S(2)}, u32[]{:S(2)}) %collective-permute-start.19) | collective-permute-done | bytes 524320 | tf_op jit(solution)/shard_map/ppermute | solution.py:90
  96.9 3.4 %collective-permute-done.18 = f32[32,4096]{1,0:T(8,128)S(1)} collective-permute-done((f32[32,4096]{1,0:T(8,128)S(1)}, f32[32,4096]{1,0:T(8,128)S(1)}, u32[]{:S(2)}, u32[]{:S(2)}) %collective-permute-start.18) | collective-permute-done | bytes 524320 | tf_op jit(solution)/shard_map/ppermute | solution.py:90
  100.5 0.8 bitcast_subtract_fusion
  101.4 20.5 %all_to_all.15 = f32[16,32,512]{2,1,0:T(8,128)S(1)} all-to-all(f32[16,32,512]{2,1,0:T(8,128)S(1)} %bitcast.50), channel_id=1, replica_groups=mesh['y'=4,'x'=4,'z'=8,'c'=2] {'y','x'}, dimensions={0} | all-to-all | bytes 2097152 | tf_op jit(solution)/shard_map/all_to_all | solution.py:116
  122.2 16.2 %all_to_all.16 = f32[16,32,512]{2,1,0:T(8,128)S(1)} all-to-all(f32[16,32,512]{2,1,0:T(8,128)S(1)} %broadcast_in_dim.33), channel_id=1, replica_groups=mesh['y'=4,'x'=4,'z'=8,'c'=2] {'y','x'}, dimensions={0} | all-to-all | bytes 2097152 | tf_op jit(solution)/shard_map/all_to_all | solution.py:119
  138.3 0.9 multiply_reduce_fusion
  139.2 1.2 broadcast_in_dim.34
  140.5 8.8 %all-to-all-start.2 = ((f32[16,1,128]{2,1,0:T(1,128)}), f32[16,1,128]{2,1,0:T(1,128)S(1)}, u32[]{:S(2)}, u32[]{:S(2)}) async-start(f32[16,1,128]{2,1,0:T(1,128)} %broadcast_in_dim.34), calls=%async_computation.2 | async-start | bytes 16384 | tf_op jit(solution)/shard_map/all_to_all | solution.py:122
  149.3 2.8 %fusion.18 = (f32[1,32,8192]{2,1,0:T(8,128)}, f32[1,32,8192]{2,1,0:T(8,128)}) fusion(f32[1,32,8192]{2,1,0:T(8,128)S(1)} %copy-done.3, f32[1,32,4096]{2,1,0:T(8,128)S(1)} %bitcast.48, f32[1,32,4096]{2,1,0:T(8,128)S(1)} %bitcast.47, f32[1,32,8192]{2,1,0:T(8,128)} %param.11), kind=kLoop, calls=%fused_computation.29 | loop fusion | flops 2097152 | bytes 5242880 | tf_op jit(solution)/shard_map/add | solution.py:107
  152.1 4.1 %all-to-all-done.2 = f32[16,1,128]{2,1,0:T(1,128)S(1)} async-done(((f32[16,1,128]{2,1,0:T(1,128)}), f32[16,1,128]{2,1,0:T(1,128)S(1)}, u32[]{:S(2)}, u32[]{:S(2)}) %all-to-all-start.2) | async-done | bytes 8224 | tf_op jit(solution)/shard_map/all_to_all | solution.py:122
  156.2 0.6 slice_reduce_fusion
  157.8 2.8 %multiply_subtract_fusion = (f32[32,8192]{1,0:T(8,128)}, f32[32,8192]{1,0:T(8,128)}) fusion(f32[32,8192]{1,0:T(8,128)S(1)} %copy-done.6, f32[32,8192]{1,0:T(8,128)S(1)} %bitcast.49, f32[32,8192]{1,0:T(8,128)} %param.13), kind=kLoop, calls=%fused_computation.45 | loop fusion | flops 1572864 | bytes 5242880 | tf_op jit(solution)/shard_map/sub | solution.py:127
  (52 shorter events, 2.2 us)
Async XLA Ops:
  0.6 1.1 copy-start
  1.7 3.4 %copy-start.2 = (bf16[1,512,8192]{2,1,0:T(8,128)(2,1)S(1)}, bf16[1,512,8192]{2,1,0:T(8,128)(2,1)}, u32[]{:S(2)}) copy-start(bf16[1,512,8192]{2,1,0:T(8,128)(2,1)} %param.8) | copy-start | bytes 25165828
  5.9 5.4 %collective-permute-start = (f32[32,4096]{1,0:T(8,128)S(1)}, f32[32,4096]{1,0:T(8,128)S(1)}, u32[]{:S(2)}, u32[]{:S(2)}) collective-permute-start(f32[32,4096]{1,0:T(8,128)S(1)} %fusion.8), channel_id=1, source_target_pairs={{0,1},{1,0},{2,3},{3,2},{4,5},{5,4},{6,7},{7,6},{8,9},{9,8},{10,11... | collective-permute-start | bytes 1572872 | tf_op jit(solution)/shard_map/ppermute | solution.py:63
  10.0 2.7 %collective-permute-start.1 = (f32[32,4096]{1,0:T(8,128)S(1)}, f32[32,4096]{1,0:T(8,128)S(1)}, u32[]{:S(2)}, u32[]{:S(2)}) collective-permute-start(f32[32,4096]{1,0:T(8,128)S(1)} %fusion.2), channel_id=1, source_target_pairs={{0,1},{1,0},{2,3},{3,2},{4,5},{5,4},{6,7},{7,6},{8,9},{9,8},{10,11... | collective-permute-start | bytes 1572872 | tf_op jit(solution)/shard_map/ppermute | solution.py:63
  13.9 14.1 %collective-permute-start.2 = (f32[224,4096]{1,0:T(8,128)S(1)}, f32[224,4096]{1,0:T(8,128)S(1)}, u32[]{:S(2)}, u32[]{:S(2)}) collective-permute-start(f32[224,4096]{1,0:T(8,128)S(1)} %fusion.6), channel_id=1, source_target_pairs={{0,1},{1,0},{2,3},{3,2},{4,5},{5,4},{6,7},{7,6},{8,9},{9,8},{10,11... | collective-permute-start | bytes 11010056 | tf_op jit(solution)/shard_map/ppermute | solution.py:85
  15.7 17.2 %collective-permute-start.7 = (f32[224,4096]{1,0:T(8,128)S(1)}, f32[224,4096]{1,0:T(8,128)S(1)}, u32[]{:S(2)}, u32[]{:S(2)}) collective-permute-start(f32[224,4096]{1,0:T(8,128)S(1)} %fusion), channel_id=1, source_target_pairs={{0,1},{1,0},{2,3},{3,2},{4,5},{5,4},{6,7},{7,6},{8,9},{9,8},{10,11... | collective-permute-start | bytes 11010056 | tf_op jit(solution)/shard_map/ppermute | solution.py:85
  15.8 9.2 %collective-permute-start.4 = (f32[32,2048]{1,0:T(8,128)S(1)}, f32[32,2048]{1,0:T(8,128)S(1)}, u32[]{:S(2)}, u32[]{:S(2)}) collective-permute-start(f32[32,2048]{1,0:T(8,128)S(1)} %get-tuple-element.62), channel_id=1, source_target_pairs={{0,14},{2,0},{4,2},{6,4},{8,6},{10,8},{12,10},{14,12},{1,15},{3,1}... | collective-permute-start | bytes 786440 | tf_op jit(solution)/shard_map/ppermute | solution.py:90
  19.7 8.4 %collective-permute-start.3 = (f32[32,2048]{1,0:T(8,128)S(1)}, f32[32,2048]{1,0:T(8,128)S(1)}, u32[]{:S(2)}, u32[]{:S(2)}) collective-permute-start(f32[32,2048]{1,0:T(8,128)S(1)} %get-tuple-element.63), channel_id=1, source_target_pairs={{0,2},{2,4},{4,6},{6,8},{8,10},{10,12},{12,14},{14,0},{1,3},{3,5},... | collective-permute-start | bytes 786440 | tf_op jit(solution)/shard_map/ppermute | solution.py:90
  19.7 11.6 %collective-permute-start.9 = (f32[32,2048]{1,0:T(8,128)S(1)}, f32[32,2048]{1,0:T(8,128)S(1)}, u32[]{:S(2)}, u32[]{:S(2)}) collective-permute-start(f32[32,2048]{1,0:T(8,128)S(1)} %get-tuple-element.60), channel_id=1, source_target_pairs={{0,14},{2,0},{4,2},{6,4},{8,6},{10,8},{12,10},{14,12},{1,15},{3,1}... | collective-permute-start | bytes 786440 | tf_op jit(solution)/shard_map/ppermute | solution.py:90
  25.0 7.9 %collective-permute-start.8 = (f32[32,2048]{1,0:T(8,128)S(1)}, f32[32,2048]{1,0:T(8,128)S(1)}, u32[]{:S(2)}, u32[]{:S(2)}) collective-permute-start(f32[32,2048]{1,0:T(8,128)S(1)} %get-tuple-element.61), channel_id=1, source_target_pairs={{0,2},{2,4},{4,6},{6,8},{8,10},{10,12},{12,14},{14,0},{1,3},{3,5},... | collective-permute-start | bytes 786440 | tf_op jit(solution)/shard_map/ppermute | solution.py:90
  28.3 15.8 %collective-permute-start.5 = (f32[32,4096]{1,0:T(8,128)S(1)}, f32[32,4096]{1,0:T(8,128)S(1)}, u32[]{:S(2)}, u32[]{:S(2)}) collective-permute-start(f32[32,4096]{1,0:T(8,128)S(1)} %pad_maximum_fusion.2), channel_id=1, source_target_pairs={{0,2},{2,4},{4,6},{6,8},{8,10},{10,12},{12,14},{14,0},{1,3},{3,5},... | collective-permute-start | bytes 1572872 | tf_op jit(solution)/shard_map/ppermute | solution.py:90
  28.6 15.5 %collective-permute-start.6 = (f32[32,4096]{1,0:T(8,128)S(1)}, f32[32,4096]{1,0:T(8,128)S(1)}, u32[]{:S(2)}, u32[]{:S(2)}) collective-permute-start(f32[32,4096]{1,0:T(8,128)S(1)} %pad_maximum_fusion.3), channel_id=1, source_target_pairs={{0,14},{2,0},{4,2},{6,4},{8,6},{10,8},{12,10},{14,12},{1,15},{3,1}... | collective-permute-start | bytes 1572872 | tf_op jit(solution)/shard_map/ppermute | solution.py:90
  33.1 22.2 %collective-permute-start.12 = (f32[32,4096]{1,0:T(8,128)S(1)}, f32[32,4096]{1,0:T(8,128)S(1)}, u32[]{:S(2)}, u32[]{:S(2)}) collective-permute-start(f32[32,4096]{1,0:T(8,128)S(1)} %pad_maximum_fusion.4), channel_id=1, source_target_pairs={{0,2},{2,4},{4,6},{6,8},{8,10},{10,12},{12,14},{14,0},{1,3},{3,5},... | collective-permute-start | bytes 1572872 | tf_op jit(solution)/shard_map/ppermute | solution.py:90
  33.2 22.1 %collective-permute-start.13 = (f32[32,4096]{1,0:T(8,128)S(1)}, f32[32,4096]{1,0:T(8,128)S(1)}, u32[]{:S(2)}, u32[]{:S(2)}) collective-permute-start(f32[32,4096]{1,0:T(8,128)S(1)} %pad_maximum_fusion.5), channel_id=1, source_target_pairs={{0,14},{2,0},{4,2},{6,4},{8,6},{10,8},{12,10},{14,12},{1,15},{3,1}... | collective-permute-start | bytes 1572872 | tf_op jit(solution)/shard_map/ppermute | solution.py:90
  44.3 18.9 %collective-permute-start.11 = (f32[32,4096]{1,0:T(8,128)S(1)}, f32[32,4096]{1,0:T(8,128)S(1)}, u32[]{:S(2)}, u32[]{:S(2)}) collective-permute-start(f32[32,4096]{1,0:T(8,128)S(1)} %get-tuple-element.50), channel_id=1, source_target_pairs={{0,14},{2,0},{4,2},{6,4},{8,6},{10,8},{12,10},{14,12},{1,15},{3,1}... | collective-permute-start | bytes 1572872 | tf_op jit(solution)/shard_map/ppermute | solution.py:90
  45.5 21.1 %collective-permute-start.10 = (f32[32,4096]{1,0:T(8,128)S(1)}, f32[32,4096]{1,0:T(8,128)S(1)}, u32[]{:S(2)}, u32[]{:S(2)}) collective-permute-start(f32[32,4096]{1,0:T(8,128)S(1)} %get-tuple-element.51), channel_id=1, source_target_pairs={{0,2},{2,4},{4,6},{6,8},{8,10},{10,12},{12,14},{14,0},{1,3},{3,5},... | collective-permute-start | bytes 1572872 | tf_op jit(solution)/shard_map/ppermute | solution.py:90
  55.6 18.8 %collective-permute-start.17 = (f32[32,4096]{1,0:T(8,128)S(1)}, f32[32,4096]{1,0:T(8,128)S(1)}, u32[]{:S(2)}, u32[]{:S(2)}) collective-permute-start(f32[32,4096]{1,0:T(8,128)S(1)} %get-tuple-element.48), channel_id=1, source_target_pairs={{0,14},{2,0},{4,2},{6,4},{8,6},{10,8},{12,10},{14,12},{1,15},{3,1}... | collective-permute-start | bytes 1572872 | tf_op jit(solution)/shard_map/ppermute | solution.py:90
  56.8 21.0 %collective-permute-start.16 = (f32[32,4096]{1,0:T(8,128)S(1)}, f32[32,4096]{1,0:T(8,128)S(1)}, u32[]{:S(2)}, u32[]{:S(2)}) collective-permute-start(f32[32,4096]{1,0:T(8,128)S(1)} %get-tuple-element.49), channel_id=1, source_target_pairs={{0,2},{2,4},{4,6},{6,8},{8,10},{10,12},{12,14},{14,0},{1,3},{3,5},... | collective-permute-start | bytes 1572872 | tf_op jit(solution)/shard_map/ppermute | solution.py:90
  66.8 18.9 %collective-permute-start.15 = (f32[32,4096]{1,0:T(8,128)S(1)}, f32[32,4096]{1,0:T(8,128)S(1)}, u32[]{:S(2)}, u32[]{:S(2)}) collective-permute-start(f32[32,4096]{1,0:T(8,128)S(1)} %get-tuple-element.46), channel_id=1, source_target_pairs={{0,14},{2,0},{4,2},{6,4},{8,6},{10,8},{12,10},{14,12},{1,15},{3,1}... | collective-permute-start | bytes 1572872 | tf_op jit(solution)/shard_map/ppermute | solution.py:90
  68.0 32.4 %copy-start.3 = (f32[1,32,8192]{2,1,0:T(8,128)S(1)}, f32[1,32,8192]{2,1,0:T(8,128)}, u32[]{:S(2)}) copy-start(f32[1,32,8192]{2,1,0:T(8,128)} %param.12) | copy-start | bytes 3145732
  68.0 32.4 %copy-start.4 = (f32[1,32,8192]{2,1,0:T(8,128)S(1)}, f32[1,32,8192]{2,1,0:T(8,128)}, u32[]{:S(2)}) copy-start(f32[1,32,8192]{2,1,0:T(8,128)} %param.11) | copy-start | bytes 3145732
  68.0 32.4 %copy-start.5 = (f32[32,8192]{1,0:T(8,128)S(1)}, f32[32,8192]{1,0:T(8,128)}, u32[]{:S(2)}) copy-start(f32[32,8192]{1,0:T(8,128)} %param.9) | copy-start | bytes 3145732
  68.0 32.4 %copy-start.7 = (f32[1,32,8192]{2,1,0:T(8,128)S(1)}, f32[1,32,8192]{2,1,0:T(8,128)}, u32[]{:S(2)}) copy-start(f32[1,32,8192]{2,1,0:T(8,128)} %param.10) | copy-start | bytes 3145732
  68.0 21.0 %collective-permute-start.14 = (f32[32,4096]{1,0:T(8,128)S(1)}, f32[32,4096]{1,0:T(8,128)S(1)}, u32[]{:S(2)}, u32[]{:S(2)}) collective-permute-start(f32[32,4096]{1,0:T(8,128)S(1)} %get-tuple-element.47), channel_id=1, source_target_pairs={{0,2},{2,4},{4,6},{6,8},{8,10},{10,12},{12,14},{14,0},{1,3},{3,5},... | collective-permute-start | bytes 1572872 | tf_op jit(solution)/shard_map/ppermute | solution.py:90
  78.0 18.8 %collective-permute-start.19 = (f32[32,4096]{1,0:T(8,128)S(1)}, f32[32,4096]{1,0:T(8,128)S(1)}, u32[]{:S(2)}, u32[]{:S(2)}) collective-permute-start(f32[32,4096]{1,0:T(8,128)S(1)} %get-tuple-element.44), channel_id=1, source_target_pairs={{0,14},{2,0},{4,2},{6,4},{8,6},{10,8},{12,10},{14,12},{1,15},{3,1}... | collective-permute-start | bytes 1572872 | tf_op jit(solution)/shard_map/ppermute | solution.py:90
  79.3 21.0 %collective-permute-start.18 = (f32[32,4096]{1,0:T(8,128)S(1)}, f32[32,4096]{1,0:T(8,128)S(1)}, u32[]{:S(2)}, u32[]{:S(2)}) collective-permute-start(f32[32,4096]{1,0:T(8,128)S(1)} %get-tuple-element.45), channel_id=1, source_target_pairs={{0,2},{2,4},{4,6},{6,8},{8,10},{10,12},{12,14},{14,0},{1,3},{3,5},... | collective-permute-start | bytes 1572872 | tf_op jit(solution)/shard_map/ppermute | solution.py:90
  140.5 15.8 %all-to-all-start.2 = ((f32[16,1,128]{2,1,0:T(1,128)}), f32[16,1,128]{2,1,0:T(1,128)S(1)}, u32[]{:S(2)}, u32[]{:S(2)}) async-start(f32[16,1,128]{2,1,0:T(1,128)} %broadcast_in_dim.34), calls=%async_computation.2 | async-start | bytes 16384 | tf_op jit(solution)/shard_map/all_to_all | solution.py:122
  152.1 5.7 %copy-start.6 = (f32[32,8192]{1,0:T(8,128)S(1)}, f32[32,8192]{1,0:T(8,128)}, u32[]{:S(2)}) copy-start(f32[32,8192]{1,0:T(8,128)} %param.9) | copy-start | bytes 3145732
  157.6 3.0 %copy-start.1 = (bf16[1,512,512]{2,1,0:T(8,128)(2,1)S(1)}, bf16[1,512,512]{2,1,0:T(8,128)(2,1)}, u32[]{:S(2)}) copy-start(bf16[1,512,512]{2,1,0:T(8,128)(2,1)} %param.7) | copy-start | bytes 1572868

commit v3 on v2

--- a/solution.py
+++ b/solution.py
@@ -3,6 +3,8 @@
 import jax
 import jax.numpy as jnp
 from jax import lax
+from jax.experimental import pallas as pl
+from jax.experimental.pallas import tpu as pltpu
 from jax.sharding import Mesh, PartitionSpec as P
 
 D = 8192
@@ -44,6 +46,59 @@
     ).astype(activations.dtype)
 
 
+def square_kernel(pieces_ref, out_ref):
+    def add(p, total):
+        x = pieces_ref[p]
+        x = x * x
+        for r in range(0, ROWS_DEV, 8):
+            for l in range(0, x.shape[1], 128):
+                total = total + x[r : r + 8, l : l + 128]
+        return total
+
+    total = lax.fori_loop(0, pieces_ref.shape[0], add, jnp.zeros((8, 128), jnp.float32))
+    out_ref[...] = jnp.broadcast_to(total[None], out_ref.shape)
+
+
+def squares_of(pieces):
+    return pl.pallas_call(
+        square_kernel,
+        out_shape=jax.ShapeDtypeStruct((PARTS, 8, 128), jnp.float32),
+        cost_estimate=pl.CostEstimate(flops=2 * pieces.size, bytes_accessed=4 * pieces.size, transcendentals=0),
+    )(pieces)
+
+
+def finish_kernel(squares_ref, pieces_ref, anchor_ref, momentum_ref, momentum_out, anchor_out):
+    squares = jnp.sum(jnp.sum(squares_ref[...], axis=0), keepdims=True)
+    ceiling = 0.3 * math.sqrt(ROWS_DEV * PARTS * D)
+    factor = ceiling / jnp.maximum(jnp.sqrt(squares), ceiling)
+    piece = pieces_ref.shape[2]
+    for p in range(pieces_ref.shape[0]):
+        at = slice(p * piece, (p + 1) * piece)
+        scaled = factor * pieces_ref[p]
+        momentum = momentum_coef * momentum_ref[:, at] + scaled
+        momentum_out[:, at] = momentum
+        anchor_out[:, at] = anchor_ref[:, at] - outer_rate * (scaled + momentum_coef * momentum)
+
+
+def finish(squares, pieces, anchor, outer_momentum):
+    replicas, _, both = pieces.shape
+    part = pl.BlockSpec((ROWS_DEV, WIDTH), lambda h: (0, h))
+    shape = jax.ShapeDtypeStruct(anchor.shape, jnp.float32)
+    return pl.pallas_call(
+        finish_kernel,
+        grid=(CHUNKS,),
+        in_specs=[
+            pl.BlockSpec(squares.shape, lambda h: (0, 0, 0)),
+            pl.BlockSpec((replicas, ROWS_DEV, both // CHUNKS), lambda h: (0, 0, h)),
+            part,
+            part,
+        ],
+        out_specs=[part, part],
+        out_shape=[shape, shape],
+        cost_estimate=pl.CostEstimate(flops=7 * anchor.size, bytes_accessed=20 * anchor.size, transcendentals=0),
+    )(squares, pieces, anchor, outer_momentum)
+
+
 def per_device(hidden_acts, out_grads, anchor, drift, adam_first, adam_second, outer_momentum):
     z = lax.axis_index("z")
     c = lax.axis_index("c")
@@ -73,58 +128,73 @@
             return local + first[k][:, lo:hi]
         return local + rest[k][at - ROWS_DEV : at, lo:hi]
 
-    lhs = mine
-    for k in chunks:
+    def start_ring(k, lhs):
         kept[k] = product(lhs, cols[k])
         up[k] = own(k, 4, HALF, WIDTH)
         down[k] = own(k, 4, 0, HALF)
-        lhs = after(mine, up[k], down[k])
-    lhs = after(theirs[ROWS_DEV:], up[-1], down[-1])
-    for k in chunks:
+
+    def swap_rest(k, lhs):
         sent = product(lhs, cols[k])
         rest[k] = lax.ppermute(sent, "c", SWAP)
-        lhs = after(theirs[ROWS_DEV:], sent)
-    last = (up[-1], down[-1])
-    for t in range(1, 5):
-        for k in chunks:
-            moved = (lax.ppermute(up[k], "z", UP), lax.ppermute(down[k], "z", DOWN))
-            u, d = after(moved, last)
-            if t == 1:
-                up[k] = jnp.concatenate([own(k, 3, 0, HALF), own(k, 3, HALF, WIDTH) + u], axis=1)
-                down[k] = jnp.concatenate([own(k, 5, 0, HALF) + d, own(k, 5, HALF, WIDTH)], axis=1)
-            elif t < 4:
-                up[k] = own(k, 4 - t) + u
-                down[k] = own(k, 4 + t) + d
-            else:
-                up[k] = down[k] = own(k, 0) + u + d
-            last = (up[k], down[k])
-
-    gradient = jnp.concatenate(up, axis=1)
+        return sent
+
+    def move(k, *tokens):
+        moved = (lax.ppermute(up[k], "z", UP), lax.ppermute(down[k], "z", DOWN))
+        return after(moved, *tokens)
+
+    def step(k, t, u, d):
+        if t == 1:
+            up[k] = jnp.concatenate([own(k, 3, 0, HALF), own(k, 3, HALF, WIDTH) + u], axis=1)
+            down[k] = jnp.concatenate([own(k, 5, 0, HALF) + d, own(k, 5, HALF, WIDTH)], axis=1)
+        else:
+            up[k] = own(k, 4 - t) + u
+            down[k] = own(k, 4 + t) + d
+
     correction_one = 1.0 - beta_first**INNER_STEP
     correction_two = 1.0 - beta_second**INNER_STEP
-    own_drift = drift[0]
-    moment_one = beta_first * adam_first[0] + (1.0 - beta_first) * gradient
-    moment_two = beta_second * adam_second[0] + (1.0 - beta_second) * gradient * gradient
-    update = moment_one / correction_one / (
-        jnp.sqrt(moment_two / correction_two) + 1e-08
-    ) + decay_weight * (anchor + own_drift)
-    pseudo = inner_rate * update - own_drift
-
     replicas = Y * X
-    piece = D // replicas
-    spread = pseudo.reshape(ROWS_DEV, replicas, piece).transpose(1, 0, 2)
-    met = lax.all_to_all(spread, ("y", "x"), split_axis=0, concat_axis=0, tiled=True)
-    part = jnp.sum(met, axis=0) / replicas
-    copies = jnp.broadcast_to(part[None], (replicas, ROWS_DEV, piece))
+    piece = WIDTH // replicas
+
+    def moments(first_old, second_old, gradient):
+        moment_one = beta_first * first_old + (1.0 - beta_first) * gradient
+        moment_two = beta_second * second_old + (1.0 - beta_second) * gradient * gradient
+        return moment_one, moment_two
+
+    def meet(k, gradient):
+        at = slice(k * WIDTH, (k + 1) * WIDTH)
+        own_drift = drift[0, :, at]
+        moment_one, moment_two = moments(adam_first[0, :, at], adam_second[0, :, at], gradient)
+        update = moment_one / correction_one / (
+            jnp.sqrt(moment_two / correction_two) + 1e-08
+        ) + decay_weight * (anchor[:, at] + own_drift)
+        pseudo = inner_rate * update - own_drift
+        spread = pseudo.reshape(ROWS_DEV, replicas, piece).transpose(1, 0, 2)
+        return lax.all_to_all(spread, ("y", "x"), split_axis=0, concat_axis=0, tiled=True)
+
+    start_ring(0, mine)
+    sent = swap_rest(0, after(theirs[ROWS_DEV:], up[0], down[0]))
+    start_ring(1, after(mine, sent))
+    step(0, 1, *move(0, up[1], down[1]))
+    u, d = move(1, up[0], down[0])
+    swap_rest(1, after(theirs[ROWS_DEV:], up[0], down[0]))
+    step(1, 1, u, d)
+    for t in (2, 3):
+        step(0, t, *move(0, up[1], down[1]))
+        step(1, t, *move(1, up[0], down[0]))
+    u, d = move(0, up[1], down[1])
+    gradients = [own(0, 0) + u + d]
+    met = [meet(0, gradients[0])]
+    u, d = move(1, met[0])
+    gradients.append(own(1, 0) + u + d)
+    met.append(meet(1, gradients[1]))
+
+    gradient = jnp.concatenate(gradients, axis=1)
+    moment_one, moment_two = moments(adam_first[0], adam_second[0], gradient)
+    part = jnp.concatenate([jnp.sum(m, axis=0) / replicas for m in met], axis=1)
+    copies = jnp.broadcast_to(part[None], (replicas, ROWS_DEV, CHUNKS * piece))
     pieces = lax.all_to_all(copies, ("y", "x"), split_axis=0, concat_axis=0, tiled=True)
-    average = pieces.transpose(1, 0, 2).reshape(ROWS_DEV, D)
-    squares = jnp.broadcast_to(jnp.sum(pieces * pieces), (PARTS, 1, 128))
-    squares = lax.all_to_all(squares, ("z", "c"), split_axis=0, concat_axis=0, tiled=True)
-    squares = jnp.sum(squares[:, 0, 0])
-    ceiling = 0.3 * math.sqrt(ROWS_DEV * PARTS * D)
-    factor = ceiling / jnp.maximum(jnp.sqrt(squares), ceiling)
-    momentum = momentum_coef * outer_momentum + factor * average
-    updated = anchor - outer_rate * (factor * average + momentum_coef * momentum)
+    squares = lax.all_to_all(squares_of(pieces), ("z", "c"), split_axis=0, concat_axis=0, tiled=True)
+    momentum, updated = finish(squares, pieces, anchor, outer_momentum)
     return (moment_one[None], moment_two[None], momentum, updated)
 
 

time: 161 us -> 166 us (1.031)
  Pallas kernels: 0 us -> 5.26 us
  blocking collectives: 36.7 us -> 32.4 us
  starting transfers between devices: 31.5 us -> 35.3 us
  waiting for transfers between devices: 68.5 us -> 71.9 us
  other arithmetic: 9.82 us -> 7.11 us
    all_to_all x1 -> x2, waiting for transfers between devices: 4.1 us -> 14.1 us  [the longest x1 8.94 us: meet(): lax.all_to_all(spread, ('y', 'x'), split_axis=0, concat_axis=0, tiled=True)]
    ppermute x18, waiting for transfers between devices: 64.4 us -> 57 us  [the longest x16 57 us: move(): moved = (lax.ppermute(up[k], 'z', UP), lax.ppermute(down[k], 'z', DOWN))]
    pallas_call x0 -> x2, Pallas kernels: none -> 5.26 us  [the longest x1 3.1 us: finish(): pl.pallas_call(finish_kernel, grid=(CHUNKS,), in_specs=[pl.BlockSpec(squa...]
    all_to_all x1, blocking collectives: 20.5 us -> 16 us  [meet(): lax.all_to_all(spread, ('y', 'x'), split_axis=0, concat_axis=0, tiled=True)]
    all_to_all x1 -> x2, starting transfers between devices: 8.85 us -> 12.6 us  [the longest x1 8.41 us: per_device(): lax.all_to_all(squares_of(pieces), ('z', 'c'), split_axis=0, concat_axis=...]
    sub x2, other arithmetic: 3.64 us -> 1.77 us  [meet(): pseudo = inner_rate * update - own_drift]
    add x9 -> x7, other arithmetic: 4.2 us -> 3.93 us  [the longest x1 2.71 us: moments(): beta_second * second_old + (1.0 - beta_second) * gradient * gradient]
  transfers between devices with their start and end apart: 21 -> 22, of which waited for: 14 -> 16; matrix products, arithmetic and copies ran while one was open for 5% -> 5% of each run, Pallas kernels for 0% -> 0%
where the time goes in v3:
time: 166 us; the launch traced here: 165 us
  waiting for transfers between devices  71.9 us (43%)
  starting transfers between devices  35.3 us (21%)
  blocking collectives  32.4 us (20%)
  other arithmetic  7.11 us (4%)
  matrix products  6.9 us (4%)
  local copies, waits for them, and re-layouts  5.52 us (3%)
  Pallas kernels  5.26 us (3%)
    ppermute x16, waiting for transfers between devices, move(): moved = (lax.ppermute(up[k], 'z', UP), lax.ppermute(down[k], 'z', DOWN))  57 us
    ppermute x16, starting transfers between devices, move(): moved = (lax.ppermute(up[k], 'z', UP), lax.ppermute(down[k], 'z', DOWN))  17.2 us
    all_to_all x1, blocking collectives, per_device(): lax.all_to_all(copies, ('y', 'x'), split_axis=0, concat_axis=0, tiled=True)  16.4 us
    all_to_all x1, blocking collectives, meet(): lax.all_to_all(spread, ('y', 'x'), split_axis=0, concat_axis=0, tiled=True)  16 us
    all_to_all x1, waiting for transfers between devices, meet(): lax.all_to_all(spread, ('y', 'x'), split_axis=0, concat_axis=0, tiled=True)  8.94 us
    all_to_all x1, starting transfers between devices, per_device(): lax.all_to_all(squares_of(pieces), ('z', 'c'), split_axis=0, concat_axis=...  8.41 us
    dot_general x6, matrix products, product(): lax.dot_general(lhs, rhs, (((1,), (0,)), ((), ())), preferred_element_typ...  6.39 us
    all_to_all x1, waiting for transfers between devices, per_device(): lax.all_to_all(squares_of(pieces), ('z', 'c'), split_axis=0, concat_axis=...  5.12 us
  transfers between devices with their start and end apart: 22, of which 16 were waited for; matrix products, arithmetic and copies ran while one was open for 5% of the time, Pallas kernels for 0%

profile of v3, /device:TPU:1, one launch (start us, length us, event | category | flops | bytes accessed | tf_op | source)
XLA Modules:
  0.0 165.3 jit_solution(4769664489846532020)
XLA Ops:
  0.7 1.0 copy-done
  1.7 0.5 convolution_convert_fusion
  2.2 2.9 %copy-done.2 = bf16[1,512,8192]{2,1,0:T(8,128)(2,1)S(1)} copy-done((bf16[1,512,8192]{2,1,0:T(8,128)(2,1)S(1)}, bf16[1,512,8192]{2,1,0:T(8,128)(2,1)}, u32[]{:S(2)}) %copy-start.2) | copy-done | bytes 8388632
  5.1 0.8 fusion.8
  5.9 3.3 %collective-permute-start = (f32[32,4096]{1,0:T(8,128)S(1)}, f32[32,4096]{1,0:T(8,128)S(1)}, u32[]{:S(2)}, u32[]{:S(2)}) collective-permute-start(f32[32,4096]{1,0:T(8,128)S(1)} %fusion.8), channel_id=1, source_target_pairs={{0,1},{1,0},{2,3},{3,2},{4,5},{5,4},{6,7},{7,6},{8,9},{9,8},{10,11... | collective-permute-start | bytes 1572872 | tf_op jit(solution)/shard_map/ppermute | solution.py:118
  9.2 1.3 fusion.10
  10.7 1.1 fusion.6
  11.9 0.5 collective-permute-start.1
  12.3 0.8 fusion.2
  13.3 3.9 %collective-permute-start.3 = (f32[32,2048]{1,0:T(8,128)S(1)}, f32[32,2048]{1,0:T(8,128)S(1)}, u32[]{:S(2)}, u32[]{:S(2)}) collective-permute-start(f32[32,2048]{1,0:T(8,128)S(1)} %get-tuple-element.68), channel_id=1, source_target_pairs={{0,14},{2,0},{4,2},{6,4},{8,6},{10,8},{12,10},{14,12},{1,15},{3,1}... | collective-permute-start | bytes 786440 | tf_op jit(solution)/shard_map/ppermute | solution.py:142
  17.2 1.3 fusion.4
  18.5 0.6 collective-permute-done.4
  19.2 3.4 %collective-permute-done.3 = f32[32,2048]{1,0:T(8,128)S(1)} collective-permute-done((f32[32,2048]{1,0:T(8,128)S(1)}, f32[32,2048]{1,0:T(8,128)S(1)}, u32[]{:S(2)}, u32[]{:S(2)}) %collective-permute-start.3) | collective-permute-done | bytes 262176 | tf_op jit(solution)/shard_map/ppermute | solution.py:142
  22.6 3.1 %collective-permute-done.2 = f32[32,2048]{1,0:T(8,128)S(1)} collective-permute-done((f32[32,2048]{1,0:T(8,128)S(1)}, f32[32,2048]{1,0:T(8,128)S(1)}, u32[]{:S(2)}, u32[]{:S(2)}) %collective-permute-start.2) | collective-permute-done | bytes 262176 | tf_op jit(solution)/shard_map/ppermute | solution.py:142
  25.9 1.1 fusion
  27.0 1.6 collective-permute-start.7
  28.7 1.5 collective-permute-start.8
  30.2 2.6 %collective-permute-start.6 = (f32[32,4096]{1,0:T(8,128)S(1)}, f32[32,4096]{1,0:T(8,128)S(1)}, u32[]{:S(2)}, u32[]{:S(2)}) collective-permute-start(f32[32,4096]{1,0:T(8,128)S(1)} %pad_maximum_fusion.2), channel_id=1, source_target_pairs={{0,14},{2,0},{4,2},{6,4},{8,6},{10,8},{12,10},{14,12},{1,15},{3,1}... | collective-permute-start | bytes 1572872 | tf_op jit(solution)/shard_map/ppermute | solution.py:142
  32.8 3.7 %collective-permute-done.9 = f32[32,2048]{1,0:T(8,128)S(1)} collective-permute-done((f32[32,2048]{1,0:T(8,128)S(1)}, f32[32,2048]{1,0:T(8,128)S(1)}, u32[]{:S(2)}, u32[]{:S(2)}) %collective-permute-start.9) | collective-permute-done | bytes 262176 | tf_op jit(solution)/shard_map/ppermute | solution.py:142
  36.5 0.9 collective-permute-done.8
  38.0 2.5 %collective-permute-start.13 = (f32[32,4096]{1,0:T(8,128)S(1)}, f32[32,4096]{1,0:T(8,128)S(1)}, u32[]{:S(2)}, u32[]{:S(2)}) collective-permute-start(f32[32,4096]{1,0:T(8,128)S(1)} %pad_maximum_fusion.4), channel_id=1, source_target_pairs={{0,14},{2,0},{4,2},{6,4},{8,6},{10,8},{12,10},{14,12},{1,15},{3,1}... | collective-permute-start | bytes 1572872 | tf_op jit(solution)/shard_map/ppermute | solution.py:142
  40.5 8.1 %collective-permute-done.5 = f32[32,4096]{1,0:T(8,128)S(1)} collective-permute-done((f32[32,4096]{1,0:T(8,128)S(1)}, f32[32,4096]{1,0:T(8,128)S(1)}, u32[]{:S(2)}, u32[]{:S(2)}) %collective-permute-start.5) | collective-permute-done | bytes 524320 | tf_op jit(solution)/shard_map/ppermute | solution.py:142
  49.2 1.2 collective-permute-start.10
  50.4 9.5 %collective-permute-done.12 = f32[32,4096]{1,0:T(8,128)S(1)} collective-permute-done((f32[32,4096]{1,0:T(8,128)S(1)}, f32[32,4096]{1,0:T(8,128)S(1)}, u32[]{:S(2)}, u32[]{:S(2)}) %collective-permute-start.12) | collective-permute-done | bytes 524320 | tf_op jit(solution)/shard_map/ppermute | solution.py:142
  60.5 1.2 collective-permute-start.16
  61.8 8.5 %collective-permute-done.11 = f32[32,4096]{1,0:T(8,128)S(1)} collective-permute-done((f32[32,4096]{1,0:T(8,128)S(1)}, f32[32,4096]{1,0:T(8,128)S(1)}, u32[]{:S(2)}, u32[]{:S(2)}) %collective-permute-start.11) | collective-permute-done | bytes 524320 | tf_op jit(solution)/shard_map/ppermute | solution.py:142
  70.2 0.9 collective-permute-done.10
  71.7 1.1 collective-permute-start.14
  72.9 8.6 %collective-permute-done.17 = f32[32,4096]{1,0:T(8,128)S(1)} collective-permute-done((f32[32,4096]{1,0:T(8,128)S(1)}, f32[32,4096]{1,0:T(8,128)S(1)}, u32[]{:S(2)}, u32[]{:S(2)}) %collective-permute-start.17) | collective-permute-done | bytes 524320 | tf_op jit(solution)/shard_map/ppermute | solution.py:142
  81.5 0.9 collective-permute-done.16
  82.6 0.4 collective-permute-start.19
  83.0 1.1 collective-permute-start.18
  84.1 8.6 %collective-permute-done.15 = f32[32,4096]{1,0:T(8,128)S(1)} collective-permute-done((f32[32,4096]{1,0:T(8,128)S(1)}, f32[32,4096]{1,0:T(8,128)S(1)}, u32[]{:S(2)}, u32[]{:S(2)}) %collective-permute-start.15) | collective-permute-done | bytes 524320 | tf_op jit(solution)/shard_map/ppermute | solution.py:142
  92.7 0.9 collective-permute-done.14
  93.6 0.5 bitcast_subtract_fusion.1
  94.2 16.0 %all_to_all.20 = f32[16,32,256]{2,1,0:T(8,128)S(1)} all-to-all(f32[16,32,256]{2,1,0:T(8,128)S(1)} %bitcast.76), channel_id=1, replica_groups=mesh['y'=4,'x'=4,'z'=8,'c'=2] {'y','x'}, dimensions={0} | all-to-all | bytes 1048576 | tf_op jit(solution)/shard_map/all_to_all | solution.py:172
  110.2 1.3 bitcast_subtract_fusion
  111.4 0.8 copy.17
  112.3 4.2 %all-to-all-start.1 = ((f32[16,32,256]{2,1,0:T(8,128)}), f32[16,32,256]{2,1,0:T(8,128)}, u32[]{:S(2)}, u32[]{:S(2)}) async-start(f32[16,32,256]{2,1,0:T(8,128)} %bitcast.75), calls=%async_computation.1 | async-start | bytes 1048576 | tf_op jit(solution)/shard_map/all_to_all | solution.py:172
  116.6 8.9 %all-to-all-done.1 = f32[16,32,256]{2,1,0:T(8,128)} async-done(((f32[16,32,256]{2,1,0:T(8,128)}), f32[16,32,256]{2,1,0:T(8,128)}, u32[]{:S(2)}, u32[]{:S(2)}) %all-to-all-start.1) | async-done | bytes 524320 | tf_op jit(solution)/shard_map/all_to_all | solution.py:172
  125.5 1.1 reduce_sum.19
  126.8 16.4 %all_to_all.21.pieces_ref = f32[16,32,512]{2,1,0:T(8,128)} all-to-all(f32[16,32,512]{2,1,0:T(8,128)S(1)} %broadcast_in_dim.30), channel_id=1, replica_groups=mesh['y'=4,'x'=4,'z'=8,'c'=2] {'y','x'}, dimensions={0} | all-to-all | bytes 2097152 | tf_op jit(solution)/shard_map/all_to_all | solution.py:195
  143.1 2.2 %shard_map.102 = f32[16,8,128]{2,1,0:T(8,128)} custom-call(f32[16,32,512]{2,1,0:T(8,128)} %all_to_all.21.pieces_ref), custom_call_target="tpu_custom_call" | custom-call | flops 524288 | bytes 1048576 | tf_op jit(solution)/shard_map/pallas_call | solution.py:63
  145.3 8.4 %all-to-all-start.3 = ((f32[16,8,128]{2,1,0:T(8,128)}), f32[16,8,128]{2,1,0:T(8,128)S(1)}, u32[]{:S(2)}, u32[]{:S(2)}) async-start(f32[16,8,128]{2,1,0:T(8,128)} %shard_map.102), calls=%async_computation.3 | async-start | bytes 131072 | tf_op jit(solution)/shard_map/all_to_all | solution.py:196
  153.7 2.7 %fusion.18 = (f32[1,32,8192]{2,1,0:T(8,128)}, f32[1,32,8192]{2,1,0:T(8,128)}) fusion(f32[1,32,8192]{2,1,0:T(8,128)S(1)} %copy-done.3, f32[1,32,4096]{2,1,0:T(8,128)} %bitcast.72, f32[1,32,4096]{2,1,0:T(8,128)S(1)} %bitcast.71, f32[1,32,8192]{2,1,0:T(8,128)S(1)} %copy-done.4), kind=kLoop, calls=%fused_computation.28 | loop fusion | flops 2097152 | bytes 5242880 | tf_op jit(solution)/shard_map/add | solution.py:160
  156.4 5.1 %all-to-all-done.3.squares_ref = f32[16,8,128]{2,1,0:T(8,128)S(1)} async-done(((f32[16,8,128]{2,1,0:T(8,128)}), f32[16,8,128]{2,1,0:T(8,128)S(1)}, u32[]{:S(2)}, u32[]{:S(2)}) %all-to-all-start.3) | async-done | bytes 65568 | tf_op jit(solution)/shard_map/all_to_all | solution.py:196
  161.5 0.6 copy-done.7
  162.2 3.1 %shard_map.103 = (f32[32,8192]{1,0:T(8,128)}, f32[32,8192]{1,0:T(8,128)}) custom-call(f32[16,8,128]{2,1,0:T(8,128)} %copy-done.7, f32[16,32,512]{2,1,0:T(8,128)} %all_to_all.21.pieces_ref, f32[32,8192]{1,0:T(8,128)} %anchor_ref.1, f32[32,8192]{1,0:T(8,128)} %momentum_ref.1), custom_call_target="tpu_custom_call" | custom-call | flops 1835008 | bytes 5242880 | tf_op jit(solution)/shard_map/pallas_call | solution.py:87
  (53 shorter events, 3.8 us)
Async XLA Ops:
  0.6 1.1 copy-start
  1.7 3.4 %copy-start.2 = (bf16[1,512,8192]{2,1,0:T(8,128)(2,1)S(1)}, bf16[1,512,8192]{2,1,0:T(8,128)(2,1)}, u32[]{:S(2)}) copy-start(bf16[1,512,8192]{2,1,0:T(8,128)(2,1)} %param.8) | copy-start | bytes 25165828
  5.9 4.8 %collective-permute-start = (f32[32,4096]{1,0:T(8,128)S(1)}, f32[32,4096]{1,0:T(8,128)S(1)}, u32[]{:S(2)}, u32[]{:S(2)}) collective-permute-start(f32[32,4096]{1,0:T(8,128)S(1)} %fusion.8), channel_id=1, source_target_pairs={{0,1},{1,0},{2,3},{3,2},{4,5},{5,4},{6,7},{7,6},{8,9},{9,8},{10,11... | collective-permute-start | bytes 1572872 | tf_op jit(solution)/shard_map/ppermute | solution.py:118
  11.9 13.8 %collective-permute-start.1 = (f32[224,4096]{1,0:T(8,128)S(1)}, f32[224,4096]{1,0:T(8,128)S(1)}, u32[]{:S(2)}, u32[]{:S(2)}) collective-permute-start(f32[224,4096]{1,0:T(8,128)S(1)} %fusion.6), channel_id=1, source_target_pairs={{0,1},{1,0},{2,3},{3,2},{4,5},{5,4},{6,7},{7,6},{8,9},{9,8},{10,11... | collective-permute-start | bytes 11010056 | tf_op jit(solution)/shard_map/ppermute | solution.py:138
  13.1 6.0 %collective-permute-start.4 = (f32[32,4096]{1,0:T(8,128)S(1)}, f32[32,4096]{1,0:T(8,128)S(1)}, u32[]{:S(2)}, u32[]{:S(2)}) collective-permute-start(f32[32,4096]{1,0:T(8,128)S(1)} %fusion.2), channel_id=1, source_target_pairs={{0,1},{1,0},{2,3},{3,2},{4,5},{5,4},{6,7},{7,6},{8,9},{9,8},{10,11... | collective-permute-start | bytes 1572872 | tf_op jit(solution)/shard_map/ppermute | solution.py:118
  13.3 9.2 %collective-permute-start.3 = (f32[32,2048]{1,0:T(8,128)S(1)}, f32[32,2048]{1,0:T(8,128)S(1)}, u32[]{:S(2)}, u32[]{:S(2)}) collective-permute-start(f32[32,2048]{1,0:T(8,128)S(1)} %get-tuple-element.68), channel_id=1, source_target_pairs={{0,14},{2,0},{4,2},{6,4},{8,6},{10,8},{12,10},{14,12},{1,15},{3,1}... | collective-permute-start | bytes 786440 | tf_op jit(solution)/shard_map/ppermute | solution.py:142
  17.2 8.4 %collective-permute-start.2 = (f32[32,2048]{1,0:T(8,128)S(1)}, f32[32,2048]{1,0:T(8,128)S(1)}, u32[]{:S(2)}, u32[]{:S(2)}) collective-permute-start(f32[32,2048]{1,0:T(8,128)S(1)} %get-tuple-element.69), channel_id=1, source_target_pairs={{0,2},{2,4},{4,6},{6,8},{8,10},{10,12},{12,14},{14,0},{1,3},{3,5},... | collective-permute-start | bytes 786440 | tf_op jit(solution)/shard_map/ppermute | solution.py:142
  27.0 10.4 %collective-permute-start.7 = (f32[224,4096]{1,0:T(8,128)S(1)}, f32[224,4096]{1,0:T(8,128)S(1)}, u32[]{:S(2)}, u32[]{:S(2)}) collective-permute-start(f32[224,4096]{1,0:T(8,128)S(1)} %fusion), channel_id=1, source_target_pairs={{0,1},{1,0},{2,3},{3,2},{4,5},{5,4},{6,7},{7,6},{8,9},{9,8},{10,11... | collective-permute-start | bytes 11010056 | tf_op jit(solution)/shard_map/ppermute | solution.py:138
  28.6 7.9 %collective-permute-start.9 = (f32[32,2048]{1,0:T(8,128)S(1)}, f32[32,2048]{1,0:T(8,128)S(1)}, u32[]{:S(2)}, u32[]{:S(2)}) collective-permute-start(f32[32,2048]{1,0:T(8,128)S(1)} %get-tuple-element.66), channel_id=1, source_target_pairs={{0,14},{2,0},{4,2},{6,4},{8,6},{10,8},{12,10},{14,12},{1,15},{3,1}... | collective-permute-start | bytes 786440 | tf_op jit(solution)/shard_map/ppermute | solution.py:142
  28.7 8.7 %collective-permute-start.8 = (f32[32,2048]{1,0:T(8,128)S(1)}, f32[32,2048]{1,0:T(8,128)S(1)}, u32[]{:S(2)}, u32[]{:S(2)}) collective-permute-start(f32[32,2048]{1,0:T(8,128)S(1)} %get-tuple-element.67), channel_id=1, source_target_pairs={{0,2},{2,4},{4,6},{6,8},{8,10},{10,12},{12,14},{14,0},{1,3},{3,5},... | collective-permute-start | bytes 786440 | tf_op jit(solution)/shard_map/ppermute | solution.py:142
  30.1 18.5 %collective-permute-start.5 = (f32[32,4096]{1,0:T(8,128)S(1)}, f32[32,4096]{1,0:T(8,128)S(1)}, u32[]{:S(2)}, u32[]{:S(2)}) collective-permute-start(f32[32,4096]{1,0:T(8,128)S(1)} %pad_maximum_fusion.1), channel_id=1, source_target_pairs={{0,2},{2,4},{4,6},{6,8},{8,10},{10,12},{12,14},{14,0},{1,3},{3,5},... | collective-permute-start | bytes 1572872 | tf_op jit(solution)/shard_map/ppermute | solution.py:142
  30.2 18.5 %collective-permute-start.6 = (f32[32,4096]{1,0:T(8,128)S(1)}, f32[32,4096]{1,0:T(8,128)S(1)}, u32[]{:S(2)}, u32[]{:S(2)}) collective-permute-start(f32[32,4096]{1,0:T(8,128)S(1)} %pad_maximum_fusion.2), channel_id=1, source_target_pairs={{0,14},{2,0},{4,2},{6,4},{8,6},{10,8},{12,10},{14,12},{1,15},{3,1}... | collective-permute-start | bytes 1572872 | tf_op jit(solution)/shard_map/ppermute | solution.py:142
  37.6 22.2 %collective-permute-start.12 = (f32[32,4096]{1,0:T(8,128)S(1)}, f32[32,4096]{1,0:T(8,128)S(1)}, u32[]{:S(2)}, u32[]{:S(2)}) collective-permute-start(f32[32,4096]{1,0:T(8,128)S(1)} %pad_maximum_fusion.3), channel_id=1, source_target_pairs={{0,2},{2,4},{4,6},{6,8},{8,10},{10,12},{12,14},{14,0},{1,3},{3,5},... | collective-permute-start | bytes 1572872 | tf_op jit(solution)/shard_map/ppermute | solution.py:142
  38.0 21.9 %collective-permute-start.13 = (f32[32,4096]{1,0:T(8,128)S(1)}, f32[32,4096]{1,0:T(8,128)S(1)}, u32[]{:S(2)}, u32[]{:S(2)}) collective-permute-start(f32[32,4096]{1,0:T(8,128)S(1)} %pad_maximum_fusion.4), channel_id=1, source_target_pairs={{0,14},{2,0},{4,2},{6,4},{8,6},{10,8},{12,10},{14,12},{1,15},{3,1}... | collective-permute-start | bytes 1572872 | tf_op jit(solution)/shard_map/ppermute | solution.py:142
  48.9 21.4 %collective-permute-start.11 = (f32[32,4096]{1,0:T(8,128)S(1)}, f32[32,4096]{1,0:T(8,128)S(1)}, u32[]{:S(2)}, u32[]{:S(2)}) collective-permute-start(f32[32,4096]{1,0:T(8,128)S(1)} %get-tuple-element.56), channel_id=1, source_target_pairs={{0,14},{2,0},{4,2},{6,4},{8,6},{10,8},{12,10},{14,12},{1,15},{3,1}... | collective-permute-start | bytes 1572872 | tf_op jit(solution)/shard_map/ppermute | solution.py:142
  49.2 21.9 %collective-permute-start.10 = (f32[32,4096]{1,0:T(8,128)S(1)}, f32[32,4096]{1,0:T(8,128)S(1)}, u32[]{:S(2)}, u32[]{:S(2)}) collective-permute-start(f32[32,4096]{1,0:T(8,128)S(1)} %get-tuple-element.57), channel_id=1, source_target_pairs={{0,2},{2,4},{4,6},{6,8},{8,10},{10,12},{12,14},{14,0},{1,3},{3,5},... | collective-permute-start | bytes 1572872 | tf_op jit(solution)/shard_map/ppermute | solution.py:142
  60.1 21.3 %collective-permute-start.17 = (f32[32,4096]{1,0:T(8,128)S(1)}, f32[32,4096]{1,0:T(8,128)S(1)}, u32[]{:S(2)}, u32[]{:S(2)}) collective-permute-start(f32[32,4096]{1,0:T(8,128)S(1)} %get-tuple-element.54), channel_id=1, source_target_pairs={{0,14},{2,0},{4,2},{6,4},{8,6},{10,8},{12,10},{14,12},{1,15},{3,1}... | collective-permute-start | bytes 1572872 | tf_op jit(solution)/shard_map/ppermute | solution.py:142
  60.5 33.1 %copy-start.3 = (f32[1,32,8192]{2,1,0:T(8,128)S(1)}, f32[1,32,8192]{2,1,0:T(8,128)}, u32[]{:S(2)}) copy-start(f32[1,32,8192]{2,1,0:T(8,128)} %param.12) | copy-start | bytes 3145732
  60.5 33.1 %copy-start.4 = (f32[1,32,8192]{2,1,0:T(8,128)S(1)}, f32[1,32,8192]{2,1,0:T(8,128)}, u32[]{:S(2)}) copy-start(f32[1,32,8192]{2,1,0:T(8,128)} %param.11) | copy-start | bytes 3145732
  60.5 33.1 %copy-start.5 = (f32[32,8192]{1,0:T(8,128)S(1)}, f32[32,8192]{1,0:T(8,128)}, u32[]{:S(2)}) copy-start(f32[32,8192]{1,0:T(8,128)} %anchor_ref.1) | copy-start | bytes 3145732
  60.5 33.1 %copy-start.6 = (f32[1,32,8192]{2,1,0:T(8,128)S(1)}, f32[1,32,8192]{2,1,0:T(8,128)}, u32[]{:S(2)}) copy-start(f32[1,32,8192]{2,1,0:T(8,128)} %param.10) | copy-start | bytes 3145732
  60.5 21.8 %collective-permute-start.16 = (f32[32,4096]{1,0:T(8,128)S(1)}, f32[32,4096]{1,0:T(8,128)S(1)}, u32[]{:S(2)}, u32[]{:S(2)}) collective-permute-start(f32[32,4096]{1,0:T(8,128)S(1)} %get-tuple-element.55), channel_id=1, source_target_pairs={{0,2},{2,4},{4,6},{6,8},{8,10},{10,12},{12,14},{14,0},{1,3},{3,5},... | collective-permute-start | bytes 1572872 | tf_op jit(solution)/shard_map/ppermute | solution.py:142
  71.3 21.4 %collective-permute-start.15 = (f32[32,4096]{1,0:T(8,128)S(1)}, f32[32,4096]{1,0:T(8,128)S(1)}, u32[]{:S(2)}, u32[]{:S(2)}) collective-permute-start(f32[32,4096]{1,0:T(8,128)S(1)} %get-tuple-element.52), channel_id=1, source_target_pairs={{0,14},{2,0},{4,2},{6,4},{8,6},{10,8},{12,10},{14,12},{1,15},{3,1}... | collective-permute-start | bytes 1572872 | tf_op jit(solution)/shard_map/ppermute | solution.py:142
  71.7 21.9 %collective-permute-start.14 = (f32[32,4096]{1,0:T(8,128)S(1)}, f32[32,4096]{1,0:T(8,128)S(1)}, u32[]{:S(2)}, u32[]{:S(2)}) collective-permute-start(f32[32,4096]{1,0:T(8,128)S(1)} %get-tuple-element.53), channel_id=1, source_target_pairs={{0,2},{2,4},{4,6},{6,8},{8,10},{10,12},{12,14},{14,0},{1,3},{3,5},... | collective-permute-start | bytes 1572872 | tf_op jit(solution)/shard_map/ppermute | solution.py:142
  82.6 27.6 %collective-permute-start.19 = (f32[32,4096]{1,0:T(8,128)S(1)}, f32[32,4096]{1,0:T(8,128)S(1)}, u32[]{:S(2)}, u32[]{:S(2)}) collective-permute-start(f32[32,4096]{1,0:T(8,128)S(1)} %get-tuple-element.50), channel_id=1, source_target_pairs={{0,14},{2,0},{4,2},{6,4},{8,6},{10,8},{12,10},{14,12},{1,15},{3,1}... | collective-permute-start | bytes 1572872 | tf_op jit(solution)/shard_map/ppermute | solution.py:142
  83.0 27.2 %collective-permute-start.18 = (f32[32,4096]{1,0:T(8,128)S(1)}, f32[32,4096]{1,0:T(8,128)S(1)}, u32[]{:S(2)}, u32[]{:S(2)}) collective-permute-start(f32[32,4096]{1,0:T(8,128)S(1)} %get-tuple-element.51), channel_id=1, source_target_pairs={{0,2},{2,4},{4,6},{6,8},{8,10},{10,12},{12,14},{14,0},{1,3},{3,5},... | collective-permute-start | bytes 1572872 | tf_op jit(solution)/shard_map/ppermute | solution.py:142
  112.3 13.2 %all-to-all-start.1 = ((f32[16,32,256]{2,1,0:T(8,128)}), f32[16,32,256]{2,1,0:T(8,128)}, u32[]{:S(2)}, u32[]{:S(2)}) async-start(f32[16,32,256]{2,1,0:T(8,128)} %bitcast.75), calls=%async_computation.1 | async-start | bytes 1048576 | tf_op jit(solution)/shard_map/all_to_all | solution.py:172
  145.3 16.2 %all-to-all-start.3 = ((f32[16,8,128]{2,1,0:T(8,128)}), f32[16,8,128]{2,1,0:T(8,128)S(1)}, u32[]{:S(2)}, u32[]{:S(2)}) async-start(f32[16,8,128]{2,1,0:T(8,128)} %shard_map.102), calls=%async_computation.3 | async-start | bytes 131072 | tf_op jit(solution)/shard_map/all_to_all | solution.py:196
  153.7 11.6 %copy-start.1 = (bf16[1,512,512]{2,1,0:T(8,128)(2,1)S(1)}, bf16[1,512,512]{2,1,0:T(8,128)(2,1)}, u32[]{:S(2)}) copy-start(bf16[1,512,512]{2,1,0:T(8,128)(2,1)} %param.7) | copy-start | bytes 1572868
  161.5 0.6 copy-start.7

commit v4 on v2

--- a/solution.py
+++ b/solution.py
@@ -3,6 +3,8 @@
 import jax
 import jax.numpy as jnp
 from jax import lax
+from jax.experimental import pallas as pl
+from jax.experimental.pallas import tpu as pltpu
 from jax.sharding import Mesh, PartitionSpec as P
 
 D = 8192
@@ -31,12 +33,13 @@
     rows = Z * C * ROWS_DEV
     place = lax.broadcasted_iota(jnp.int32, (rows, rows), 1)
     source = lax.broadcasted_iota(jnp.int32, (rows, rows), 0)
-    mine = place // (Z * ROWS_DEV)
-    core = jnp.where(mine == 1, c, 1 - c)
-    slot = (place // ROWS_DEV) % Z
+    block = place // ROWS_DEV
+    mine = jnp.where(block < 2, block == 1, block >= 2 + (Z - 1))
+    slot = jnp.where(block < 2, 0, jnp.where(block < Z + 1, block - 1, block - Z))
     step = jnp.zeros_like(slot)
     for at, distance in enumerate(STEPS):
         step = jnp.where(slot == at, distance, step)
+    core = jnp.where(mine, c, 1 - c)
     wanted = (((z + step) % Z) * C + core) * ROWS_DEV + place % ROWS_DEV
     pick = (wanted == source).astype(activations.dtype)
     return lax.dot_general(
@@ -44,13 +47,75 @@
     ).astype(activations.dtype)
 
 
+def head_kernel(rows_ref, cols_ref, theirs_ref, mine_ref):
+    out = jnp.dot(rows_ref[...], cols_ref[...], preferred_element_type=jnp.float32)
+    theirs_ref[...] = out[:ROWS_DEV]
+    mine_ref[...] = out[ROWS_DEV:]
+
+
+def head_rows(ordered, cotangent, k):
+    tokens = cotangent.shape[0]
+    block = 1024
+    count = WIDTH // block
+    out = pl.BlockSpec((ROWS_DEV, block), lambda n: (0, n))
+    shape = jax.ShapeDtypeStruct((ROWS_DEV, WIDTH), jnp.float32)
+    return pl.pallas_call(
+        head_kernel,
+        grid=(count,),
+        in_specs=[
+            pl.BlockSpec((2 * ROWS_DEV, tokens), lambda n: (0, 0)),
+            pl.BlockSpec((tokens, block), lambda n: (0, k * count + n)),
+        ],
+        out_specs=[out, out],
+        out_shape=[shape, shape],
+        cost_estimate=pl.CostEstimate(
+            flops=4 * ROWS_DEV * tokens * WIDTH,
+            bytes_accessed=2 * tokens * WIDTH + 8 * ROWS_DEV * WIDTH,
+            transcendentals=0,
+        ),
+    )(ordered, cotangent)
+
+
+def finish_kernel(squares_ref, pieces_ref, anchor_ref, momentum_ref, momentum_out, anchor_out):
+    squares = jnp.sum(squares_ref[:, 0, 0:1], axis=0, keepdims=True)
+    ceiling = 0.3 * math.sqrt(ROWS_DEV * PARTS * D)
+    factor = ceiling / jnp.maximum(jnp.sqrt(squares), ceiling)
+    piece = pieces_ref.shape[2]
+    for p in range(pieces_ref.shape[0]):
+        at = slice(p * piece, (p + 1) * piece)
+        scaled = factor * pieces_ref[p]
+        momentum = momentum_coef * momentum_ref[:, at] + scaled
+        momentum_out[:, at] = momentum
+        anchor_out[:, at] = anchor_ref[:, at] - outer_rate * (scaled + momentum_coef * momentum)
+
+
+def finish(squares, pieces, anchor, outer_momentum):
+    replicas, _, piece = pieces.shape
+    parts = 2
+    part = pl.BlockSpec((ROWS_DEV, D // parts), lambda h: (0, h))
+    shape = jax.ShapeDtypeStruct(anchor.shape, jnp.float32)
+    return pl.pallas_call(
+        finish_kernel,
+        grid=(parts,),
+        in_specs=[
+            pl.BlockSpec(squares.shape, lambda h: (0, 0, 0)),
+            pl.BlockSpec((replicas // parts, ROWS_DEV, piece), lambda h: (h, 0, 0)),
+            part,
+            part,
+        ],
+        out_specs=[part, part],
+        out_shape=[shape, shape],
+        cost_estimate=pl.CostEstimate(flops=7 * anchor.size, bytes_accessed=20 * anchor.size, transcendentals=0),
+    )(squares, pieces, anchor, outer_momentum)
+
+
 def per_device(hidden_acts, out_grads, anchor, drift, adam_first, adam_second, outer_momentum):
     z = lax.axis_index("z")
     c = lax.axis_index("c")
     ordered = reorder_rows(hidden_acts[0], z, c)
     cotangent = out_grads[0]
-    half_rows = Z * ROWS_DEV
-    theirs, mine = ordered[:half_rows], ordered[half_rows:]
+    near = 2 * ROWS_DEV
+    stay = near + (Z - 1) * ROWS_DEV
 
     def product(lhs, rhs):
         return lax.dot_general(lhs, rhs, (((1,), (0,)), ((), ())), preferred_element_type=jnp.float32)
@@ -60,31 +125,27 @@
 
     chunks = range(CHUNKS)
     cols = [lax.slice_in_dim(cotangent, k * WIDTH, (k + 1) * WIDTH, axis=1) for k in chunks]
-    first = [lax.ppermute(product(theirs[:ROWS_DEV], cols[k]), "c", SWAP) for k in chunks]
-    kept = [None] * CHUNKS
-    rest = [None] * CHUNKS
     up = [None] * CHUNKS
     down = [None] * CHUNKS
 
     def own(k, distance, lo=0, hi=WIDTH):
-        at = STEPS.index(distance) * ROWS_DEV
-        local = kept[k][at : at + ROWS_DEV, lo:hi]
-        if at == 0:
-            return local + first[k][:, lo:hi]
-        return local + rest[k][at - ROWS_DEV : at, lo:hi]
-
-    lhs = mine
+        at = (STEPS.index(distance) - 1) * ROWS_DEV
+        base = k * WIDTH
+        return kept[k][at : at + ROWS_DEV, lo:hi] + rest[at : at + ROWS_DEV, base + lo : base + hi]
+
+    first_rows = ordered[:near]
+    last = ()
     for k in chunks:
-        kept[k] = product(lhs, cols[k])
-        up[k] = own(k, 4, HALF, WIDTH)
-        down[k] = own(k, 4, 0, HALF)
-        lhs = after(mine, up[k], down[k])
-    lhs = after(theirs[ROWS_DEV:], up[-1], down[-1])
-    for k in chunks:
-        sent = product(lhs, cols[k])
-        rest[k] = lax.ppermute(sent, "c", SWAP)
-        lhs = after(theirs[ROWS_DEV:], sent)
+        sent, stays = head_rows(first_rows, cotangent, k)
+        first = stays + after(lax.ppermute(sent, "c", SWAP), last)
+        up[k], down[k] = first[:, HALF:], first[:, :HALF]
+        first_rows = after(first_rows, sent)
+        last = (up[k], down[k])
     last = (up[-1], down[-1])
+    sent = product(after(ordered[near:stay], last), cotangent)
+    rest = lax.ppermute(sent, "c", SWAP)
+    lhs = after(ordered[stay:], sent)
+    kept = [product(lhs, cols[k]) for k in chunks]
     for t in range(1, 5):
         for k in chunks:
             moved = (lax.ppermute(up[k], "z", UP), lax.ppermute(down[k], "z", DOWN))
@@ -117,14 +178,9 @@
     part = jnp.sum(met, axis=0) / replicas
     copies = jnp.broadcast_to(part[None], (replicas, ROWS_DEV, piece))
     pieces = lax.all_to_all(copies, ("y", "x"), split_axis=0, concat_axis=0, tiled=True)
-    average = pieces.transpose(1, 0, 2).reshape(ROWS_DEV, D)
     squares = jnp.broadcast_to(jnp.sum(pieces * pieces), (PARTS, 1, 128))
     squares = lax.all_to_all(squares, ("z", "c"), split_axis=0, concat_axis=0, tiled=True)
-    squares = jnp.sum(squares[:, 0, 0])
-    ceiling = 0.3 * math.sqrt(ROWS_DEV * PARTS * D)
-    factor = ceiling / jnp.maximum(jnp.sqrt(squares), ceiling)
-    momentum = momentum_coef * outer_momentum + factor * average
-    updated = anchor - outer_rate * (factor * average + momentum_coef * momentum)
+    momentum, updated = finish(squares, pieces, anchor, outer_momentum)
     return (moment_one[None], moment_two[None], momentum, updated)
 
 

time: 161 us -> 172 us (1.068)
  Pallas kernels: 0 us -> 12.1 us
  blocking collectives: 36.7 us -> 40.8 us
  waiting for transfers between devices: 68.5 us -> 64.9 us
  other arithmetic: 9.82 us -> 7.6 us
    pallas_call x0 -> x3, Pallas kernels: none -> 12.1 us  [the longest x2 9.01 us: head_rows(): pl.pallas_call(head_kernel, grid=(count,), in_specs=[pl.BlockSpec((2 * RO...]
    ppermute x16, waiting for transfers between devices: 64.4 us -> 57.9 us  [per_device(): moved = (lax.ppermute(up[k], 'z', UP), lax.ppermute(down[k], 'z', DOWN))]
    ppermute x16, starting transfers between devices: 18.6 us -> 23.3 us  [per_device(): moved = (lax.ppermute(up[k], 'z', UP), lax.ppermute(down[k], 'z', DOWN))]
    ppermute x4 -> x3, waiting for transfers between devices: 0.01 us -> 3.19 us  [the longest x2 1.88 us: per_device(): first = stays + after(lax.ppermute(sent, 'c', SWAP), last)]
    sub x2 -> x0, other arithmetic: 2.8 us -> none  [the longest x1 2.8 us: per_device(): anchor - outer_rate * (factor * average + momentum_coef * momentum)]
    all_to_all x1, starting transfers between devices: 8.85 us -> 6.21 us  [per_device(): lax.all_to_all(squares, ('z', 'c'), split_axis=0, concat_axis=0, tiled=True)]
    unnamed x16 -> x22, local copies, waits for them, and re-layouts: 3.86 us -> 1.65 us
    all_to_all x1, blocking collectives: 16.2 us -> 18.4 us  [per_device(): lax.all_to_all(copies, ('y', 'x'), split_axis=0, concat_axis=0, tiled=True)]
  transfers between devices with their start and end apart: 21 -> 20, of which waited for: 14 -> 14; matrix products, arithmetic and copies ran while one was open for 5% -> 4% of each run, Pallas kernels for 0% -> 3%
where the time goes in v4:
time: 172 us
  waiting for transfers between devices  64.9 us (38%)
  blocking collectives  40.8 us (24%)
  starting transfers between devices  33 us (19%)
  Pallas kernels  12.1 us (7%)
  matrix products  8.36 us (5%)
  other arithmetic  7.6 us (4%)
  local copies, waits for them, and re-layouts  3.83 us (2%)
    ppermute x16, waiting for transfers between devices, per_device(): moved = (lax.ppermute(up[k], 'z', UP), lax.ppermute(down[k], 'z', DOWN))  57.9 us
    ppermute x16, starting transfers between devices, per_device(): moved = (lax.ppermute(up[k], 'z', UP), lax.ppermute(down[k], 'z', DOWN))  23.3 us
    all_to_all x1, blocking collectives, per_device(): lax.all_to_all(spread, ('y', 'x'), split_axis=0, concat_axis=0, tiled=True)  22.4 us
    all_to_all x1, blocking collectives, per_device(): lax.all_to_all(copies, ('y', 'x'), split_axis=0, concat_axis=0, tiled=True)  18.4 us
    pallas_call x2, Pallas kernels, head_rows(): pl.pallas_call(head_kernel, grid=(count,), in_specs=[pl.BlockSpec((2 * RO...  9.01 us
    dot_general x3, matrix products, product(): lax.dot_general(lhs, rhs, (((1,), (0,)), ((), ())), preferred_element_typ...  7.85 us
    all_to_all x1, starting transfers between devices, per_device(): lax.all_to_all(squares, ('z', 'c'), split_axis=0, concat_axis=0, tiled=True)  6.21 us
    all_to_all x1, waiting for transfers between devices, per_device(): lax.all_to_all(squares, ('z', 'c'), split_axis=0, concat_axis=0, tiled=True)  3.83 us
  transfers between devices with their start and end apart: 20, of which 14 were waited for; matrix products, arithmetic and copies ran while one was open for 4% of the time, Pallas kernels for 3%

profile of v4, /device:TPU:1, one launch (start us, length us, event | category | flops | bytes accessed | tf_op | source)
XLA Modules:
  0.0 171.5 jit_solution(12644620314327896449)
XLA Ops:
  0.7 1.0 copy-done
  1.7 0.5 convolution_convert_fusion
  2.2 0.6 slice.182.rows_ref
  2.8 4.5 %shard_map.102 = (f32[32,4096]{1,0:T(8,128)}, f32[32,4096]{1,0:T(8,128)}) custom-call(bf16[64,512]{1,0:T(8,128)(2,1)} %slice.182.rows_ref, bf16[512,8192]{1,0:T(8,128)(2,1)} %bitcast.39), custom_call_target="tpu_custom_call" | custom-call | flops 268435456 | bytes 5242880 | tf_op jit(solution)/shard_map/pallas_call | solution.py:62
  7.3 3.2 %collective-permute-start.1 = (f32[32,4096]{1,0:T(8,128)}, f32[32,4096]{1,0:T(8,128)S(1)}, u32[]{:S(2)}, u32[]{:S(2)}) collective-permute-start(f32[32,4096]{1,0:T(8,128)} %get-tuple-element.30), channel_id=1, source_target_pairs={{0,1},{1,0},{2,3},{3,2},{4,5},{5,4},{6,7},{7,6},{8,9},{9,8},{10,11... | collective-permute-start | bytes 1572872 | tf_op jit(solution)/shard_map/ppermute | solution.py:140
  10.6 4.5 %shard_map.103 = (f32[32,4096]{1,0:T(8,128)}, f32[32,4096]{1,0:T(8,128)}) custom-call(bf16[64,512]{1,0:T(8,128)(2,1)} %slice.182.rows_ref, bf16[512,8192]{1,0:T(8,128)(2,1)} %bitcast.40), custom_call_target="tpu_custom_call" | custom-call | flops 268435456 | bytes 5242880 | tf_op jit(solution)/shard_map/pallas_call | solution.py:62
  15.3 1.9 %collective-permute-done = f32[32,4096]{1,0:T(8,128)S(1)} collective-permute-done((f32[32,4096]{1,0:T(8,128)}, f32[32,4096]{1,0:T(8,128)S(1)}, u32[]{:S(2)}, u32[]{:S(2)}) %collective-permute-start) | collective-permute-done | bytes 524320 | tf_op jit(solution)/shard_map/ppermute | solution.py:140
  17.2 1.1 add.166
  18.4 5.6 %fusion.69 = f32[224,8192]{1,0:T(8,128)S(1)} fusion(bf16[224,512]{1,0:T(8,128)(2,1)S(1)} %get-tuple-element.36, bf16[1,512,8192]{2,1,0:T(8,128)(2,1)} %param.8), kind=kOutput, calls=%fused_computation.115 | convolution fusion | flops 1879048192 | bytes 15958016 | tf_op jit(solution)/shard_map/dot_general | solution.py:121
  24.0 0.2 collective-permute-start.2
  24.2 3.9 %collective-permute-start.4 = (f32[32,2048]{1,0:T(8,128)S(1)}, f32[32,2048]{1,0:T(8,128)S(1)}, u32[]{:S(2)}, u32[]{:S(2)}) collective-permute-start(f32[32,2048]{1,0:T(8,128)S(1)} %get-tuple-element.78), channel_id=1, source_target_pairs={{0,14},{2,0},{4,2},{6,4},{8,6},{10,8},{12,10},{14,12},{1,15},{3,1}... | collective-permute-start | bytes 786440 | tf_op jit(solution)/shard_map/ppermute | solution.py:151
  28.1 2.7 %collective-permute-start.8 = (f32[32,2048]{1,0:T(8,128)S(1)}, f32[32,2048]{1,0:T(8,128)S(1)}, u32[]{:S(2)}, u32[]{:S(2)}) collective-permute-start(f32[32,2048]{1,0:T(8,128)S(1)} %get-tuple-element.76), channel_id=1, source_target_pairs={{0,14},{2,0},{4,2},{6,4},{8,6},{10,8},{12,10},{14,12},{1,15},{3,1}... | collective-permute-start | bytes 786440 | tf_op jit(solution)/shard_map/ppermute | solution.py:151
  30.8 1.1 fusion.2
  31.9 1.1 fusion
  33.1 1.4 collective-permute-done.3
  34.5 1.3 collective-permute-done.2
  35.9 3.9 %collective-permute-start.6 = (f32[32,4096]{1,0:T(8,128)S(1)}, f32[32,4096]{1,0:T(8,128)S(1)}, u32[]{:S(2)}, u32[]{:S(2)}) collective-permute-start(f32[32,4096]{1,0:T(8,128)S(1)} %pad_maximum_fusion.3), channel_id=1, source_target_pairs={{0,14},{2,0},{4,2},{6,4},{8,6},{10,8},{12,10},{14,12},{1,15},{3,1}... | collective-permute-start | bytes 1572872 | tf_op jit(solution)/shard_map/ppermute | solution.py:151
  40.3 2.9 %collective-permute-start.12 = (f32[32,4096]{1,0:T(8,128)S(1)}, f32[32,4096]{1,0:T(8,128)S(1)}, u32[]{:S(2)}, u32[]{:S(2)}) collective-permute-start(f32[32,4096]{1,0:T(8,128)S(1)} %pad_maximum_fusion.5), channel_id=1, source_target_pairs={{0,14},{2,0},{4,2},{6,4},{8,6},{10,8},{12,10},{14,12},{1,15},{3,1}... | collective-permute-start | bytes 1572872 | tf_op jit(solution)/shard_map/ppermute | solution.py:151
  43.2 7.8 %collective-permute-done.6 = f32[32,4096]{1,0:T(8,128)S(1)} collective-permute-done((f32[32,4096]{1,0:T(8,128)S(1)}, f32[32,4096]{1,0:T(8,128)S(1)}, u32[]{:S(2)}, u32[]{:S(2)}) %collective-permute-start.6) | collective-permute-done | bytes 524320 | tf_op jit(solution)/shard_map/ppermute | solution.py:151
  51.0 3.2 %collective-permute-done.5 = f32[32,4096]{1,0:T(8,128)S(1)} collective-permute-done((f32[32,4096]{1,0:T(8,128)S(1)}, f32[32,4096]{1,0:T(8,128)S(1)}, u32[]{:S(2)}, u32[]{:S(2)}) %collective-permute-start.5) | collective-permute-done | bytes 524320 | tf_op jit(solution)/shard_map/ppermute | solution.py:151
  54.3 0.2 fusion.31
  54.5 0.3 collective-permute-start.10
  54.8 1.3 collective-permute-start.9
  56.0 6.3 %collective-permute-done.12 = f32[32,4096]{1,0:T(8,128)S(1)} collective-permute-done((f32[32,4096]{1,0:T(8,128)S(1)}, f32[32,4096]{1,0:T(8,128)S(1)}, u32[]{:S(2)}, u32[]{:S(2)}) %collective-permute-start.12) | collective-permute-done | bytes 524320 | tf_op jit(solution)/shard_map/ppermute | solution.py:151
  62.3 3.2 %collective-permute-done.11 = f32[32,4096]{1,0:T(8,128)S(1)} collective-permute-done((f32[32,4096]{1,0:T(8,128)S(1)}, f32[32,4096]{1,0:T(8,128)S(1)}, u32[]{:S(2)}, u32[]{:S(2)}) %collective-permute-start.11) | collective-permute-done | bytes 524320 | tf_op jit(solution)/shard_map/ppermute | solution.py:151
  65.5 0.2 fusion.29
  65.8 2.7 %collective-permute-start.16 = (f32[32,4096]{1,0:T(8,128)S(1)}, f32[32,4096]{1,0:T(8,128)S(1)}, u32[]{:S(2)}, u32[]{:S(2)}) collective-permute-start(f32[32,4096]{1,0:T(8,128)S(1)} %get-tuple-element.60), channel_id=1, source_target_pairs={{0,14},{2,0},{4,2},{6,4},{8,6},{10,8},{12,10},{14,12},{1,15},{3,1}... | collective-permute-start | bytes 1572872 | tf_op jit(solution)/shard_map/ppermute | solution.py:151
  68.5 5.0 %collective-permute-done.10 = f32[32,4096]{1,0:T(8,128)S(1)} collective-permute-done((f32[32,4096]{1,0:T(8,128)S(1)}, f32[32,4096]{1,0:T(8,128)S(1)}, u32[]{:S(2)}, u32[]{:S(2)}) %collective-permute-start.10) | collective-permute-done | bytes 524320 | tf_op jit(solution)/shard_map/ppermute | solution.py:151
  73.5 3.2 %collective-permute-done.9 = f32[32,4096]{1,0:T(8,128)S(1)} collective-permute-done((f32[32,4096]{1,0:T(8,128)S(1)}, f32[32,4096]{1,0:T(8,128)S(1)}, u32[]{:S(2)}, u32[]{:S(2)}) %collective-permute-start.9) | collective-permute-done | bytes 524320 | tf_op jit(solution)/shard_map/ppermute | solution.py:151
  76.7 0.2 fusion.28
  77.0 2.7 %collective-permute-start.14 = (f32[32,4096]{1,0:T(8,128)S(1)}, f32[32,4096]{1,0:T(8,128)S(1)}, u32[]{:S(2)}, u32[]{:S(2)}) collective-permute-start(f32[32,4096]{1,0:T(8,128)S(1)} %get-tuple-element.58), channel_id=1, source_target_pairs={{0,14},{2,0},{4,2},{6,4},{8,6},{10,8},{12,10},{14,12},{1,15},{3,1}... | collective-permute-start | bytes 1572872 | tf_op jit(solution)/shard_map/ppermute | solution.py:151
  79.7 8.3 %collective-permute-done.15 = f32[32,4096]{1,0:T(8,128)S(1)} collective-permute-done((f32[32,4096]{1,0:T(8,128)S(1)}, f32[32,4096]{1,0:T(8,128)S(1)}, u32[]{:S(2)}, u32[]{:S(2)}) %collective-permute-start.15) | collective-permute-done | bytes 524320 | tf_op jit(solution)/shard_map/ppermute | solution.py:151
  88.0 0.2 fusion.26
  88.3 2.7 %collective-permute-start.18 = (f32[32,4096]{1,0:T(8,128)S(1)}, f32[32,4096]{1,0:T(8,128)S(1)}, u32[]{:S(2)}, u32[]{:S(2)}) collective-permute-start(f32[32,4096]{1,0:T(8,128)S(1)} %get-tuple-element.56), channel_id=1, source_target_pairs={{0,14},{2,0},{4,2},{6,4},{8,6},{10,8},{12,10},{14,12},{1,15},{3,1}... | collective-permute-start | bytes 1572872 | tf_op jit(solution)/shard_map/ppermute | solution.py:151
  90.9 8.3 %collective-permute-done.13 = f32[32,4096]{1,0:T(8,128)S(1)} collective-permute-done((f32[32,4096]{1,0:T(8,128)S(1)}, f32[32,4096]{1,0:T(8,128)S(1)}, u32[]{:S(2)}, u32[]{:S(2)}) %collective-permute-start.13) | collective-permute-done | bytes 524320 | tf_op jit(solution)/shard_map/ppermute | solution.py:151
  99.2 0.1 fusion.35
  99.3 11.1 %collective-permute-done.17 = f32[32,4096]{1,0:T(8,128)S(1)} collective-permute-done((f32[32,4096]{1,0:T(8,128)S(1)}, f32[32,4096]{1,0:T(8,128)S(1)}, u32[]{:S(2)}, u32[]{:S(2)}) %collective-permute-start.17) | collective-permute-done | bytes 524320 | tf_op jit(solution)/shard_map/ppermute | solution.py:151
  110.4 0.1 fusion.25
  110.6 0.8 bitcast_subtract_fusion
  111.6 22.4 %all_to_all.15 = f32[16,32,512]{2,1,0:T(8,128)S(1)} all-to-all(f32[16,32,512]{2,1,0:T(8,128)S(1)} %bitcast.47), channel_id=1, replica_groups=mesh['y'=4,'x'=4,'z'=8,'c'=2] {'y','x'}, dimensions={0} | all-to-all | bytes 2097152 | tf_op jit(solution)/shard_map/all_to_all | solution.py:177
  134.2 18.4 %all_to_all.16.pieces_ref = f32[16,32,512]{2,1,0:T(8,128)S(1)} all-to-all(f32[16,32,512]{2,1,0:T(8,128)S(1)} %broadcast_in_dim.31), channel_id=1, replica_groups=mesh['y'=4,'x'=4,'z'=8,'c'=2] {'y','x'}, dimensions={0} | all-to-all | bytes 2097152 | tf_op jit(solution)/shard_map/all_to_all | solution.py:180
  152.6 0.9 multiply_reduce_fusion
  153.5 1.2 broadcast_in_dim.32
  154.7 6.2 %all-to-all-start.2 = ((f32[16,1,128]{2,1,0:T(1,128)}), f32[16,1,128]{2,1,0:T(1,128)S(1)}, u32[]{:S(2)}, u32[]{:S(2)}) async-start(f32[16,1,128]{2,1,0:T(1,128)} %broadcast_in_dim.32), calls=%async_computation.2 | async-start | bytes 16384 | tf_op jit(solution)/shard_map/all_to_all | solution.py:182
  160.9 3.2 %fusion.12 = (f32[1,32,8192]{2,1,0:T(8,128)}, f32[1,32,8192]{2,1,0:T(8,128)}) fusion(f32[1,32,8192]{2,1,0:T(8,128)} %param.12, f32[1,32,4096]{2,1,0:T(8,128)S(1)} %bitcast.46, f32[1,32,4096]{2,1,0:T(8,128)S(1)} %bitcast.45, f32[1,32,8192]{2,1,0:T(8,128)} %param.11), kind=kLoop, calls=%fused_computation.24 | loop fusion | flops 2097152 | bytes 5242880 | tf_op jit(solution)/shard_map/add | solution.py:168
  164.1 3.8 %all-to-all-done.2.squares_ref = f32[16,1,128]{2,1,0:T(1,128)S(1)} async-done(((f32[16,1,128]{2,1,0:T(1,128)}), f32[16,1,128]{2,1,0:T(1,128)S(1)}, u32[]{:S(2)}, u32[]{:S(2)}) %all-to-all-start.2) | async-done | bytes 8224 | tf_op jit(solution)/shard_map/all_to_all | solution.py:182
  167.9 0.6 copy-done.8
  168.5 3.0 %shard_map.104 = (f32[32,8192]{1,0:T(8,128)}, f32[32,8192]{1,0:T(8,128)}) custom-call(f32[16,1,128]{2,1,0:T(1,128)} %copy-done.8, f32[16,32,512]{2,1,0:T(8,128)} %copy-done.2, f32[32,8192]{1,0:T(8,128)} %anchor_ref.1, f32[32,8192]{1,0:T(8,128)} %momentum_ref.1), custom_call_target="tpu_custom_call" | custom-call | flops 1835008 | bytes 5242880 | tf_op jit(solution)/shard_map/pallas_call | solution.py:97
  (53 shorter events, 1.5 us)
Async XLA Ops:
  0.6 1.1 copy-start
  7.3 7.9 %copy-start.7 = (f32[32,4096]{1,0:T(8,128)S(1)}, f32[32,4096]{1,0:T(8,128)}, u32[]{:S(2)}) copy-start(f32[32,4096]{1,0:T(8,128)} %get-tuple-element.34) | copy-start | bytes 1572868
  7.3 7.9 %collective-permute-start.1 = (f32[32,4096]{1,0:T(8,128)}, f32[32,4096]{1,0:T(8,128)S(1)}, u32[]{:S(2)}, u32[]{:S(2)}) collective-permute-start(f32[32,4096]{1,0:T(8,128)} %get-tuple-element.30), channel_id=1, source_target_pairs={{0,1},{1,0},{2,3},{3,2},{4,5},{5,4},{6,7},{7,6},{8,9},{9,8},{10,11... | collective-permute-start | bytes 1572872 | tf_op jit(solution)/shard_map/ppermute | solution.py:140
  15.1 2.1 %collective-permute-start = (f32[32,4096]{1,0:T(8,128)}, f32[32,4096]{1,0:T(8,128)S(1)}, u32[]{:S(2)}, u32[]{:S(2)}) collective-permute-start(f32[32,4096]{1,0:T(8,128)} %get-tuple-element.33), channel_id=1, source_target_pairs={{0,1},{1,0},{2,3},{3,2},{4,5},{5,4},{6,7},{7,6},{8,9},{9,8},{10,11... | collective-permute-start | bytes 1572872 | tf_op jit(solution)/shard_map/ppermute | solution.py:140
  18.3 12.5 %slice-start = ((s8[8388608]{0:T(1024)(128)(4,1)}), s8[4194304]{0:T(1024)(128)(4,1)S(1)}, s32[]{:S(2)}) async-start(s8[8388608]{0:T(1024)(128)(4,1)} %bitcast.41), calls=%async_computation.3 | async-start | bytes 8388608
  18.4 12.4 %slice-start.1 = ((s8[8388608]{0:T(1024)(128)(4,1)}), s8[4194304]{0:T(1024)(128)(4,1)S(1)}, s32[]{:S(2)}) async-start(s8[8388608]{0:T(1024)(128)(4,1)} %bitcast.41), calls=%async_computation.4 | async-start | bytes 8388608
  24.0 11.7 %collective-permute-start.2 = (f32[224,8192]{1,0:T(8,128)S(1)}, f32[224,8192]{1,0:T(8,128)S(1)}, u32[]{:S(2)}, u32[]{:S(2)}) collective-permute-start(f32[224,8192]{1,0:T(8,128)S(1)} %fusion.69), channel_id=1, source_target_pairs={{0,1},{1,0},{2,3},{3,2},{4,5},{5,4},{6,7},{7,6},{8,9},{9,8},{10,11... | collective-permute-start | bytes 22020104 | tf_op jit(solution)/shard_map/ppermute | solution.py:146
  24.2 10.2 %collective-permute-start.3 = (f32[32,2048]{1,0:T(8,128)S(1)}, f32[32,2048]{1,0:T(8,128)S(1)}, u32[]{:S(2)}, u32[]{:S(2)}) collective-permute-start(f32[32,2048]{1,0:T(8,128)S(1)} %get-tuple-element.79), channel_id=1, source_target_pairs={{0,2},{2,4},{4,6},{6,8},{8,10},{10,12},{12,14},{14,0},{1,3},{3,5},... | collective-permute-start | bytes 786440 | tf_op jit(solution)/shard_map/ppermute | solution.py:151
  24.2 10.2 %collective-permute-start.4 = (f32[32,2048]{1,0:T(8,128)S(1)}, f32[32,2048]{1,0:T(8,128)S(1)}, u32[]{:S(2)}, u32[]{:S(2)}) collective-permute-start(f32[32,2048]{1,0:T(8,128)S(1)} %get-tuple-element.78), channel_id=1, source_target_pairs={{0,14},{2,0},{4,2},{6,4},{8,6},{10,8},{12,10},{14,12},{1,15},{3,1}... | collective-permute-start | bytes 786440 | tf_op jit(solution)/shard_map/ppermute | solution.py:151
  28.1 11.9 %collective-permute-start.7 = (f32[32,2048]{1,0:T(8,128)S(1)}, f32[32,2048]{1,0:T(8,128)S(1)}, u32[]{:S(2)}, u32[]{:S(2)}) collective-permute-start(f32[32,2048]{1,0:T(8,128)S(1)} %get-tuple-element.77), channel_id=1, source_target_pairs={{0,2},{2,4},{4,6},{6,8},{8,10},{10,12},{12,14},{14,0},{1,3},{3,5},... | collective-permute-start | bytes 786440 | tf_op jit(solution)/shard_map/ppermute | solution.py:151
  28.1 11.9 %collective-permute-start.8 = (f32[32,2048]{1,0:T(8,128)S(1)}, f32[32,2048]{1,0:T(8,128)S(1)}, u32[]{:S(2)}, u32[]{:S(2)}) collective-permute-start(f32[32,2048]{1,0:T(8,128)S(1)} %get-tuple-element.76), channel_id=1, source_target_pairs={{0,14},{2,0},{4,2},{6,4},{8,6},{10,8},{12,10},{14,12},{1,15},{3,1}... | collective-permute-start | bytes 786440 | tf_op jit(solution)/shard_map/ppermute | solution.py:151
  35.9 15.1 %collective-permute-start.6 = (f32[32,4096]{1,0:T(8,128)S(1)}, f32[32,4096]{1,0:T(8,128)S(1)}, u32[]{:S(2)}, u32[]{:S(2)}) collective-permute-start(f32[32,4096]{1,0:T(8,128)S(1)} %pad_maximum_fusion.3), channel_id=1, source_target_pairs={{0,14},{2,0},{4,2},{6,4},{8,6},{10,8},{12,10},{14,12},{1,15},{3,1}... | collective-permute-start | bytes 1572872 | tf_op jit(solution)/shard_map/ppermute | solution.py:151
  39.9 14.4 %collective-permute-start.5 = (f32[32,4096]{1,0:T(8,128)S(1)}, f32[32,4096]{1,0:T(8,128)S(1)}, u32[]{:S(2)}, u32[]{:S(2)}) collective-permute-start(f32[32,4096]{1,0:T(8,128)S(1)} %pad_maximum_fusion.2), channel_id=1, source_target_pairs={{0,2},{2,4},{4,6},{6,8},{8,10},{10,12},{12,14},{14,0},{1,3},{3,5},... | collective-permute-start | bytes 1572872 | tf_op jit(solution)/shard_map/ppermute | solution.py:151
  40.3 22.0 %collective-permute-start.12 = (f32[32,4096]{1,0:T(8,128)S(1)}, f32[32,4096]{1,0:T(8,128)S(1)}, u32[]{:S(2)}, u32[]{:S(2)}) collective-permute-start(f32[32,4096]{1,0:T(8,128)S(1)} %pad_maximum_fusion.5), channel_id=1, source_target_pairs={{0,14},{2,0},{4,2},{6,4},{8,6},{10,8},{12,10},{14,12},{1,15},{3,1}... | collective-permute-start | bytes 1572872 | tf_op jit(solution)/shard_map/ppermute | solution.py:151
  43.1 22.3 %collective-permute-start.11 = (f32[32,4096]{1,0:T(8,128)S(1)}, f32[32,4096]{1,0:T(8,128)S(1)}, u32[]{:S(2)}, u32[]{:S(2)}) collective-permute-start(f32[32,4096]{1,0:T(8,128)S(1)} %pad_maximum_fusion.4), channel_id=1, source_target_pairs={{0,2},{2,4},{4,6},{6,8},{8,10},{10,12},{12,14},{14,0},{1,3},{3,5},... | collective-permute-start | bytes 1572872 | tf_op jit(solution)/shard_map/ppermute | solution.py:151
  54.5 19.1 %collective-permute-start.10 = (f32[32,4096]{1,0:T(8,128)S(1)}, f32[32,4096]{1,0:T(8,128)S(1)}, u32[]{:S(2)}, u32[]{:S(2)}) collective-permute-start(f32[32,4096]{1,0:T(8,128)S(1)} %get-tuple-element.62), channel_id=1, source_target_pairs={{0,14},{2,0},{4,2},{6,4},{8,6},{10,8},{12,10},{14,12},{1,15},{3,1}... | collective-permute-start | bytes 1572872 | tf_op jit(solution)/shard_map/ppermute | solution.py:151
  54.8 22.0 %collective-permute-start.9 = (f32[32,4096]{1,0:T(8,128)S(1)}, f32[32,4096]{1,0:T(8,128)S(1)}, u32[]{:S(2)}, u32[]{:S(2)}) collective-permute-start(f32[32,4096]{1,0:T(8,128)S(1)} %get-tuple-element.63), channel_id=1, source_target_pairs={{0,2},{2,4},{4,6},{6,8},{8,10},{10,12},{12,14},{14,0},{1,3},{3,5},... | collective-permute-start | bytes 1572872 | tf_op jit(solution)/shard_map/ppermute | solution.py:151
  65.7 44.9 %copy-start.3 = (f32[1,32,8192]{2,1,0:T(8,128)S(1)}, f32[1,32,8192]{2,1,0:T(8,128)}, u32[]{:S(2)}) copy-start(f32[1,32,8192]{2,1,0:T(8,128)} %param.12) | copy-start | bytes 3145732
  65.7 44.9 %copy-start.4 = (f32[1,32,8192]{2,1,0:T(8,128)S(1)}, f32[1,32,8192]{2,1,0:T(8,128)}, u32[]{:S(2)}) copy-start(f32[1,32,8192]{2,1,0:T(8,128)} %param.11) | copy-start | bytes 3145732
  65.7 44.9 %copy-start.5 = (f32[32,8192]{1,0:T(8,128)S(1)}, f32[32,8192]{1,0:T(8,128)}, u32[]{:S(2)}) copy-start(f32[32,8192]{1,0:T(8,128)} %anchor_ref.1) | copy-start | bytes 3145732
  65.7 44.9 %copy-start.6 = (f32[1,32,8192]{2,1,0:T(8,128)S(1)}, f32[1,32,8192]{2,1,0:T(8,128)}, u32[]{:S(2)}) copy-start(f32[1,32,8192]{2,1,0:T(8,128)} %param.10) | copy-start | bytes 3145732
  65.7 22.2 %collective-permute-start.15 = (f32[32,4096]{1,0:T(8,128)S(1)}, f32[32,4096]{1,0:T(8,128)S(1)}, u32[]{:S(2)}, u32[]{:S(2)}) collective-permute-start(f32[32,4096]{1,0:T(8,128)S(1)} %get-tuple-element.61), channel_id=1, source_target_pairs={{0,2},{2,4},{4,6},{6,8},{8,10},{10,12},{12,14},{14,0},{1,3},{3,5},... | collective-permute-start | bytes 1572872 | tf_op jit(solution)/shard_map/ppermute | solution.py:151
  65.8 22.1 %collective-permute-start.16 = (f32[32,4096]{1,0:T(8,128)S(1)}, f32[32,4096]{1,0:T(8,128)S(1)}, u32[]{:S(2)}, u32[]{:S(2)}) collective-permute-start(f32[32,4096]{1,0:T(8,128)S(1)} %get-tuple-element.60), channel_id=1, source_target_pairs={{0,14},{2,0},{4,2},{6,4},{8,6},{10,8},{12,10},{14,12},{1,15},{3,1}... | collective-permute-start | bytes 1572872 | tf_op jit(solution)/shard_map/ppermute | solution.py:151
  76.9 22.3 %collective-permute-start.13 = (f32[32,4096]{1,0:T(8,128)S(1)}, f32[32,4096]{1,0:T(8,128)S(1)}, u32[]{:S(2)}, u32[]{:S(2)}) collective-permute-start(f32[32,4096]{1,0:T(8,128)S(1)} %get-tuple-element.59), channel_id=1, source_target_pairs={{0,2},{2,4},{4,6},{6,8},{8,10},{10,12},{12,14},{14,0},{1,3},{3,5},... | collective-permute-start | bytes 1572872 | tf_op jit(solution)/shard_map/ppermute | solution.py:151
  77.0 22.2 %collective-permute-start.14 = (f32[32,4096]{1,0:T(8,128)S(1)}, f32[32,4096]{1,0:T(8,128)S(1)}, u32[]{:S(2)}, u32[]{:S(2)}) collective-permute-start(f32[32,4096]{1,0:T(8,128)S(1)} %get-tuple-element.58), channel_id=1, source_target_pairs={{0,14},{2,0},{4,2},{6,4},{8,6},{10,8},{12,10},{14,12},{1,15},{3,1}... | collective-permute-start | bytes 1572872 | tf_op jit(solution)/shard_map/ppermute | solution.py:151
  88.2 22.3 %collective-permute-start.17 = (f32[32,4096]{1,0:T(8,128)S(1)}, f32[32,4096]{1,0:T(8,128)S(1)}, u32[]{:S(2)}, u32[]{:S(2)}) collective-permute-start(f32[32,4096]{1,0:T(8,128)S(1)} %get-tuple-element.57), channel_id=1, source_target_pairs={{0,2},{2,4},{4,6},{6,8},{8,10},{10,12},{12,14},{14,0},{1,3},{3,5},... | collective-permute-start | bytes 1572872 | tf_op jit(solution)/shard_map/ppermute | solution.py:151
  88.3 22.2 %collective-permute-start.18 = (f32[32,4096]{1,0:T(8,128)S(1)}, f32[32,4096]{1,0:T(8,128)S(1)}, u32[]{:S(2)}, u32[]{:S(2)}) collective-permute-start(f32[32,4096]{1,0:T(8,128)S(1)} %get-tuple-element.56), channel_id=1, source_target_pairs={{0,14},{2,0},{4,2},{6,4},{8,6},{10,8},{12,10},{14,12},{1,15},{3,1}... | collective-permute-start | bytes 1572872 | tf_op jit(solution)/shard_map/ppermute | solution.py:151
  111.5 60.0 %copy-start.1 = (bf16[1,512,512]{2,1,0:T(8,128)(2,1)S(1)}, bf16[1,512,512]{2,1,0:T(8,128)(2,1)}, u32[]{:S(2)}) copy-start(bf16[1,512,512]{2,1,0:T(8,128)(2,1)} %param.7) | copy-start | bytes 1572868
  152.6 15.3 %copy-start.2 = (f32[16,32,512]{2,1,0:T(8,128)}, f32[16,32,512]{2,1,0:T(8,128)S(1)}, u32[]{:S(2)}) copy-start(f32[16,32,512]{2,1,0:T(8,128)S(1)} %all_to_all.16.pieces_ref) | copy-start | bytes 3145732
  154.7 13.2 %all-to-all-start.2 = ((f32[16,1,128]{2,1,0:T(1,128)}), f32[16,1,128]{2,1,0:T(1,128)S(1)}, u32[]{:S(2)}, u32[]{:S(2)}) async-start(f32[16,1,128]{2,1,0:T(1,128)} %broadcast_in_dim.32), calls=%async_computation.2 | async-start | bytes 16384 | tf_op jit(solution)/shard_map/all_to_all | solution.py:182
  167.9 0.6 copy-start.8

commit v5 on v4

--- a/solution.py
+++ b/solution.py
@@ -47,37 +47,8 @@
     ).astype(activations.dtype)
 
 
-def head_kernel(rows_ref, cols_ref, theirs_ref, mine_ref):
-    out = jnp.dot(rows_ref[...], cols_ref[...], preferred_element_type=jnp.float32)
-    theirs_ref[...] = out[:ROWS_DEV]
-    mine_ref[...] = out[ROWS_DEV:]
-
-
-def head_rows(ordered, cotangent, k):
-    tokens = cotangent.shape[0]
-    block = 1024
-    count = WIDTH // block
-    out = pl.BlockSpec((ROWS_DEV, block), lambda n: (0, n))
-    shape = jax.ShapeDtypeStruct((ROWS_DEV, WIDTH), jnp.float32)
-    return pl.pallas_call(
-        head_kernel,
-        grid=(count,),
-        in_specs=[
-            pl.BlockSpec((2 * ROWS_DEV, tokens), lambda n: (0, 0)),
-            pl.BlockSpec((tokens, block), lambda n: (0, k * count + n)),
-        ],
-        out_specs=[out, out],
-        out_shape=[shape, shape],
-        cost_estimate=pl.CostEstimate(
-            flops=4 * ROWS_DEV * tokens * WIDTH,
-            bytes_accessed=2 * tokens * WIDTH + 8 * ROWS_DEV * WIDTH,
-            transcendentals=0,
-        ),
-    )(ordered, cotangent)
-
-
 def finish_kernel(squares_ref, pieces_ref, anchor_ref, momentum_ref, momentum_out, anchor_out):
-    squares = jnp.sum(squares_ref[:, 0, 0:1], axis=0, keepdims=True)
+    squares = jnp.sum(jnp.sum(squares_ref[...], axis=0), keepdims=True)
     ceiling = 0.3 * math.sqrt(ROWS_DEV * PARTS * D)
     factor = ceiling / jnp.maximum(jnp.sqrt(squares), ceiling)
     piece = pieces_ref.shape[2]
@@ -133,18 +104,18 @@
         base = k * WIDTH
         return kept[k][at : at + ROWS_DEV, lo:hi] + rest[at : at + ROWS_DEV, base + lo : base + hi]
 
-    first_rows = ordered[:near]
-    last = ()
+    first = product(ordered[:near], cotangent)
+    theirs = lax.optimization_barrier(first[:ROWS_DEV])
+    got = lax.ppermute(theirs, "c", SWAP)
+    sent = product(after(ordered[near:stay], theirs), cotangent)
+    rest = lax.ppermute(after(sent, got), "c", SWAP)
+    first = first[ROWS_DEV:] + got
     for k in chunks:
-        sent, stays = head_rows(first_rows, cotangent, k)
-        first = stays + after(lax.ppermute(sent, "c", SWAP), last)
-        up[k], down[k] = first[:, HALF:], first[:, :HALF]
-        first_rows = after(first_rows, sent)
-        last = (up[k], down[k])
+        up[k] = first[:, k * WIDTH + HALF : (k + 1) * WIDTH]
+        down[k] = first[:, k * WIDTH : k * WIDTH + HALF]
+        first = after(first, up[k], down[k])
     last = (up[-1], down[-1])
-    sent = product(after(ordered[near:stay], last), cotangent)
-    rest = lax.ppermute(sent, "c", SWAP)
-    lhs = after(ordered[stay:], sent)
+    lhs = after(ordered[stay:], sent, last)
     kept = [product(lhs, cols[k]) for k in chunks]
     for t in range(1, 5):
         for k in chunks:
@@ -178,7 +149,8 @@
     part = jnp.sum(met, axis=0) / replicas
     copies = jnp.broadcast_to(part[None], (replicas, ROWS_DEV, piece))
     pieces = lax.all_to_all(copies, ("y", "x"), split_axis=0, concat_axis=0, tiled=True)
-    squares = jnp.broadcast_to(jnp.sum(pieces * pieces), (PARTS, 1, 128))
+    squares = jnp.sum(jnp.sum(pieces * pieces, axis=(0, 1)).reshape(-1, 128), axis=0)
+    squares = jnp.broadcast_to(squares, (PARTS, 1, 128))
     squares = lax.all_to_all(squares, ("z", "c"), split_axis=0, concat_axis=0, tiled=True)
     momentum, updated = finish(squares, pieces, anchor, outer_momentum)
     return (moment_one[None], moment_two[None], momentum, updated)

time: 172 us -> 159 us (0.924)
  Pallas kernels: 12.1 us -> 3.1 us
  waiting for transfers between devices: 64.9 us -> 58.8 us
  starting transfers between devices: 33 us -> 36.6 us
  matrix products: 8.36 us -> 6.39 us
  other arithmetic: 7.6 us -> 5.81 us
  local copies, waits for them, and re-layouts: 3.83 us -> 5.62 us
    pallas_call x2 -> x0, Pallas kernels: 9.01 us -> none  [head_rows(): pl.pallas_call(head_kernel, grid=(count,), in_specs=[pl.BlockSpec((2 * RO...]
    ppermute x16, waiting for transfers between devices: 57.9 us -> 54.2 us  [per_device(): moved = (lax.ppermute(up[k], 'z', UP), lax.ppermute(down[k], 'z', DOWN))]
    unnamed x22 -> x18, local copies, waits for them, and re-layouts: 1.65 us -> 4.49 us
    ppermute x3 -> x2, waiting for transfers between devices: 3.19 us -> 0.83 us  [the longest x1 0.66 us: per_device(): rest = lax.ppermute(after(sent, got), 'c', SWAP)]
    all_to_all x1, starting transfers between devices: 6.21 us -> 8.2 us  [per_device(): lax.all_to_all(squares, ('z', 'c'), split_axis=0, concat_axis=0, tiled=True)]
    dot_general x3 -> x4, matrix products: 7.85 us -> 5.88 us  [product(): lax.dot_general(lhs, rhs, (((1,), (0,)), ((), ())), preferred_element_typ...]
    ppermute x3 -> x2, starting transfers between devices: 3.54 us -> 3.7 us  [the longest x1 3.33 us: per_device(): got = lax.ppermute(theirs, 'c', SWAP)]
  transfers between devices with their start and end apart: 20 -> 19, of which waited for: 14 -> 11; matrix products, arithmetic and copies ran while one was open for 4% -> 6% of each run, Pallas kernels for 3% -> 0%
where the time goes in v5:
time: 159 us; the launch traced here: 158 us
  waiting for transfers between devices  58.8 us (37%)
  blocking collectives  41 us (26%)
  starting transfers between devices  36.6 us (23%)
  matrix products  6.39 us (4%)
  other arithmetic  5.81 us (4%)
  local copies, waits for them, and re-layouts  5.62 us (4%)
  Pallas kernels  3.1 us (2%)
    ppermute x16, waiting for transfers between devices, per_device(): moved = (lax.ppermute(up[k], 'z', UP), lax.ppermute(down[k], 'z', DOWN))  54.2 us
    ppermute x16, starting transfers between devices, per_device(): moved = (lax.ppermute(up[k], 'z', UP), lax.ppermute(down[k], 'z', DOWN))  24.7 us
    all_to_all x1, blocking collectives, per_device(): lax.all_to_all(spread, ('y', 'x'), split_axis=0, concat_axis=0, tiled=True)  22.8 us
    all_to_all x1, blocking collectives, per_device(): lax.all_to_all(copies, ('y', 'x'), split_axis=0, concat_axis=0, tiled=True)  18.3 us
    all_to_all x1, starting transfers between devices, per_device(): lax.all_to_all(squares, ('z', 'c'), split_axis=0, concat_axis=0, tiled=True)  8.2 us
    dot_general x4, matrix products, product(): lax.dot_general(lhs, rhs, (((1,), (0,)), ((), ())), preferred_element_typ...  5.88 us
    unnamed x18, local copies, waits for them, and re-layouts  4.49 us
    all_to_all x1, waiting for transfers between devices, per_device(): lax.all_to_all(squares, ('z', 'c'), split_axis=0, concat_axis=0, tiled=True)  3.79 us
  transfers between devices with their start and end apart: 19, of which 11 were waited for; matrix products, arithmetic and copies ran while one was open for 6% of the time, Pallas kernels for 0%

profile of v5, /device:TPU:1, one launch (start us, length us, event | category | flops | bytes accessed | tf_op | source)
XLA Modules:
  0.0 158.4 jit_solution(17226235281010439103)
XLA Ops:
  0.7 1.0 copy-done
  1.7 0.5 convolution_convert_fusion
  2.2 2.9 %copy-done.2 = bf16[1,512,8192]{2,1,0:T(8,128)(2,1)S(1)} copy-done((bf16[1,512,8192]{2,1,0:T(8,128)(2,1)S(1)}, bf16[1,512,8192]{2,1,0:T(8,128)(2,1)}, u32[]{:S(2)}) %copy-start.2) | copy-done | bytes 8388632
  5.1 1.6 fusion.63
  6.7 3.3 %collective-permute-start = (f32[32,8192]{1,0:T(8,128)S(1)}, f32[32,8192]{1,0:T(8,128)S(1)}, u32[]{:S(2)}, u32[]{:S(2)}) collective-permute-start(f32[32,8192]{1,0:T(8,128)S(1)} %slice.191), channel_id=1, source_target_pairs={{0,1},{1,0},{2,3},{3,2},{4,5},{5,4},{6,7},{7,6},{8,9},{9,8},{10,11... | collective-permute-start | bytes 3145736 | tf_op jit(solution)/shard_map/ppermute | solution.py:109
  10.1 2.1 %fusion.71 = f32[224,8192]{1,0:T(8,128)S(1)} fusion(bf16[224,512]{1,0:T(8,128)(2,1)S(1)} %get-tuple-element.26, bf16[1,512,8192]{2,1,0:T(8,128)(2,1)S(1)} %copy-done.2), kind=kOutput, calls=%fused_computation.119 | convolution fusion | flops 1879048192 | bytes 15958016 | tf_op jit(solution)/shard_map/dot_general | solution.py:92
  12.2 0.2 collective-permute-done
  12.3 0.4 collective-permute-start.1
  12.7 0.1 slice_add_fusion
  12.9 3.9 %collective-permute-start.3 = (f32[32,2048]{1,0:T(8,128)S(1)}, f32[32,2048]{1,0:T(8,128)S(1)}, u32[]{:S(2)}, u32[]{:S(2)}) collective-permute-start(f32[32,2048]{1,0:T(8,128)S(1)} %get-tuple-element.68), channel_id=1, source_target_pairs={{0,14},{2,0},{4,2},{6,4},{8,6},{10,8},{12,10},{14,12},{1,15},{3,1}... | collective-permute-start | bytes 786440 | tf_op jit(solution)/shard_map/ppermute | solution.py:122
  17.0 2.7 %collective-permute-start.7 = (f32[32,2048]{1,0:T(8,128)S(1)}, f32[32,2048]{1,0:T(8,128)S(1)}, u32[]{:S(2)}, u32[]{:S(2)}) collective-permute-start(f32[32,2048]{1,0:T(8,128)S(1)} %get-tuple-element.66), channel_id=1, source_target_pairs={{0,14},{2,0},{4,2},{6,4},{8,6},{10,8},{12,10},{14,12},{1,15},{3,1}... | collective-permute-start | bytes 786440 | tf_op jit(solution)/shard_map/ppermute | solution.py:122
  19.7 1.1 fusion.2
  20.8 1.1 fusion
  21.9 1.4 collective-permute-done.2
  23.3 0.7 collective-permute-done.1
  24.0 0.1 fusion.61
  24.3 3.9 %collective-permute-start.5 = (f32[32,4096]{1,0:T(8,128)S(1)}, f32[32,4096]{1,0:T(8,128)S(1)}, u32[]{:S(2)}, u32[]{:S(2)}) collective-permute-start(f32[32,4096]{1,0:T(8,128)S(1)} %pad_maximum_fusion.3), channel_id=1, source_target_pairs={{0,14},{2,0},{4,2},{6,4},{8,6},{10,8},{12,10},{14,12},{1,15},{3,1}... | collective-permute-start | bytes 1572872 | tf_op jit(solution)/shard_map/ppermute | solution.py:122
  28.2 0.7 collective-permute-done.6
  28.9 0.1 fusion.59
  29.1 0.3 collective-permute-start.10
  29.4 2.7 %collective-permute-start.11 = (f32[32,4096]{1,0:T(8,128)S(1)}, f32[32,4096]{1,0:T(8,128)S(1)}, u32[]{:S(2)}, u32[]{:S(2)}) collective-permute-start(f32[32,4096]{1,0:T(8,128)S(1)} %pad_maximum_fusion.5), channel_id=1, source_target_pairs={{0,14},{2,0},{4,2},{6,4},{8,6},{10,8},{12,10},{14,12},{1,15},{3,1}... | collective-permute-start | bytes 1572872 | tf_op jit(solution)/shard_map/ppermute | solution.py:122
  32.2 7.9 %collective-permute-done.4 = f32[32,4096]{1,0:T(8,128)S(1)} collective-permute-done((f32[32,4096]{1,0:T(8,128)S(1)}, f32[32,4096]{1,0:T(8,128)S(1)}, u32[]{:S(2)}, u32[]{:S(2)}) %collective-permute-start.4) | collective-permute-done | bytes 524320 | tf_op jit(solution)/shard_map/ppermute | solution.py:122
  40.1 0.2 fusion.31
  40.4 2.7 %collective-permute-start.9 = (f32[32,4096]{1,0:T(8,128)S(1)}, f32[32,4096]{1,0:T(8,128)S(1)}, u32[]{:S(2)}, u32[]{:S(2)}) collective-permute-start(f32[32,4096]{1,0:T(8,128)S(1)} %get-tuple-element.54), channel_id=1, source_target_pairs={{0,14},{2,0},{4,2},{6,4},{8,6},{10,8},{12,10},{14,12},{1,15},{3,1}... | collective-permute-start | bytes 1572872 | tf_op jit(solution)/shard_map/ppermute | solution.py:122
  43.1 8.3 %collective-permute-done.10 = f32[32,4096]{1,0:T(8,128)S(1)} collective-permute-done((f32[32,4096]{1,0:T(8,128)S(1)}, f32[32,4096]{1,0:T(8,128)S(1)}, u32[]{:S(2)}, u32[]{:S(2)}) %collective-permute-start.10) | collective-permute-done | bytes 524320 | tf_op jit(solution)/shard_map/ppermute | solution.py:122
  51.3 0.2 fusion.29
  51.7 2.7 %collective-permute-start.15 = (f32[32,4096]{1,0:T(8,128)S(1)}, f32[32,4096]{1,0:T(8,128)S(1)}, u32[]{:S(2)}, u32[]{:S(2)}) collective-permute-start(f32[32,4096]{1,0:T(8,128)S(1)} %get-tuple-element.52), channel_id=1, source_target_pairs={{0,14},{2,0},{4,2},{6,4},{8,6},{10,8},{12,10},{14,12},{1,15},{3,1}... | collective-permute-start | bytes 1572872 | tf_op jit(solution)/shard_map/ppermute | solution.py:122
  54.3 8.2 %collective-permute-done.8 = f32[32,4096]{1,0:T(8,128)S(1)} collective-permute-done((f32[32,4096]{1,0:T(8,128)S(1)}, f32[32,4096]{1,0:T(8,128)S(1)}, u32[]{:S(2)}, u32[]{:S(2)}) %collective-permute-start.8) | collective-permute-done | bytes 524320 | tf_op jit(solution)/shard_map/ppermute | solution.py:122
  62.6 0.2 fusion.28
  62.8 2.7 %collective-permute-start.13 = (f32[32,4096]{1,0:T(8,128)S(1)}, f32[32,4096]{1,0:T(8,128)S(1)}, u32[]{:S(2)}, u32[]{:S(2)}) collective-permute-start(f32[32,4096]{1,0:T(8,128)S(1)} %get-tuple-element.50), channel_id=1, source_target_pairs={{0,14},{2,0},{4,2},{6,4},{8,6},{10,8},{12,10},{14,12},{1,15},{3,1}... | collective-permute-start | bytes 1572872 | tf_op jit(solution)/shard_map/ppermute | solution.py:122
  65.5 8.3 %collective-permute-done.14 = f32[32,4096]{1,0:T(8,128)S(1)} collective-permute-done((f32[32,4096]{1,0:T(8,128)S(1)}, f32[32,4096]{1,0:T(8,128)S(1)}, u32[]{:S(2)}, u32[]{:S(2)}) %collective-permute-start.14) | collective-permute-done | bytes 524320 | tf_op jit(solution)/shard_map/ppermute | solution.py:122
  73.8 0.2 fusion.26
  74.1 2.7 %collective-permute-start.17 = (f32[32,4096]{1,0:T(8,128)S(1)}, f32[32,4096]{1,0:T(8,128)S(1)}, u32[]{:S(2)}, u32[]{:S(2)}) collective-permute-start(f32[32,4096]{1,0:T(8,128)S(1)} %get-tuple-element.48), channel_id=1, source_target_pairs={{0,14},{2,0},{4,2},{6,4},{8,6},{10,8},{12,10},{14,12},{1,15},{3,1}... | collective-permute-start | bytes 1572872 | tf_op jit(solution)/shard_map/ppermute | solution.py:122
  76.8 8.3 %collective-permute-done.12 = f32[32,4096]{1,0:T(8,128)S(1)} collective-permute-done((f32[32,4096]{1,0:T(8,128)S(1)}, f32[32,4096]{1,0:T(8,128)S(1)}, u32[]{:S(2)}, u32[]{:S(2)}) %collective-permute-start.12) | collective-permute-done | bytes 524320 | tf_op jit(solution)/shard_map/ppermute | solution.py:122
  85.0 0.1 fusion.35
  85.2 11.1 %collective-permute-done.16 = f32[32,4096]{1,0:T(8,128)S(1)} collective-permute-done((f32[32,4096]{1,0:T(8,128)S(1)}, f32[32,4096]{1,0:T(8,128)S(1)}, u32[]{:S(2)}, u32[]{:S(2)}) %collective-permute-start.16) | collective-permute-done | bytes 524320 | tf_op jit(solution)/shard_map/ppermute | solution.py:122
  96.3 0.1 fusion.25
  96.4 0.8 bitcast_subtract_fusion
  97.4 22.8 %all_to_all.15 = f32[16,32,512]{2,1,0:T(8,128)S(1)} all-to-all(f32[16,32,512]{2,1,0:T(8,128)S(1)} %bitcast.47), channel_id=1, replica_groups=mesh['y'=4,'x'=4,'z'=8,'c'=2] {'y','x'}, dimensions={0} | all-to-all | bytes 2097152 | tf_op jit(solution)/shard_map/all_to_all | solution.py:148
  120.2 0.1 broadcast_in_dim.31
  120.3 18.3 %all_to_all.16.pieces_ref = f32[16,32,512]{2,1,0:T(8,128)S(1)} all-to-all(f32[16,32,512]{2,1,0:T(8,128)S(1)} %broadcast_in_dim.31), channel_id=1, replica_groups=mesh['y'=4,'x'=4,'z'=8,'c'=2] {'y','x'}, dimensions={0} | all-to-all | bytes 2097152 | tf_op jit(solution)/shard_map/all_to_all | solution.py:151
  138.6 0.1 multiply_reduce_fusion
  138.8 0.8 broadcast_in_dim.32
  139.5 8.2 %all-to-all-start.2 = ((f32[16,1,128]{2,1,0:T(1,128)}), f32[16,1,128]{2,1,0:T(1,128)S(1)}, u32[]{:S(2)}, u32[]{:S(2)}) async-start(f32[16,1,128]{2,1,0:T(1,128)} %broadcast_in_dim.32), calls=%async_computation.2 | async-start | bytes 16384 | tf_op jit(solution)/shard_map/all_to_all | solution.py:154
  147.7 3.2 %fusion.12 = (f32[1,32,8192]{2,1,0:T(8,128)}, f32[1,32,8192]{2,1,0:T(8,128)}) fusion(f32[1,32,8192]{2,1,0:T(8,128)} %param.12, f32[1,32,4096]{2,1,0:T(8,128)S(1)} %bitcast.46, f32[1,32,4096]{2,1,0:T(8,128)S(1)} %bitcast.45, f32[1,32,8192]{2,1,0:T(8,128)} %param.11), kind=kLoop, calls=%fused_computation.24 | loop fusion | flops 2097152 | bytes 5242880 | tf_op jit(solution)/shard_map/add | solution.py:139
  150.9 3.8 %all-to-all-done.2.squares_ref = f32[16,1,128]{2,1,0:T(1,128)S(1)} async-done(((f32[16,1,128]{2,1,0:T(1,128)}), f32[16,1,128]{2,1,0:T(1,128)S(1)}, u32[]{:S(2)}, u32[]{:S(2)}) %all-to-all-start.2) | async-done | bytes 8224 | tf_op jit(solution)/shard_map/all_to_all | solution.py:154
  154.7 0.6 copy-done.8
  155.3 3.1 %shard_map.102 = (f32[32,8192]{1,0:T(8,128)}, f32[32,8192]{1,0:T(8,128)}) custom-call(f32[16,1,128]{2,1,0:T(1,128)} %copy-done.8, f32[16,32,512]{2,1,0:T(8,128)} %copy-done.3, f32[32,8192]{1,0:T(8,128)} %anchor_ref.1, f32[32,8192]{1,0:T(8,128)} %momentum_ref.1), custom_call_target="tpu_custom_call" | custom-call | flops 1835008 | bytes 5242880 | tf_op jit(solution)/shard_map/pallas_call | solution.py:68
  (45 shorter events, 1.2 us)
Async XLA Ops:
  0.6 1.1 copy-start
  1.7 3.4 %copy-start.2 = (bf16[1,512,8192]{2,1,0:T(8,128)(2,1)S(1)}, bf16[1,512,8192]{2,1,0:T(8,128)(2,1)}, u32[]{:S(2)}) copy-start(bf16[1,512,8192]{2,1,0:T(8,128)(2,1)} %param.8) | copy-start | bytes 25165828
  6.7 5.6 %collective-permute-start = (f32[32,8192]{1,0:T(8,128)S(1)}, f32[32,8192]{1,0:T(8,128)S(1)}, u32[]{:S(2)}, u32[]{:S(2)}) collective-permute-start(f32[32,8192]{1,0:T(8,128)S(1)} %slice.191), channel_id=1, source_target_pairs={{0,1},{1,0},{2,3},{3,2},{4,5},{5,4},{6,7},{7,6},{8,9},{9,8},{10,11... | collective-permute-start | bytes 3145736 | tf_op jit(solution)/shard_map/ppermute | solution.py:109
  12.3 11.7 %collective-permute-start.1 = (f32[224,8192]{1,0:T(8,128)S(1)}, f32[224,8192]{1,0:T(8,128)S(1)}, u32[]{:S(2)}, u32[]{:S(2)}) collective-permute-start(f32[224,8192]{1,0:T(8,128)S(1)} %fusion.71), channel_id=1, source_target_pairs={{0,1},{1,0},{2,3},{3,2},{4,5},{5,4},{6,7},{7,6},{8,9},{9,8},{10,11... | collective-permute-start | bytes 22020104 | tf_op jit(solution)/shard_map/ppermute | solution.py:111
  12.9 10.5 %collective-permute-start.2 = (f32[32,2048]{1,0:T(8,128)S(1)}, f32[32,2048]{1,0:T(8,128)S(1)}, u32[]{:S(2)}, u32[]{:S(2)}) collective-permute-start(f32[32,2048]{1,0:T(8,128)S(1)} %get-tuple-element.69), channel_id=1, source_target_pairs={{0,2},{2,4},{4,6},{6,8},{8,10},{10,12},{12,14},{14,0},{1,3},{3,5},... | collective-permute-start | bytes 786440 | tf_op jit(solution)/shard_map/ppermute | solution.py:122
  12.9 10.4 %collective-permute-start.3 = (f32[32,2048]{1,0:T(8,128)S(1)}, f32[32,2048]{1,0:T(8,128)S(1)}, u32[]{:S(2)}, u32[]{:S(2)}) collective-permute-start(f32[32,2048]{1,0:T(8,128)S(1)} %get-tuple-element.68), channel_id=1, source_target_pairs={{0,14},{2,0},{4,2},{6,4},{8,6},{10,8},{12,10},{14,12},{1,15},{3,1}... | collective-permute-start | bytes 786440 | tf_op jit(solution)/shard_map/ppermute | solution.py:122
  16.9 12.0 %collective-permute-start.6 = (f32[32,2048]{1,0:T(8,128)S(1)}, f32[32,2048]{1,0:T(8,128)S(1)}, u32[]{:S(2)}, u32[]{:S(2)}) collective-permute-start(f32[32,2048]{1,0:T(8,128)S(1)} %get-tuple-element.67), channel_id=1, source_target_pairs={{0,2},{2,4},{4,6},{6,8},{8,10},{10,12},{12,14},{14,0},{1,3},{3,5},... | collective-permute-start | bytes 786440 | tf_op jit(solution)/shard_map/ppermute | solution.py:122
  17.0 11.9 %collective-permute-start.7 = (f32[32,2048]{1,0:T(8,128)S(1)}, f32[32,2048]{1,0:T(8,128)S(1)}, u32[]{:S(2)}, u32[]{:S(2)}) collective-permute-start(f32[32,2048]{1,0:T(8,128)S(1)} %get-tuple-element.66), channel_id=1, source_target_pairs={{0,14},{2,0},{4,2},{6,4},{8,6},{10,8},{12,10},{14,12},{1,15},{3,1}... | collective-permute-start | bytes 786440 | tf_op jit(solution)/shard_map/ppermute | solution.py:122
  24.2 15.9 %collective-permute-start.4 = (f32[32,4096]{1,0:T(8,128)S(1)}, f32[32,4096]{1,0:T(8,128)S(1)}, u32[]{:S(2)}, u32[]{:S(2)}) collective-permute-start(f32[32,4096]{1,0:T(8,128)S(1)} %pad_maximum_fusion.2), channel_id=1, source_target_pairs={{0,2},{2,4},{4,6},{6,8},{8,10},{10,12},{12,14},{14,0},{1,3},{3,5},... | collective-permute-start | bytes 1572872 | tf_op jit(solution)/shard_map/ppermute | solution.py:122
  24.3 15.8 %collective-permute-start.5 = (f32[32,4096]{1,0:T(8,128)S(1)}, f32[32,4096]{1,0:T(8,128)S(1)}, u32[]{:S(2)}, u32[]{:S(2)}) collective-permute-start(f32[32,4096]{1,0:T(8,128)S(1)} %pad_maximum_fusion.3), channel_id=1, source_target_pairs={{0,14},{2,0},{4,2},{6,4},{8,6},{10,8},{12,10},{14,12},{1,15},{3,1}... | collective-permute-start | bytes 1572872 | tf_op jit(solution)/shard_map/ppermute | solution.py:122
  29.1 22.2 %collective-permute-start.10 = (f32[32,4096]{1,0:T(8,128)S(1)}, f32[32,4096]{1,0:T(8,128)S(1)}, u32[]{:S(2)}, u32[]{:S(2)}) collective-permute-start(f32[32,4096]{1,0:T(8,128)S(1)} %pad_maximum_fusion.4), channel_id=1, source_target_pairs={{0,2},{2,4},{4,6},{6,8},{8,10},{10,12},{12,14},{14,0},{1,3},{3,5},... | collective-permute-start | bytes 1572872 | tf_op jit(solution)/shard_map/ppermute | solution.py:122
  29.4 21.9 %collective-permute-start.11 = (f32[32,4096]{1,0:T(8,128)S(1)}, f32[32,4096]{1,0:T(8,128)S(1)}, u32[]{:S(2)}, u32[]{:S(2)}) collective-permute-start(f32[32,4096]{1,0:T(8,128)S(1)} %pad_maximum_fusion.5), channel_id=1, source_target_pairs={{0,14},{2,0},{4,2},{6,4},{8,6},{10,8},{12,10},{14,12},{1,15},{3,1}... | collective-permute-start | bytes 1572872 | tf_op jit(solution)/shard_map/ppermute | solution.py:122
  40.3 22.3 %collective-permute-start.8 = (f32[32,4096]{1,0:T(8,128)S(1)}, f32[32,4096]{1,0:T(8,128)S(1)}, u32[]{:S(2)}, u32[]{:S(2)}) collective-permute-start(f32[32,4096]{1,0:T(8,128)S(1)} %get-tuple-element.55), channel_id=1, source_target_pairs={{0,2},{2,4},{4,6},{6,8},{8,10},{10,12},{12,14},{14,0},{1,3},{3,5},... | collective-permute-start | bytes 1572872 | tf_op jit(solution)/shard_map/ppermute | solution.py:122
  40.4 22.2 %collective-permute-start.9 = (f32[32,4096]{1,0:T(8,128)S(1)}, f32[32,4096]{1,0:T(8,128)S(1)}, u32[]{:S(2)}, u32[]{:S(2)}) collective-permute-start(f32[32,4096]{1,0:T(8,128)S(1)} %get-tuple-element.54), channel_id=1, source_target_pairs={{0,14},{2,0},{4,2},{6,4},{8,6},{10,8},{12,10},{14,12},{1,15},{3,1}... | collective-permute-start | bytes 1572872 | tf_op jit(solution)/shard_map/ppermute | solution.py:122
  51.5 44.9 %copy-start.4 = (f32[1,32,8192]{2,1,0:T(8,128)S(1)}, f32[1,32,8192]{2,1,0:T(8,128)}, u32[]{:S(2)}) copy-start(f32[1,32,8192]{2,1,0:T(8,128)} %param.12) | copy-start | bytes 3145732
  51.5 44.9 %copy-start.5 = (f32[1,32,8192]{2,1,0:T(8,128)S(1)}, f32[1,32,8192]{2,1,0:T(8,128)}, u32[]{:S(2)}) copy-start(f32[1,32,8192]{2,1,0:T(8,128)} %param.11) | copy-start | bytes 3145732
  51.5 44.9 %copy-start.6 = (f32[32,8192]{1,0:T(8,128)S(1)}, f32[32,8192]{1,0:T(8,128)}, u32[]{:S(2)}) copy-start(f32[32,8192]{1,0:T(8,128)} %anchor_ref.1) | copy-start | bytes 3145732
  51.6 44.9 %copy-start.7 = (f32[1,32,8192]{2,1,0:T(8,128)S(1)}, f32[1,32,8192]{2,1,0:T(8,128)}, u32[]{:S(2)}) copy-start(f32[1,32,8192]{2,1,0:T(8,128)} %param.10) | copy-start | bytes 3145732
  51.6 22.2 %collective-permute-start.14 = (f32[32,4096]{1,0:T(8,128)S(1)}, f32[32,4096]{1,0:T(8,128)S(1)}, u32[]{:S(2)}, u32[]{:S(2)}) collective-permute-start(f32[32,4096]{1,0:T(8,128)S(1)} %get-tuple-element.53), channel_id=1, source_target_pairs={{0,2},{2,4},{4,6},{6,8},{8,10},{10,12},{12,14},{14,0},{1,3},{3,5},... | collective-permute-start | bytes 1572872 | tf_op jit(solution)/shard_map/ppermute | solution.py:122
  51.7 22.1 %collective-permute-start.15 = (f32[32,4096]{1,0:T(8,128)S(1)}, f32[32,4096]{1,0:T(8,128)S(1)}, u32[]{:S(2)}, u32[]{:S(2)}) collective-permute-start(f32[32,4096]{1,0:T(8,128)S(1)} %get-tuple-element.52), channel_id=1, source_target_pairs={{0,14},{2,0},{4,2},{6,4},{8,6},{10,8},{12,10},{14,12},{1,15},{3,1}... | collective-permute-start | bytes 1572872 | tf_op jit(solution)/shard_map/ppermute | solution.py:122
  62.7 22.3 %collective-permute-start.12 = (f32[32,4096]{1,0:T(8,128)S(1)}, f32[32,4096]{1,0:T(8,128)S(1)}, u32[]{:S(2)}, u32[]{:S(2)}) collective-permute-start(f32[32,4096]{1,0:T(8,128)S(1)} %get-tuple-element.51), channel_id=1, source_target_pairs={{0,2},{2,4},{4,6},{6,8},{8,10},{10,12},{12,14},{14,0},{1,3},{3,5},... | collective-permute-start | bytes 1572872 | tf_op jit(solution)/shard_map/ppermute | solution.py:122
  62.8 22.2 %collective-permute-start.13 = (f32[32,4096]{1,0:T(8,128)S(1)}, f32[32,4096]{1,0:T(8,128)S(1)}, u32[]{:S(2)}, u32[]{:S(2)}) collective-permute-start(f32[32,4096]{1,0:T(8,128)S(1)} %get-tuple-element.50), channel_id=1, source_target_pairs={{0,14},{2,0},{4,2},{6,4},{8,6},{10,8},{12,10},{14,12},{1,15},{3,1}... | collective-permute-start | bytes 1572872 | tf_op jit(solution)/shard_map/ppermute | solution.py:122
  74.0 22.3 %collective-permute-start.16 = (f32[32,4096]{1,0:T(8,128)S(1)}, f32[32,4096]{1,0:T(8,128)S(1)}, u32[]{:S(2)}, u32[]{:S(2)}) collective-permute-start(f32[32,4096]{1,0:T(8,128)S(1)} %get-tuple-element.49), channel_id=1, source_target_pairs={{0,2},{2,4},{4,6},{6,8},{8,10},{10,12},{12,14},{14,0},{1,3},{3,5},... | collective-permute-start | bytes 1572872 | tf_op jit(solution)/shard_map/ppermute | solution.py:122
  74.1 22.2 %collective-permute-start.17 = (f32[32,4096]{1,0:T(8,128)S(1)}, f32[32,4096]{1,0:T(8,128)S(1)}, u32[]{:S(2)}, u32[]{:S(2)}) collective-permute-start(f32[32,4096]{1,0:T(8,128)S(1)} %get-tuple-element.48), channel_id=1, source_target_pairs={{0,14},{2,0},{4,2},{6,4},{8,6},{10,8},{12,10},{14,12},{1,15},{3,1}... | collective-permute-start | bytes 1572872 | tf_op jit(solution)/shard_map/ppermute | solution.py:122
  97.4 61.0 %copy-start.1 = (bf16[1,512,512]{2,1,0:T(8,128)(2,1)S(1)}, bf16[1,512,512]{2,1,0:T(8,128)(2,1)}, u32[]{:S(2)}) copy-start(bf16[1,512,512]{2,1,0:T(8,128)(2,1)} %param.7) | copy-start | bytes 1572868
  138.6 16.0 %copy-start.3 = (f32[16,32,512]{2,1,0:T(8,128)}, f32[16,32,512]{2,1,0:T(8,128)S(1)}, u32[]{:S(2)}) copy-start(f32[16,32,512]{2,1,0:T(8,128)S(1)} %all_to_all.16.pieces_ref) | copy-start | bytes 3145732
  139.5 15.1 %all-to-all-start.2 = ((f32[16,1,128]{2,1,0:T(1,128)}), f32[16,1,128]{2,1,0:T(1,128)S(1)}, u32[]{:S(2)}, u32[]{:S(2)}) async-start(f32[16,1,128]{2,1,0:T(1,128)} %broadcast_in_dim.32), calls=%async_computation.2 | async-start | bytes 16384 | tf_op jit(solution)/shard_map/all_to_all | solution.py:154
  154.7 0.6 copy-start.8

commit v6 on v5

v6 whole, which is shorter than its diff:
```python
import math

import jax
import jax.numpy as jnp
from jax import lax
from jax.experimental import pallas as pl
from jax.experimental.pallas import tpu as pltpu
from jax.sharding import Mesh, PartitionSpec as P

D = 8192
INNER_STEP = 100

beta_first = 0.9
beta_second = 0.95
inner_rate = 0.5
decay_weight = 0.1
outer_rate = 0.7
momentum_coef = 0.9

Y, X, Z, C = 4, 4, 8, 2
ROWS_DEV = 32
PARTS = Z * C
CHUNKS = ((0, D // 2), (D // 2, D // 2))
SHARES = ((0, D // 4), (D // 4, 3 * D // 4))
STEPS = (4, 3, 5, 2, 6, 1, 7, 0)
UP = [(i, (i + 1) % Z) for i in range(Z)]
DOWN = [(i, (i - 1) % Z) for i in range(Z)]
SWAP = [(0, 1), (1, 0)]


def reorder_rows(activations, z, c):
    rows = Z * C * ROWS_DEV
    place = lax.broadcasted_iota(jnp.int32, (rows, rows), 1)
    source = lax.broadcasted_iota(jnp.int32, (rows, rows), 0)
    block = place // ROWS_DEV
    mine = jnp.where(block < 2, block == 1, block >= 2 + (Z - 1))
    slot = jnp.where(block < 2, 0, jnp.where(block < Z + 1, block - 1, block - Z))
    step = jnp.zeros_like(slot)
    for at, distance in enumerate(STEPS):
        step = jnp.where(slot == at, distance, step)
    core = jnp.where(mine, c, 1 - c)
    wanted = (((z + step) % Z) * C + core) * ROWS_DEV + place % ROWS_DEV
    pick = (wanted == source).astype(activations.dtype)
    return lax.dot_general(
        pick, activations, (((0,), (1,)), ((), ())), preferred_element_type=jnp.float32
    ).astype(activations.dtype)


def finish_kernel(squares_ref, pieces_ref, anchor_ref, momentum_ref, momentum_out, anchor_out):
    squares = jnp.sum(jnp.sum(squares_ref[...], axis=0), keepdims=True)
    ceiling = 0.3 * math.sqrt(ROWS_DEV * PARTS * D)
    factor = ceiling / jnp.maximum(jnp.sqrt(squares), ceiling)
    replicas = pieces_ref.shape[0]
    for p in range(replicas):
        lane = 0
        for lo, width in SHARES:
            piece = width // replicas
            at = slice(lo + p * piece, lo + (p + 1) * piece)
            scaled = factor * pieces_ref[p, :, lane : lane + piece]
            momentum = momentum_coef * momentum_ref[:, at] + scaled
            momentum_out[:, at] = momentum
            anchor_out[:, at] = anchor_ref[:, at] - outer_rate * (scaled + momentum_coef * momentum)
            lane += piece


def finish(squares, pieces, anchor, outer_momentum):
    replicas, rows, share = pieces.shape
    block = 8
    part = pl.BlockSpec((block, D), lambda r: (r, 0))
    shape = jax.ShapeDtypeStruct(anchor.shape, jnp.float32)
    return pl.pallas_call(
        finish_kernel,
        grid=(rows // block,),
        in_specs=[
            pl.BlockSpec(squares.shape, lambda r: (0, 0, 0)),
            pl.BlockSpec((replicas, block, share), lambda r: (0, r, 0)),
            part,
            part,
        ],
        out_specs=[part, part],
        out_shape=[shape, shape],
        cost_estimate=pl.CostEstimate(flops=7 * anchor.size, bytes_accessed=20 * anchor.size, transcendentals=0),
    )(squares, pieces, anchor, outer_momentum)


def per_device(hidden_acts, out_grads, anchor, drift, adam_first, adam_second, outer_momentum):
    z = lax.axis_index("z")
    c = lax.axis_index("c")
    ordered = reorder_rows(hidden_acts[0], z, c)
    cotangent = out_grads[0]
    near = 2 * ROWS_DEV
    stay = near + (Z - 1) * ROWS_DEV

    def product(lhs, rhs):
        return lax.dot_general(lhs, rhs, (((1,), (0,)), ((), ())), preferred_element_type=jnp.float32)

    def after(values, *tokens):
        return lax.optimization_barrier((values, tokens))[0]

    chunks = range(len(CHUNKS))
    up = [None] * len(CHUNKS)
    down = [None] * len(CHUNKS)

    def own(k, distance, lo=0, hi=None):
        at = (STEPS.index(distance) - 1) * ROWS_DEV
        base, width = CHUNKS[k]
        hi = width if hi is None else hi
        return kept[k][at : at + ROWS_DEV, lo:hi] + rest[at : at + ROWS_DEV, base + lo : base + hi]

    first = product(ordered[:near], cotangent)
    theirs = lax.optimization_barrier(first[:ROWS_DEV])
    got = lax.ppermute(theirs, "c", SWAP)
    sent = product(after(ordered[near:stay], theirs), cotangent)
    rest = lax.ppermute(after(sent, got), "c", SWAP)
    first = first[ROWS_DEV:] + got
    for k, (lo, width) in enumerate(CHUNKS):
        up[k] = first[:, lo + width // 2 : lo + width]
        down[k] = first[:, lo : lo + width // 2]
        first = after(first, up[k], down[k])
    last = (up[-1], down[-1])
    lhs = after(ordered[stay:], sent, last)
    kept = [product(lhs, cotangent[:, lo : lo + width]) for lo, width in CHUNKS]
    for t in range(1, 4):
        for k in chunks:
            moved = (lax.ppermute(up[k], "z", UP), lax.ppermute(down[k], "z", DOWN))
            u, d = after(moved, last)
            if t == 1:
                half = CHUNKS[k][1] // 2
                up[k] = jnp.concatenate([own(k, 3, 0, half), own(k, 3, half) + u], axis=1)
                down[k] = jnp.concatenate([own(k, 5, 0, half) + d, own(k, 5, half)], axis=1)
            else:
                up[k] = own(k, 4 - t) + u
                down[k] = own(k, 4 + t) + d
            last = (up[k], down[k])

    correction_one = 1.0 - beta_first**INNER_STEP
    correction_two = 1.0 - beta_second**INNER_STEP
    replicas = Y * X

    def moments(first_old, second_old, gradient):
        moment_one = beta_first * first_old + (1.0 - beta_first) * gradient
        moment_two = beta_second * second_old + (1.0 - beta_second) * gradient * gradient
        return moment_one, moment_two

    def pseudo_of(lo, width, gradient):
        at = slice(lo, lo + width)
        own_drift = drift[0, :, at]
        moment_one, moment_two = moments(adam_first[0, :, at], adam_second[0, :, at], gradient)
        update = moment_one / correction_one / (
            jnp.sqrt(moment_two / correction_two) + 1e-08
        ) + decay_weight * (anchor[:, at] + own_drift)
        pseudo = inner_rate * update - own_drift
        return pseudo.reshape(ROWS_DEV, replicas, width // replicas).transpose(1, 0, 2)

    def exchange(shares, axes=("y", "x")):
        return lax.all_to_all(shares, axes, split_axis=0, concat_axis=0, tiled=True)

    def finished(k, *tokens):
        moved = (lax.ppermute(up[k], "z", UP), lax.ppermute(down[k], "z", DOWN))
        u, d = after(moved, *tokens)
        return own(k, 0) + u + d

    half = finished(0, last)
    (_, early), (lo, late) = SHARES
    last = pseudo_of(0, early, half[:, :early])
    met = [exchange(last)]
    gradient = jnp.concatenate([half, finished(1, last, met)], axis=1)
    last = pseudo_of(lo, late, gradient[:, lo:])
    met.append(exchange(last))
    part = jnp.concatenate([jnp.sum(after(m, last), axis=0) / replicas for m in met], axis=1)
    pieces = exchange(jnp.broadcast_to(part[None], (replicas,) + part.shape))
    moment_one, moment_two = moments(adam_first[0], adam_second[0], gradient)
    squares = jnp.sum(jnp.sum(pieces * pieces, axis=(0, 1)).reshape(-1, 128), axis=0)
    squares = exchange(jnp.broadcast_to(squares, (PARTS, 1, 128)), ("z", "c"))
    momentum, updated = finish(squares, pieces, anchor, outer_momentum)
    return (moment_one[None], moment_two[None], momentum, updated)


def solution(mesh):
    devices = mesh.devices.reshape(Y, X, Z, C)
    grid = Mesh(devices, ("y", "x", "z", "c"))
    rep, fsdp = ("y", "x"), ("z", "c")
    return jax.shard_map(
        per_device,
        mesh=grid,
        in_specs=(
            P(rep, fsdp, None),
            P(rep, fsdp, None),
            P(fsdp, None),
            P(rep, fsdp, None),
            P(rep, fsdp, None),
            P(rep, fsdp, None),
            P(fsdp, None),
        ),
        out_specs=(
            P(rep, fsdp, None),
            P(rep, fsdp, None),
            P(fsdp, None),
            P(fsdp, None),
        ),
        check_vma=False,
    )
```

time: 159 us -> 160 us (level)
  blocking collectives: 41 us -> 16.9 us
  starting transfers between devices: 36.6 us -> 47.2 us
  waiting for transfers between devices: 58.8 us -> 66.1 us
  other arithmetic: 5.81 us -> 11.4 us
    all_to_all x2 -> x1, blocking collectives: 41 us -> 16.9 us  [exchange(): return lax.all_to_all(shares, axes, split_axis=0, concat_axis=0, tiled=True)]
    ppermute x16 -> x12, waiting for transfers between devices: 54.2 us -> 34.8 us  [per_device(): moved = (lax.ppermute(up[k], 'z', UP), lax.ppermute(down[k], 'z', DOWN))]
    all_to_all x1 -> x3, waiting for transfers between devices: 3.79 us -> 20.8 us  [exchange(): return lax.all_to_all(shares, axes, split_axis=0, concat_axis=0, tiled=True)]
    all_to_all x1 -> x3, starting transfers between devices: 8.2 us -> 18.9 us  [exchange(): return lax.all_to_all(shares, axes, split_axis=0, concat_axis=0, tiled=True)]
    ppermute x0 -> x4, waiting for transfers between devices: none -> 9.67 us  [finished(): moved = (lax.ppermute(up[k], 'z', UP), lax.ppermute(down[k], 'z', DOWN))]
    ppermute x16 -> x12, starting transfers between devices: 24.7 us -> 19.2 us  [per_device(): moved = (lax.ppermute(up[k], 'z', UP), lax.ppermute(down[k], 'z', DOWN))]
    ppermute x0 -> x4, starting transfers between devices: none -> 5.42 us  [finished(): moved = (lax.ppermute(up[k], 'z', UP), lax.ppermute(down[k], 'z', DOWN))]
    transpose x0 -> x1, other arithmetic: none -> 2.03 us  [pseudo_of(): pseudo.reshape(ROWS_DEV, replicas, width // replicas).transpose(1, 0, 2)]
  transfers between devices with their start and end apart: 19 -> 21, of which waited for: 11 -> 13; matrix products, arithmetic and copies ran while one was open for 6% -> 8% of each run, Pallas kernels for 0% -> 0%
where the time goes in v6:
time: 160 us
  waiting for transfers between devices  66.1 us (41%)
  starting transfers between devices  47.2 us (30%)
  blocking collectives  16.9 us (11%)
  other arithmetic  11.4 us (7%)
  local copies, waits for them, and re-layouts  6.49 us (4%)
  matrix products  6.46 us (4%)
  Pallas kernels  4.28 us (3%)
    ppermute x12, waiting for transfers between devices, per_device(): moved = (lax.ppermute(up[k], 'z', UP), lax.ppermute(down[k], 'z', DOWN))  34.8 us
    all_to_all x3, waiting for transfers between devices, exchange(): return lax.all_to_all(shares, axes, split_axis=0, concat_axis=0, tiled=True)  20.8 us
    ppermute x12, starting transfers between devices, per_device(): moved = (lax.ppermute(up[k], 'z', UP), lax.ppermute(down[k], 'z', DOWN))  19.2 us
    all_to_all x3, starting transfers between devices, exchange(): return lax.all_to_all(shares, axes, split_axis=0, concat_axis=0, tiled=True)  18.9 us
    all_to_all x1, blocking collectives, exchange(): return lax.all_to_all(shares, axes, split_axis=0, concat_axis=0, tiled=True)  16.9 us
    ppermute x4, waiting for transfers between devices, finished(): moved = (lax.ppermute(up[k], 'z', UP), lax.ppermute(down[k], 'z', DOWN))  9.67 us
    dot_general x4, matrix products, product(): lax.dot_general(lhs, rhs, (((1,), (0,)), ((), ())), preferred_element_typ...  5.95 us
    ppermute x4, starting transfers between devices, finished(): moved = (lax.ppermute(up[k], 'z', UP), lax.ppermute(down[k], 'z', DOWN))  5.42 us
  transfers between devices with their start and end apart: 21, of which 13 were waited for; matrix products, arithmetic and copies ran while one was open for 8% of the time, Pallas kernels for 0%

profile of v6, /device:TPU:1, one launch (start us, length us, event | category | flops | bytes accessed | tf_op | source)
XLA Modules:
  0.0 159.8 jit_solution(11515410810991873049)
XLA Ops:
  0.7 1.0 copy-done
  1.7 0.5 convolution_convert_fusion
  2.2 2.9 %copy-done.2 = bf16[1,512,8192]{2,1,0:T(8,128)(2,1)S(1)} copy-done((bf16[1,512,8192]{2,1,0:T(8,128)(2,1)S(1)}, bf16[1,512,8192]{2,1,0:T(8,128)(2,1)}, u32[]{:S(2)}) %copy-start.2) | copy-done | bytes 8388632
  5.1 1.6 %fusion.72 = f32[64,8192]{1,0:T(8,128)S(1)} fusion(bf16[512,512]{1,0:T(8,128)(2,1)S(1)} %convolution_convert_fusion, bf16[1,512,8192]{2,1,0:T(8,128)(2,1)S(1)} %copy-done.2), kind=kOutput, calls=%fused_computation.119 | convolution fusion | flops 536870912 | bytes 10551296 | tf_op jit(solution)/shard_map/dot_general | solution.py:95
  6.8 3.3 %collective-permute-start = (f32[32,8192]{1,0:T(8,128)S(1)}, f32[32,8192]{1,0:T(8,128)S(1)}, u32[]{:S(2)}, u32[]{:S(2)}) collective-permute-start(f32[32,8192]{1,0:T(8,128)S(1)} %slice.231), channel_id=1, source_target_pairs={{0,1},{1,0},{2,3},{3,2},{4,5},{5,4},{6,7},{7,6},{8,9},{9,8},{10,11... | collective-permute-start | bytes 3145736 | tf_op jit(solution)/shard_map/ppermute | solution.py:112
  10.1 2.1 %fusion.80 = f32[224,8192]{1,0:T(8,128)S(1)} fusion(bf16[224,512]{1,0:T(8,128)(2,1)S(1)} %get-tuple-element.28, bf16[1,512,8192]{2,1,0:T(8,128)(2,1)S(1)} %copy-done.2), kind=kOutput, calls=%fused_computation.135 | convolution fusion | flops 1879048192 | bytes 15958016 | tf_op jit(solution)/shard_map/dot_general | solution.py:95
  12.2 0.2 collective-permute-done
  12.4 0.4 collective-permute-start.1
  13.0 3.9 %collective-permute-start.3 = (f32[32,2048]{1,0:T(8,128)S(1)}, f32[32,2048]{1,0:T(8,128)S(1)}, u32[]{:S(2)}, u32[]{:S(2)}) collective-permute-start(f32[32,2048]{1,0:T(8,128)S(1)} %get-tuple-element.72), channel_id=1, source_target_pairs={{0,14},{2,0},{4,2},{6,4},{8,6},{10,8},{12,10},{14,12},{1,15},{3,1}... | collective-permute-start | bytes 786440 | tf_op jit(solution)/shard_map/ppermute | solution.py:125
  17.1 2.7 %collective-permute-start.7 = (f32[32,2048]{1,0:T(8,128)S(1)}, f32[32,2048]{1,0:T(8,128)S(1)}, u32[]{:S(2)}, u32[]{:S(2)}) collective-permute-start(f32[32,2048]{1,0:T(8,128)S(1)} %get-tuple-element.70), channel_id=1, source_target_pairs={{0,14},{2,0},{4,2},{6,4},{8,6},{10,8},{12,10},{14,12},{1,15},{3,1}... | collective-permute-start | bytes 786440 | tf_op jit(solution)/shard_map/ppermute | solution.py:125
  19.7 1.1 fusion.2
  20.8 1.1 fusion
  22.0 1.4 collective-permute-done.2
  23.4 0.7 collective-permute-done.1
  24.1 0.1 fusion.67
  24.4 3.9 %collective-permute-start.5 = (f32[32,4096]{1,0:T(8,128)S(1)}, f32[32,4096]{1,0:T(8,128)S(1)}, u32[]{:S(2)}, u32[]{:S(2)}) collective-permute-start(f32[32,4096]{1,0:T(8,128)S(1)} %pad_maximum_fusion.3), channel_id=1, source_target_pairs={{0,14},{2,0},{4,2},{6,4},{8,6},{10,8},{12,10},{14,12},{1,15},{3,1}... | collective-permute-start | bytes 1572872 | tf_op jit(solution)/shard_map/ppermute | solution.py:125
  28.3 0.7 collective-permute-done.6
  29.2 0.3 collective-permute-start.10
  29.5 2.7 %collective-permute-start.11 = (f32[32,4096]{1,0:T(8,128)S(1)}, f32[32,4096]{1,0:T(8,128)S(1)}, u32[]{:S(2)}, u32[]{:S(2)}) collective-permute-start(f32[32,4096]{1,0:T(8,128)S(1)} %pad_maximum_fusion.5), channel_id=1, source_target_pairs={{0,14},{2,0},{4,2},{6,4},{8,6},{10,8},{12,10},{14,12},{1,15},{3,1}... | collective-permute-start | bytes 1572872 | tf_op jit(solution)/shard_map/ppermute | solution.py:125
  32.2 7.9 %collective-permute-done.4 = f32[32,4096]{1,0:T(8,128)S(1)} collective-permute-done((f32[32,4096]{1,0:T(8,128)S(1)}, f32[32,4096]{1,0:T(8,128)S(1)}, u32[]{:S(2)}, u32[]{:S(2)}) %collective-permute-start.4) | collective-permute-done | bytes 524320 | tf_op jit(solution)/shard_map/ppermute | solution.py:125
  40.2 0.2 fusion.31
  40.5 2.7 %collective-permute-start.9 = (f32[32,4096]{1,0:T(8,128)S(1)}, f32[32,4096]{1,0:T(8,128)S(1)}, u32[]{:S(2)}, u32[]{:S(2)}) collective-permute-start(f32[32,4096]{1,0:T(8,128)S(1)} %get-tuple-element.58), channel_id=1, source_target_pairs={{0,14},{2,0},{4,2},{6,4},{8,6},{10,8},{12,10},{14,12},{1,15},{3,1}... | collective-permute-start | bytes 1572872 | tf_op jit(solution)/shard_map/ppermute | solution.py:125
  43.1 8.3 %collective-permute-done.10 = f32[32,4096]{1,0:T(8,128)S(1)} collective-permute-done((f32[32,4096]{1,0:T(8,128)S(1)}, f32[32,4096]{1,0:T(8,128)S(1)}, u32[]{:S(2)}, u32[]{:S(2)}) %collective-permute-start.10) | collective-permute-done | bytes 524320 | tf_op jit(solution)/shard_map/ppermute | solution.py:125
  51.4 0.2 fusion.29
  51.7 2.7 %collective-permute-start.15 = (f32[32,4096]{1,0:T(8,128)S(1)}, f32[32,4096]{1,0:T(8,128)S(1)}, u32[]{:S(2)}, u32[]{:S(2)}) collective-permute-start(f32[32,4096]{1,0:T(8,128)S(1)} %get-tuple-element.56), channel_id=1, source_target_pairs={{0,14},{2,0},{4,2},{6,4},{8,6},{10,8},{12,10},{14,12},{1,15},{3,1}... | collective-permute-start | bytes 1572872 | tf_op jit(solution)/shard_map/ppermute | solution.py:125
  54.3 8.3 %collective-permute-done.8 = f32[32,4096]{1,0:T(8,128)S(1)} collective-permute-done((f32[32,4096]{1,0:T(8,128)S(1)}, f32[32,4096]{1,0:T(8,128)S(1)}, u32[]{:S(2)}, u32[]{:S(2)}) %collective-permute-start.8) | collective-permute-done | bytes 524320 | tf_op jit(solution)/shard_map/ppermute | solution.py:125
  62.6 0.2 fusion.28
  62.9 2.7 %collective-permute-start.13 = (f32[32,4096]{1,0:T(8,128)S(1)}, f32[32,4096]{1,0:T(8,128)S(1)}, u32[]{:S(2)}, u32[]{:S(2)}) collective-permute-start(f32[32,4096]{1,0:T(8,128)S(1)} %get-tuple-element.54), channel_id=1, source_target_pairs={{0,14},{2,0},{4,2},{6,4},{8,6},{10,8},{12,10},{14,12},{1,15},{3,1}... | collective-permute-start | bytes 1572872 | tf_op jit(solution)/shard_map/ppermute | solution.py:159
  65.6 8.3 %collective-permute-done.14 = f32[32,4096]{1,0:T(8,128)S(1)} collective-permute-done((f32[32,4096]{1,0:T(8,128)S(1)}, f32[32,4096]{1,0:T(8,128)S(1)}, u32[]{:S(2)}, u32[]{:S(2)}) %collective-permute-start.14) | collective-permute-done | bytes 524320 | tf_op jit(solution)/shard_map/ppermute | solution.py:125
  73.9 1.2 fusion.26
  75.0 2.7 %collective-permute-start.17 = (f32[32,4096]{1,0:T(8,128)}, f32[32,4096]{1,0:T(8,128)S(1)}, u32[]{:S(2)}, u32[]{:S(2)}) collective-permute-start(f32[32,4096]{1,0:T(8,128)} %get-tuple-element.52), channel_id=1, source_target_pairs={{0,14},{2,0},{4,2},{6,4},{8,6},{10,8},{12,10},{14,12},{1,15},{3,1}... | collective-permute-start | bytes 1572872 | tf_op jit(solution)/shard_map/ppermute | solution.py:159
  77.7 7.4 %collective-permute-done.12 = f32[32,4096]{1,0:T(8,128)S(1)} collective-permute-done((f32[32,4096]{1,0:T(8,128)S(1)}, f32[32,4096]{1,0:T(8,128)S(1)}, u32[]{:S(2)}, u32[]{:S(2)}) %collective-permute-start.12) | collective-permute-done | bytes 524320 | tf_op jit(solution)/shard_map/ppermute | solution.py:159
  85.2 2.0 %bitcast_bitcast_fusion.1 = f32[16,32,128]{2,1,0:T(8,128)} fusion(f32[32,8192]{1,0:T(8,128)} %anchor_ref.1, f32[1,32,8192]{2,1,0:T(8,128)} %param.10, f32[1,32,8192]{2,1,0:T(8,128)S(1)} %copy-done.6, f32[32,4096]{1,0:T(8,128)S(1)} %fusion.35, f32[1,32,8192]{2,1,0:T(8,128)} %param.11), kind=kLoop, calls=%fused_computation.100 | loop fusion | flops 1048576 | bytes 1572864 | tf_op jit(solution)/shard_map/transpose | solution.py:153
  87.3 6.8 %all-to-all-start = ((f32[16,32,128]{2,1,0:T(8,128)}), f32[16,32,128]{2,1,0:T(8,128)S(1)}, u32[]{:S(2)}, u32[]{:S(2)}) async-start(f32[16,32,128]{2,1,0:T(8,128)} %bitcast_bitcast_fusion.1), calls=%async_computation | async-start | bytes 524288 | tf_op jit(solution)/shard_map/all_to_all | solution.py:156
  94.0 2.3 %collective-permute-done.16 = f32[32,4096]{1,0:T(8,128)S(1)} collective-permute-done((f32[32,4096]{1,0:T(8,128)}, f32[32,4096]{1,0:T(8,128)S(1)}, u32[]{:S(2)}, u32[]{:S(2)}) %collective-permute-start.16) | collective-permute-done | bytes 524320 | tf_op jit(solution)/shard_map/ppermute | solution.py:159
  96.3 5.3 %all-to-all-done = f32[16,32,128]{2,1,0:T(8,128)S(1)} async-done(((f32[16,32,128]{2,1,0:T(8,128)}), f32[16,32,128]{2,1,0:T(8,128)S(1)}, u32[]{:S(2)}, u32[]{:S(2)}) %all-to-all-start) | async-done | bytes 262176 | tf_op jit(solution)/shard_map/all_to_all | solution.py:156
  101.7 1.3 fusion.25
  103.0 2.2 %bitcast_subtract_fusion = f32[32,6144]{1,0:T(8,128)S(1)} fusion(f32[32,8192]{1,0:T(8,128)} %anchor_ref.1, f32[1,32,8192]{2,1,0:T(8,128)} %param.10, f32[1,32,8192]{2,1,0:T(8,128)S(1)} %copy-done.6, f32[32,4096]{1,0:T(8,128)S(1)} %fusion.25, f32[32,4096]{1,0:T(8,128)S(1)} %fusion.35, f32[1,32,8192]{2,1,0:T(8,128)} %param.11), kind=kLoop, calls=%fused_computation.39 | loop fusion | flops 3342336 | bytes 4980736 | tf_op jit(solution)/shard_map/sub | solution.py:152
  105.2 1.0 copy.19
  106.2 3.6 %all-to-all-start.1 = ((f32[16,32,384]{2,1,0:T(8,128)}), f32[16,32,384]{2,1,0:T(8,128)S(1)}, u32[]{:S(2)}, u32[]{:S(2)}) async-start(f32[16,32,384]{2,1,0:T(8,128)} %bitcast.75), calls=%async_computation.1 | async-start | bytes 1572864 | tf_op jit(solution)/shard_map/all_to_all | solution.py:156
  109.8 11.7 %all-to-all-done.1 = f32[16,32,384]{2,1,0:T(8,128)S(1)} async-done(((f32[16,32,384]{2,1,0:T(8,128)}), f32[16,32,384]{2,1,0:T(8,128)S(1)}, u32[]{:S(2)}, u32[]{:S(2)}) %all-to-all-start.1) | async-done | bytes 786464 | tf_op jit(solution)/shard_map/all_to_all | solution.py:156
  121.7 16.9 %all_to_all.20.pieces_ref = f32[16,32,512]{2,1,0:T(8,128)S(1)} all-to-all(f32[16,32,512]{2,1,0:T(8,128)S(1)} %broadcast_in_dim.31), channel_id=1, replica_groups=mesh['y'=4,'x'=4,'z'=8,'c'=2] {'y','x'}, dimensions={0} | all-to-all | bytes 2097152 | tf_op jit(solution)/shard_map/all_to_all | solution.py:156
  138.7 0.8 broadcast_in_dim.32
  139.5 8.5 %all-to-all-start.3 = ((f32[16,1,128]{2,1,0:T(1,128)}), f32[16,1,128]{2,1,0:T(1,128)S(1)}, u32[]{:S(2)}, u32[]{:S(2)}) async-start(f32[16,1,128]{2,1,0:T(1,128)} %broadcast_in_dim.32), calls=%async_computation.3 | async-start | bytes 16384 | tf_op jit(solution)/shard_map/all_to_all | solution.py:156
  148.0 3.2 %fusion.12 = (f32[1,32,8192]{2,1,0:T(8,128)}, f32[1,32,8192]{2,1,0:T(8,128)}) fusion(f32[1,32,8192]{2,1,0:T(8,128)} %param.12, f32[1,32,4096]{2,1,0:T(8,128)S(1)} %bitcast.79, f32[1,32,4096]{2,1,0:T(8,128)S(1)} %bitcast.78, f32[1,32,8192]{2,1,0:T(8,128)} %param.11), kind=kLoop, calls=%fused_computation.24 | loop fusion | flops 2097152 | bytes 5242880 | tf_op jit(solution)/shard_map/add | solution.py:142
  151.1 3.8 %all-to-all-done.3.squares_ref = f32[16,1,128]{2,1,0:T(1,128)S(1)} async-done(((f32[16,1,128]{2,1,0:T(1,128)}), f32[16,1,128]{2,1,0:T(1,128)S(1)}, u32[]{:S(2)}, u32[]{:S(2)}) %all-to-all-start.3) | async-done | bytes 8224 | tf_op jit(solution)/shard_map/all_to_all | solution.py:156
  154.9 0.6 copy-done.7
  155.5 4.3 %shard_map.102 = (f32[32,8192]{1,0:T(8,128)}, f32[32,8192]{1,0:T(8,128)}) custom-call(f32[16,1,128]{2,1,0:T(1,128)} %copy-done.7, f32[16,32,512]{2,1,0:T(8,128)} %copy-done.4, f32[32,8192]{1,0:T(8,128)} %anchor_ref.1, f32[32,8192]{1,0:T(8,128)} %momentum_ref.1), custom_call_target="tpu_custom_call" | custom-call | flops 1835008 | bytes 5242880 | tf_op jit(solution)/shard_map/pallas_call | solution.py:71
  (50 shorter events, 1.6 us)
Async XLA Ops:
  0.6 1.1 copy-start
  1.7 3.4 %copy-start.2 = (bf16[1,512,8192]{2,1,0:T(8,128)(2,1)S(1)}, bf16[1,512,8192]{2,1,0:T(8,128)(2,1)}, u32[]{:S(2)}) copy-start(bf16[1,512,8192]{2,1,0:T(8,128)(2,1)} %param.8) | copy-start | bytes 25165828
  6.8 5.6 %collective-permute-start = (f32[32,8192]{1,0:T(8,128)S(1)}, f32[32,8192]{1,0:T(8,128)S(1)}, u32[]{:S(2)}, u32[]{:S(2)}) collective-permute-start(f32[32,8192]{1,0:T(8,128)S(1)} %slice.231), channel_id=1, source_target_pairs={{0,1},{1,0},{2,3},{3,2},{4,5},{5,4},{6,7},{7,6},{8,9},{9,8},{10,11... | collective-permute-start | bytes 3145736 | tf_op jit(solution)/shard_map/ppermute | solution.py:112
  12.4 11.7 %collective-permute-start.1 = (f32[224,8192]{1,0:T(8,128)S(1)}, f32[224,8192]{1,0:T(8,128)S(1)}, u32[]{:S(2)}, u32[]{:S(2)}) collective-permute-start(f32[224,8192]{1,0:T(8,128)S(1)} %fusion.80), channel_id=1, source_target_pairs={{0,1},{1,0},{2,3},{3,2},{4,5},{5,4},{6,7},{7,6},{8,9},{9,8},{10,11... | collective-permute-start | bytes 22020104 | tf_op jit(solution)/shard_map/ppermute | solution.py:114
  12.9 10.5 %collective-permute-start.2 = (f32[32,2048]{1,0:T(8,128)S(1)}, f32[32,2048]{1,0:T(8,128)S(1)}, u32[]{:S(2)}, u32[]{:S(2)}) collective-permute-start(f32[32,2048]{1,0:T(8,128)S(1)} %get-tuple-element.73), channel_id=1, source_target_pairs={{0,2},{2,4},{4,6},{6,8},{8,10},{10,12},{12,14},{14,0},{1,3},{3,5},... | collective-permute-start | bytes 786440 | tf_op jit(solution)/shard_map/ppermute | solution.py:125
  13.0 10.4 %collective-permute-start.3 = (f32[32,2048]{1,0:T(8,128)S(1)}, f32[32,2048]{1,0:T(8,128)S(1)}, u32[]{:S(2)}, u32[]{:S(2)}) collective-permute-start(f32[32,2048]{1,0:T(8,128)S(1)} %get-tuple-element.72), channel_id=1, source_target_pairs={{0,14},{2,0},{4,2},{6,4},{8,6},{10,8},{12,10},{14,12},{1,15},{3,1}... | collective-permute-start | bytes 786440 | tf_op jit(solution)/shard_map/ppermute | solution.py:125
  17.0 12.0 %collective-permute-start.6 = (f32[32,2048]{1,0:T(8,128)S(1)}, f32[32,2048]{1,0:T(8,128)S(1)}, u32[]{:S(2)}, u32[]{:S(2)}) collective-permute-start(f32[32,2048]{1,0:T(8,128)S(1)} %get-tuple-element.71), channel_id=1, source_target_pairs={{0,2},{2,4},{4,6},{6,8},{8,10},{10,12},{12,14},{14,0},{1,3},{3,5},... | collective-permute-start | bytes 786440 | tf_op jit(solution)/shard_map/ppermute | solution.py:125
  17.1 11.9 %collective-permute-start.7 = (f32[32,2048]{1,0:T(8,128)S(1)}, f32[32,2048]{1,0:T(8,128)S(1)}, u32[]{:S(2)}, u32[]{:S(2)}) collective-permute-start(f32[32,2048]{1,0:T(8,128)S(1)} %get-tuple-element.70), channel_id=1, source_target_pairs={{0,14},{2,0},{4,2},{6,4},{8,6},{10,8},{12,10},{14,12},{1,15},{3,1}... | collective-permute-start | bytes 786440 | tf_op jit(solution)/shard_map/ppermute | solution.py:125
  22.0 51.9 %copy-start.3 = (f32[224,4096]{1,0:T(8,128)}, f32[224,4096]{1,0:T(8,128)S(1)}, u32[]{:S(2)}) copy-start(f32[224,4096]{1,0:T(8,128)S(1)} %fusion) | copy-start | bytes 11010052
  24.1 61.0 %copy-start.5 = (f32[224,8192]{1,0:T(8,128)}, f32[224,8192]{1,0:T(8,128)S(1)}, u32[]{:S(2)}) copy-start(f32[224,8192]{1,0:T(8,128)S(1)} %collective-permute-done.1) | copy-start | bytes 22020100
  24.2 15.9 %collective-permute-start.4 = (f32[32,4096]{1,0:T(8,128)S(1)}, f32[32,4096]{1,0:T(8,128)S(1)}, u32[]{:S(2)}, u32[]{:S(2)}) collective-permute-start(f32[32,4096]{1,0:T(8,128)S(1)} %pad_maximum_fusion.2), channel_id=1, source_target_pairs={{0,2},{2,4},{4,6},{6,8},{8,10},{10,12},{12,14},{14,0},{1,3},{3,5},... | collective-permute-start | bytes 1572872 | tf_op jit(solution)/shard_map/ppermute | solution.py:125
  24.4 15.8 %collective-permute-start.5 = (f32[32,4096]{1,0:T(8,128)S(1)}, f32[32,4096]{1,0:T(8,128)S(1)}, u32[]{:S(2)}, u32[]{:S(2)}) collective-permute-start(f32[32,4096]{1,0:T(8,128)S(1)} %pad_maximum_fusion.3), channel_id=1, source_target_pairs={{0,14},{2,0},{4,2},{6,4},{8,6},{10,8},{12,10},{14,12},{1,15},{3,1}... | collective-permute-start | bytes 1572872 | tf_op jit(solution)/shard_map/ppermute | solution.py:125
  29.2 22.2 %collective-permute-start.10 = (f32[32,4096]{1,0:T(8,128)S(1)}, f32[32,4096]{1,0:T(8,128)S(1)}, u32[]{:S(2)}, u32[]{:S(2)}) collective-permute-start(f32[32,4096]{1,0:T(8,128)S(1)} %pad_maximum_fusion.4), channel_id=1, source_target_pairs={{0,2},{2,4},{4,6},{6,8},{8,10},{10,12},{12,14},{14,0},{1,3},{3,5},... | collective-permute-start | bytes 1572872 | tf_op jit(solution)/shard_map/ppermute | solution.py:125
  29.5 21.9 %collective-permute-start.11 = (f32[32,4096]{1,0:T(8,128)S(1)}, f32[32,4096]{1,0:T(8,128)S(1)}, u32[]{:S(2)}, u32[]{:S(2)}) collective-permute-start(f32[32,4096]{1,0:T(8,128)S(1)} %pad_maximum_fusion.5), channel_id=1, source_target_pairs={{0,14},{2,0},{4,2},{6,4},{8,6},{10,8},{12,10},{14,12},{1,15},{3,1}... | collective-permute-start | bytes 1572872 | tf_op jit(solution)/shard_map/ppermute | solution.py:125
  40.4 22.3 %collective-permute-start.8 = (f32[32,4096]{1,0:T(8,128)S(1)}, f32[32,4096]{1,0:T(8,128)S(1)}, u32[]{:S(2)}, u32[]{:S(2)}) collective-permute-start(f32[32,4096]{1,0:T(8,128)S(1)} %get-tuple-element.59), channel_id=1, source_target_pairs={{0,2},{2,4},{4,6},{6,8},{8,10},{10,12},{12,14},{14,0},{1,3},{3,5},... | collective-permute-start | bytes 1572872 | tf_op jit(solution)/shard_map/ppermute | solution.py:125
  40.5 44.8 %copy-start.6 = (f32[1,32,8192]{2,1,0:T(8,128)S(1)}, f32[1,32,8192]{2,1,0:T(8,128)}, u32[]{:S(2)}) copy-start(f32[1,32,8192]{2,1,0:T(8,128)} %param.12) | copy-start | bytes 3145732
  40.5 22.2 %collective-permute-start.9 = (f32[32,4096]{1,0:T(8,128)S(1)}, f32[32,4096]{1,0:T(8,128)S(1)}, u32[]{:S(2)}, u32[]{:S(2)}) collective-permute-start(f32[32,4096]{1,0:T(8,128)S(1)} %get-tuple-element.58), channel_id=1, source_target_pairs={{0,14},{2,0},{4,2},{6,4},{8,6},{10,8},{12,10},{14,12},{1,15},{3,1}... | collective-permute-start | bytes 1572872 | tf_op jit(solution)/shard_map/ppermute | solution.py:125
  51.6 22.3 %collective-permute-start.14 = (f32[32,4096]{1,0:T(8,128)S(1)}, f32[32,4096]{1,0:T(8,128)S(1)}, u32[]{:S(2)}, u32[]{:S(2)}) collective-permute-start(f32[32,4096]{1,0:T(8,128)S(1)} %get-tuple-element.57), channel_id=1, source_target_pairs={{0,2},{2,4},{4,6},{6,8},{8,10},{10,12},{12,14},{14,0},{1,3},{3,5},... | collective-permute-start | bytes 1572872 | tf_op jit(solution)/shard_map/ppermute | solution.py:125
  51.7 22.2 %collective-permute-start.15 = (f32[32,4096]{1,0:T(8,128)S(1)}, f32[32,4096]{1,0:T(8,128)S(1)}, u32[]{:S(2)}, u32[]{:S(2)}) collective-permute-start(f32[32,4096]{1,0:T(8,128)S(1)} %get-tuple-element.56), channel_id=1, source_target_pairs={{0,14},{2,0},{4,2},{6,4},{8,6},{10,8},{12,10},{14,12},{1,15},{3,1}... | collective-permute-start | bytes 1572872 | tf_op jit(solution)/shard_map/ppermute | solution.py:125
  62.8 22.3 %collective-permute-start.12 = (f32[32,4096]{1,0:T(8,128)S(1)}, f32[32,4096]{1,0:T(8,128)S(1)}, u32[]{:S(2)}, u32[]{:S(2)}) collective-permute-start(f32[32,4096]{1,0:T(8,128)S(1)} %get-tuple-element.55), channel_id=1, source_target_pairs={{0,2},{2,4},{4,6},{6,8},{8,10},{10,12},{12,14},{14,0},{1,3},{3,5},... | collective-permute-start | bytes 1572872 | tf_op jit(solution)/shard_map/ppermute | solution.py:159
  62.9 22.2 %collective-permute-start.13 = (f32[32,4096]{1,0:T(8,128)S(1)}, f32[32,4096]{1,0:T(8,128)S(1)}, u32[]{:S(2)}, u32[]{:S(2)}) collective-permute-start(f32[32,4096]{1,0:T(8,128)S(1)} %get-tuple-element.54), channel_id=1, source_target_pairs={{0,14},{2,0},{4,2},{6,4},{8,6},{10,8},{12,10},{14,12},{1,15},{3,1}... | collective-permute-start | bytes 1572872 | tf_op jit(solution)/shard_map/ppermute | solution.py:159
  75.0 21.3 %collective-permute-start.16 = (f32[32,4096]{1,0:T(8,128)}, f32[32,4096]{1,0:T(8,128)S(1)}, u32[]{:S(2)}, u32[]{:S(2)}) collective-permute-start(f32[32,4096]{1,0:T(8,128)} %get-tuple-element.53), channel_id=1, source_target_pairs={{0,2},{2,4},{4,6},{6,8},{8,10},{10,12},{12,14},{14,0},{1,3},{3,5},... | collective-permute-start | bytes 1572872 | tf_op jit(solution)/shard_map/ppermute | solution.py:159
  75.0 21.3 %collective-permute-start.17 = (f32[32,4096]{1,0:T(8,128)}, f32[32,4096]{1,0:T(8,128)S(1)}, u32[]{:S(2)}, u32[]{:S(2)}) collective-permute-start(f32[32,4096]{1,0:T(8,128)} %get-tuple-element.52), channel_id=1, source_target_pairs={{0,14},{2,0},{4,2},{6,4},{8,6},{10,8},{12,10},{14,12},{1,15},{3,1}... | collective-permute-start | bytes 1572872 | tf_op jit(solution)/shard_map/ppermute | solution.py:159
  87.3 14.4 %all-to-all-start = ((f32[16,32,128]{2,1,0:T(8,128)}), f32[16,32,128]{2,1,0:T(8,128)S(1)}, u32[]{:S(2)}, u32[]{:S(2)}) async-start(f32[16,32,128]{2,1,0:T(8,128)} %bitcast_bitcast_fusion.1), calls=%async_computation | async-start | bytes 524288 | tf_op jit(solution)/shard_map/all_to_all | solution.py:156
  106.2 15.3 %all-to-all-start.1 = ((f32[16,32,384]{2,1,0:T(8,128)}), f32[16,32,384]{2,1,0:T(8,128)S(1)}, u32[]{:S(2)}, u32[]{:S(2)}) async-start(f32[16,32,384]{2,1,0:T(8,128)} %bitcast.75), calls=%async_computation.1 | async-start | bytes 1572864 | tf_op jit(solution)/shard_map/all_to_all | solution.py:156
  109.8 50.0 %copy-start.1 = (bf16[1,512,512]{2,1,0:T(8,128)(2,1)S(1)}, bf16[1,512,512]{2,1,0:T(8,128)(2,1)}, u32[]{:S(2)}) copy-start(bf16[1,512,512]{2,1,0:T(8,128)(2,1)} %param.7) | copy-start | bytes 1572868
  138.6 16.4 %copy-start.4 = (f32[16,32,512]{2,1,0:T(8,128)}, f32[16,32,512]{2,1,0:T(8,128)S(1)}, u32[]{:S(2)}) copy-start(f32[16,32,512]{2,1,0:T(8,128)S(1)} %all_to_all.20.pieces_ref) | copy-start | bytes 3145732
  139.5 15.5 %all-to-all-start.3 = ((f32[16,1,128]{2,1,0:T(1,128)}), f32[16,1,128]{2,1,0:T(1,128)S(1)}, u32[]{:S(2)}, u32[]{:S(2)}) async-start(f32[16,1,128]{2,1,0:T(1,128)} %broadcast_in_dim.32), calls=%async_computation.3 | async-start | bytes 16384 | tf_op jit(solution)/shard_map/all_to_all | solution.py:156
  154.9 0.6 copy-start.7

commit v7 on v6

v7 whole, which is shorter than its diff:
```python
import math

import jax
import jax.numpy as jnp
from jax import lax
from jax.experimental import pallas as pl
from jax.experimental.pallas import tpu as pltpu
from jax.sharding import Mesh, PartitionSpec as P

D = 8192
INNER_STEP = 100

beta_first = 0.9
beta_second = 0.95
inner_rate = 0.5
decay_weight = 0.1
outer_rate = 0.7
momentum_coef = 0.9

Y, X, Z, C = 4, 4, 8, 2
ROWS_DEV = 32
PARTS = Z * C
WIDTH = D // 2
CHUNKS = ((0, WIDTH), (WIDTH, WIDTH // 2), (WIDTH + WIDTH // 2, WIDTH // 2))
EARLY = ((0, 0), (1, 0), (0, 1), (1, 1), (0, 2), (2, 0), (0, 3), (2, 1), (1, 2))
STEPS = (4, 3, 5, 2, 6, 1, 7, 0)
UP = [(i, (i + 1) % Z) for i in range(Z)]
DOWN = [(i, (i - 1) % Z) for i in range(Z)]
SWAP = [(0, 1), (1, 0)]


def reorder_rows(activations, z, c):
    rows = Z * C * ROWS_DEV
    place = lax.broadcasted_iota(jnp.int32, (rows, rows), 1)
    source = lax.broadcasted_iota(jnp.int32, (rows, rows), 0)
    block = place // ROWS_DEV
    mine = jnp.where(block < 2, block == 1, block >= 2 + (Z - 1))
    slot = jnp.where(block < 2, 0, jnp.where(block < Z + 1, block - 1, block - Z))
    step = jnp.zeros_like(slot)
    for at, distance in enumerate(STEPS):
        step = jnp.where(slot == at, distance, step)
    core = jnp.where(mine, c, 1 - c)
    wanted = (((z + step) % Z) * C + core) * ROWS_DEV + place % ROWS_DEV
    pick = (wanted == source).astype(activations.dtype)
    return lax.dot_general(
        pick, activations, (((0,), (1,)), ((), ())), preferred_element_type=jnp.float32
    ).astype(activations.dtype)


def finish_kernel(squares_ref, pieces_ref, anchor_ref, momentum_ref, momentum_out, anchor_out):
    squares = jnp.sum(jnp.sum(squares_ref[...], axis=0), keepdims=True)
    ceiling = 0.3 * math.sqrt(ROWS_DEV * PARTS * D)
    factor = ceiling / jnp.maximum(jnp.sqrt(squares), ceiling)
    piece = pieces_ref.shape[2]
    for p in range(pieces_ref.shape[0]):
        at = slice(p * piece, (p + 1) * piece)
        scaled = factor * pieces_ref[p]
        momentum = momentum_coef * momentum_ref[:, at] + scaled
        momentum_out[:, at] = momentum
        anchor_out[:, at] = anchor_ref[:, at] - outer_rate * (scaled + momentum_coef * momentum)


def finish(squares, pieces, anchor, outer_momentum):
    replicas, _, both = pieces.shape
    part = pl.BlockSpec((ROWS_DEV, WIDTH), lambda h: (0, h))
    shape = jax.ShapeDtypeStruct(anchor.shape, jnp.float32)
    return pl.pallas_call(
        finish_kernel,
        grid=(2,),
        in_specs=[
            pl.BlockSpec(squares.shape, lambda h: (0, 0, 0)),
            pl.BlockSpec((replicas, ROWS_DEV, both // 2), lambda h: (0, 0, h)),
            part,
            part,
        ],
        out_specs=[part, part],
        out_shape=[shape, shape],
        cost_estimate=pl.CostEstimate(flops=7 * anchor.size, bytes_accessed=20 * anchor.size, transcendentals=0),
    )(squares, pieces, anchor, outer_momentum)


def per_device(hidden_acts, out_grads, anchor, drift, adam_first, adam_second, outer_momentum):
    z = lax.axis_index("z")
    c = lax.axis_index("c")
    ordered = reorder_rows(hidden_acts[0], z, c)
    cotangent = out_grads[0]
    near = 2 * ROWS_DEV
    stay = near + (Z - 1) * ROWS_DEV

    def product(lhs, rhs):
        return lax.dot_general(lhs, rhs, (((1,), (0,)), ((), ())), preferred_element_type=jnp.float32)

    def after(values, *tokens):
        return lax.optimization_barrier((values, tokens))[0]

    moved = [None] * len(CHUNKS)

    def own(k, distance, lo=0, hi=None):
        at = (STEPS.index(distance) - 1) * ROWS_DEV
        base, width = CHUNKS[k]
        hi = width if hi is None else hi
        return kept[k][at : at + ROWS_DEV, lo:hi] + rest[at : at + ROWS_DEV, base + lo : base + hi]

    def send(k, t, *tokens):
        lo, width = CHUNKS[k]
        half = width // 2
        if t == 0:
            source = after(first, *tokens)
            up, down = source[:, lo + half : lo + width], source[:, lo : lo + half]
        else:
            u, d = after(moved[k], *tokens)
            if t == 1:
                up = jnp.concatenate([own(k, 3, 0, half), own(k, 3, half) + u], axis=1)
                down = jnp.concatenate([own(k, 5, 0, half) + d, own(k, 5, half)], axis=1)
            else:
                up = own(k, 4 - t) + u
                down = own(k, 4 + t) + d
        moved[k] = (lax.ppermute(up, "z", UP), lax.ppermute(down, "z", DOWN))
        return up, down

    def finished(k, *tokens):
        u, d = after(moved[k], *tokens)
        return own(k, 0) + u + d

    first = product(ordered[:near], cotangent)
    theirs = lax.optimization_barrier(first[:ROWS_DEV])
    got = lax.ppermute(theirs, "c", SWAP)
    sent = product(after(ordered[near:stay], theirs), cotangent)
    rest = lax.ppermute(after(sent, got), "c", SWAP)
    first = first[ROWS_DEV:] + got
    last = ()
    for k, t in EARLY[:2]:
        last = send(k, t, last)
    lhs = after(ordered[stay:], sent, last)
    kept = [product(lhs, cotangent[:, lo : lo + width]) for lo, width in CHUNKS]
    for k, t in EARLY[2:]:
        last = send(k, t, last)

    correction_one = 1.0 - beta_first**INNER_STEP
    correction_two = 1.0 - beta_second**INNER_STEP
    replicas = Y * X
    piece = WIDTH // replicas

    def moments(first_old, second_old, gradient):
        moment_one = beta_first * first_old + (1.0 - beta_first) * gradient
        moment_two = beta_second * second_old + (1.0 - beta_second) * gradient * gradient
        return moment_one, moment_two

    def pseudo_of(lo, gradient):
        at = slice(lo, lo + WIDTH)
        own_drift = drift[0, :, at]
        moment_one, moment_two = moments(adam_first[0, :, at], adam_second[0, :, at], gradient)
        update = moment_one / correction_one / (
            jnp.sqrt(moment_two / correction_two) + 1e-08
        ) + decay_weight * (anchor[:, at] + own_drift)
        pseudo = inner_rate * update - own_drift
        return pseudo.reshape(ROWS_DEV, replicas, piece).transpose(1, 0, 2)

    def exchange(shares, axes=("y", "x")):
        return lax.all_to_all(shares, axes, split_axis=0, concat_axis=0, tiled=True)

    gradient_one = finished(0, last)
    last = pseudo_of(0, gradient_one)
    met = exchange(last)
    last = send(2, 2, last)
    last = send(1, 3, last)
    part = jnp.sum(after(met, last), axis=0)
    last = send(2, 3, last, part)
    gradient_two = finished(1, last)
    gradient_three = finished(2, gradient_two)
    gradient_two = jnp.concatenate([gradient_two, gradient_three], axis=1)
    met = exchange(pseudo_of(WIDTH, gradient_two))
    part = jnp.concatenate([part, jnp.sum(met, axis=0)], axis=1) / replicas
    pieces = exchange(jnp.broadcast_to(part[None], (replicas,) + part.shape))
    gradient = jnp.concatenate([gradient_one, gradient_two], axis=1)
    moment_one, moment_two = moments(adam_first[0], adam_second[0], gradient)
    squares = jnp.sum(jnp.sum(pieces * pieces, axis=(0, 1)).reshape(-1, 128), axis=0)
    squares = exchange(jnp.broadcast_to(squares, (PARTS, 1, 128)), ("z", "c"))
    momentum, updated = finish(squares, pieces, anchor, outer_momentum)
    return (moment_one[None], moment_two[None], momentum, updated)


def solution(mesh):
    devices = mesh.devices.reshape(Y, X, Z, C)
    grid = Mesh(devices, ("y", "x", "z", "c"))
    rep, fsdp = ("y", "x"), ("z", "c")
    return jax.shard_map(
        per_device,
        mesh=grid,
        in_specs=(
            P(rep, fsdp, None),
            P(rep, fsdp, None),
            P(fsdp, None),
            P(rep, fsdp, None),
            P(rep, fsdp, None),
            P(rep, fsdp, None),
            P(fsdp, None),
        ),
        out_specs=(
            P(rep, fsdp, None),
            P(rep, fsdp, None),
            P(fsdp, None),
            P(fsdp, None),
        ),
        check_vma=False,
    )
```

time: 160 us -> 166 us (1.038)
  waiting for transfers between devices: 66.1 us -> 43.6 us
  blocking collectives: 16.9 us -> 30.5 us
  starting transfers between devices: 47.2 us -> 57 us
  other arithmetic: 11.4 us -> 17.6 us
    all_to_all x3 -> x2, waiting for transfers between devices: 20.8 us -> 3.95 us  [exchange(): return lax.all_to_all(shares, axes, split_axis=0, concat_axis=0, tiled=True)]
    all_to_all x1 -> x2, blocking collectives: 16.9 us -> 30.5 us  [exchange(): return lax.all_to_all(shares, axes, split_axis=0, concat_axis=0, tiled=True)]
    ppermute x16 -> x24, starting transfers between devices: 24.6 us -> 30.7 us  [send(): moved[k] = (lax.ppermute(up, 'z', UP), lax.ppermute(down, 'z', DOWN))]
    ppermute x16 -> x24, waiting for transfers between devices: 44.5 us -> 38.8 us  [send(): moved[k] = (lax.ppermute(up, 'z', UP), lax.ppermute(down, 'z', DOWN))]
    add x6 -> x9, other arithmetic: 2.06 us -> 7.32 us  [the longest x6 7.03 us: send(): down = own(k, 4 + t) + d]
    all_to_all x3 -> x2, starting transfers between devices: 18.9 us -> 22.6 us  [exchange(): return lax.all_to_all(shares, axes, split_axis=0, concat_axis=0, tiled=True)]
    transpose x1 -> x0, other arithmetic: 2.03 us -> none  [pseudo_of(): pseudo.reshape(ROWS_DEV, replicas, width // replicas).transpose(1, 0, 2)]
    dot_general x4 -> x5, matrix products: 5.95 us -> 6.04 us  [product(): lax.dot_general(lhs, rhs, (((1,), (0,)), ((), ())), preferred_element_typ...]
  transfers between devices with their start and end apart: 21 -> 28, of which waited for: 13 -> 10; matrix products, arithmetic and copies ran while one was open for 8% -> 12% of each run, Pallas kernels for 0% -> 0%
where the time goes in v7:
time: 166 us
  starting transfers between devices  57 us (34%)
  waiting for transfers between devices  43.6 us (26%)
  blocking collectives  30.5 us (18%)
  other arithmetic  17.6 us (11%)
  matrix products  6.55 us (4%)
  local copies, waits for them, and re-layouts  6.45 us (4%)
  Pallas kernels  3.1 us (2%)
    ppermute x24, waiting for transfers between devices, send(): moved[k] = (lax.ppermute(up, 'z', UP), lax.ppermute(down, 'z', DOWN))  38.8 us
    ppermute x24, starting transfers between devices, send(): moved[k] = (lax.ppermute(up, 'z', UP), lax.ppermute(down, 'z', DOWN))  30.7 us
    all_to_all x2, blocking collectives, exchange(): return lax.all_to_all(shares, axes, split_axis=0, concat_axis=0, tiled=True)  30.5 us
    all_to_all x2, starting transfers between devices, exchange(): return lax.all_to_all(shares, axes, split_axis=0, concat_axis=0, tiled=True)  22.6 us
    add x6, other arithmetic, send(): down = own(k, 4 + t) + d  7.03 us
    dot_general x5, matrix products, product(): lax.dot_general(lhs, rhs, (((1,), (0,)), ((), ())), preferred_element_typ...  6.04 us
    unnamed x24, local copies, waits for them, and re-layouts  4.5 us
    all_to_all x2, waiting for transfers between devices, exchange(): return lax.all_to_all(shares, axes, split_axis=0, concat_axis=0, tiled=True)  3.95 us
  transfers between devices with their start and end apart: 28, of which 10 were waited for; matrix products, arithmetic and copies ran while one was open for 12% of the time, Pallas kernels for 0%

profile of v7, /device:TPU:1, one launch (start us, length us, event | category | flops | bytes accessed | tf_op | source)
XLA Modules:
  0.0 165.9 jit_solution(10516768862172643225)
XLA Ops:
  0.7 1.0 copy-done
  2.2 2.9 %copy-done.2 = bf16[1,512,8192]{2,1,0:T(8,128)(2,1)S(1)} copy-done((bf16[1,512,8192]{2,1,0:T(8,128)(2,1)S(1)}, bf16[1,512,8192]{2,1,0:T(8,128)(2,1)}, u32[]{:S(2)}) %copy-start.2) | copy-done | bytes 8388632
  5.1 1.6 fusion.81
  6.7 3.3 %collective-permute-start = (f32[32,8192]{1,0:T(8,128)S(1)}, f32[32,8192]{1,0:T(8,128)S(1)}, u32[]{:S(2)}, u32[]{:S(2)}) collective-permute-start(f32[32,8192]{1,0:T(8,128)S(1)} %slice.307), channel_id=1, source_target_pairs={{0,1},{1,0},{2,3},{3,2},{4,5},{5,4},{6,7},{7,6},{8,9},{9,8},{10,11... | collective-permute-start | bytes 3145736 | tf_op jit(solution)/shard_map/ppermute | solution.py:127
  10.1 2.1 %fusion.89 = f32[224,8192]{1,0:T(8,128)S(1)} fusion(bf16[224,512]{1,0:T(8,128)(2,1)S(1)} %get-tuple-element.36, bf16[1,512,8192]{2,1,0:T(8,128)(2,1)S(1)} %copy-done.2), kind=kOutput, calls=%fused_computation.153 | convolution fusion | flops 1879048192 | bytes 15958016 | tf_op jit(solution)/shard_map/dot_general | solution.py:91
  12.9 3.9 %collective-permute-start.3 = (f32[32,2048]{1,0:T(8,128)S(1)}, f32[32,2048]{1,0:T(8,128)S(1)}, u32[]{:S(2)}, u32[]{:S(2)}) collective-permute-start(f32[32,2048]{1,0:T(8,128)S(1)} %get-tuple-element.100), channel_id=1, source_target_pairs={{0,14},{2,0},{4,2},{6,4},{8,6},{10,8},{12,10},{14,12},{1,15},{3,1}... | collective-permute-start | bytes 786440 | tf_op jit(solution)/shard_map/ppermute | solution.py:118
  17.0 2.7 %collective-permute-start.7 = (f32[32,1024]{1,0:T(8,128)S(1)}, f32[32,1024]{1,0:T(8,128)S(1)}, u32[]{:S(2)}, u32[]{:S(2)}) collective-permute-start(f32[32,1024]{1,0:T(8,128)S(1)} %get-tuple-element.98), channel_id=1, source_target_pairs={{0,14},{2,0},{4,2},{6,4},{8,6},{10,8},{12,10},{14,12},{1,15},{3,1}... | collective-permute-start | bytes 393224 | tf_op jit(solution)/shard_map/ppermute | solution.py:118
  19.6 1.1 fusion
  20.8 0.6 fusion.4
  21.4 1.9 %collective-permute-done.2 = f32[32,2048]{1,0:T(8,128)S(1)} collective-permute-done((f32[32,2048]{1,0:T(8,128)S(1)}, f32[32,2048]{1,0:T(8,128)S(1)}, u32[]{:S(2)}, u32[]{:S(2)}) %collective-permute-start.2) | collective-permute-done | bytes 262176 | tf_op jit(solution)/shard_map/ppermute | solution.py:118
  23.3 0.7 collective-permute-done.1
  24.3 3.9 %collective-permute-start.5 = (f32[32,4096]{1,0:T(8,128)S(1)}, f32[32,4096]{1,0:T(8,128)S(1)}, u32[]{:S(2)}, u32[]{:S(2)}) collective-permute-start(f32[32,4096]{1,0:T(8,128)S(1)} %pad_maximum_fusion.2), channel_id=1, source_target_pairs={{0,14},{2,0},{4,2},{6,4},{8,6},{10,8},{12,10},{14,12},{1,15},{3,1}... | collective-permute-start | bytes 1572872 | tf_op jit(solution)/shard_map/ppermute | solution.py:118
  28.4 11.7 %collective-permute-done.4 = f32[32,4096]{1,0:T(8,128)S(1)} collective-permute-done((f32[32,4096]{1,0:T(8,128)S(1)}, f32[32,4096]{1,0:T(8,128)S(1)}, u32[]{:S(2)}, u32[]{:S(2)}) %collective-permute-start.4) | collective-permute-done | bytes 524320 | tf_op jit(solution)/shard_map/ppermute | solution.py:118
  40.6 2.7 %collective-permute-start.9 = (f32[32,4096]{1,0:T(8,128)S(1)}, f32[32,4096]{1,0:T(8,128)S(1)}, u32[]{:S(2)}, u32[]{:S(2)}) collective-permute-start(f32[32,4096]{1,0:T(8,128)S(1)} %get-tuple-element.72), channel_id=1, source_target_pairs={{0,14},{2,0},{4,2},{6,4},{8,6},{10,8},{12,10},{14,12},{1,15},{3,1}... | collective-permute-start | bytes 1572872 | tf_op jit(solution)/shard_map/ppermute | solution.py:118
  43.3 0.6 fusion.2
  44.0 2.7 %collective-permute-start.13 = (f32[32,2048]{1,0:T(8,128)S(1)}, f32[32,2048]{1,0:T(8,128)S(1)}, u32[]{:S(2)}, u32[]{:S(2)}) collective-permute-start(f32[32,2048]{1,0:T(8,128)S(1)} %pad_maximum_fusion.5), channel_id=1, source_target_pairs={{0,14},{2,0},{4,2},{6,4},{8,6},{10,8},{12,10},{14,12},{1,15},{3,1}... | collective-permute-start | bytes 786440 | tf_op jit(solution)/shard_map/ppermute | solution.py:118
  46.8 7.6 %collective-permute-done.8 = f32[32,4096]{1,0:T(8,128)S(1)} collective-permute-done((f32[32,4096]{1,0:T(8,128)S(1)}, f32[32,4096]{1,0:T(8,128)S(1)}, u32[]{:S(2)}, u32[]{:S(2)}) %collective-permute-start.8) | collective-permute-done | bytes 524320 | tf_op jit(solution)/shard_map/ppermute | solution.py:118
  54.4 0.9 collective-permute-start.15
  55.5 0.6 collective-permute-start.10
  56.1 6.7 %collective-permute-done.14 = f32[32,1024]{1,0:T(8,128)S(1)} collective-permute-done((f32[32,1024]{1,0:T(8,128)S(1)}, f32[32,1024]{1,0:T(8,128)S(1)}, u32[]{:S(2)}, u32[]{:S(2)}) %collective-permute-start.14) | collective-permute-done | bytes 131104 | tf_op jit(solution)/shard_map/ppermute | solution.py:118
  62.8 0.9 collective-permute-start.11
  63.8 0.7 pad_maximum_fusion.6
  65.1 0.7 pad_maximum_fusion.7
  65.8 2.1 %collective-permute-start.19 = (f32[32,2048]{1,0:T(8,128)}, f32[32,2048]{1,0:T(8,128)}, u32[]{:S(2)}, u32[]{:S(2)}) collective-permute-start(f32[32,2048]{1,0:T(8,128)} %pad_maximum_fusion.7), channel_id=1, source_target_pairs={{0,14},{2,0},{4,2},{6,4},{8,6},{10,8},{12,10},{14,12},{1,15},{3,1}... | collective-permute-start | bytes 786440 | tf_op jit(solution)/shard_map/ppermute | solution.py:118
  67.9 0.9 fusion.73
  68.8 5.2 %collective-permute-done.10 = f32[32,4096]{1,0:T(8,128)S(1)} collective-permute-done((f32[32,4096]{1,0:T(8,128)S(1)}, f32[32,4096]{1,0:T(8,128)S(1)}, u32[]{:S(2)}, u32[]{:S(2)}) %collective-permute-start.10) | collective-permute-done | bytes 524320 | tf_op jit(solution)/shard_map/ppermute | solution.py:118
  74.0 0.9 collective-permute-start.17
  75.0 1.2 bitcast_subtract_fusion.1
  76.3 0.8 copy.20
  77.1 6.8 %all-to-all-start = ((f32[16,32,256]{2,1,0:T(8,128)}), f32[16,32,256]{2,1,0:T(8,128)S(1)}, u32[]{:S(2)}, u32[]{:S(2)}) async-start(f32[16,32,256]{2,1,0:T(8,128)} %bitcast.80), calls=%async_computation | async-start | bytes 1048576 | tf_op jit(solution)/shard_map/all_to_all | solution.py:160
  83.9 2.2 %fusion.68 = (f32[32,2048]{1,0:T(8,128)}, f32[32,2048]{1,0:T(8,128)}) fusion(f32[32,2048]{1,0:T(8,128)} %collective-permute-done.19, f32[224,8192]{1,0:T(8,128)} %copy-done.4, f32[224,2048]{1,0:T(8,128)} %copy-done.5, f32[32,2048]{1,0:T(8,128)} %collective-permute-done.18), kind=kLoop, calls=%fused_computation.105 | loop fusion | flops 262144 | bytes 2097152 | tf_op jit(solution)/shard_map/add | solution.py:117
  86.6 2.1 %collective-permute-start.23 = (f32[32,2048]{1,0:T(8,128)}, f32[32,2048]{1,0:T(8,128)}, u32[]{:S(2)}, u32[]{:S(2)}) collective-permute-start(f32[32,2048]{1,0:T(8,128)} %get-tuple-element.82), channel_id=1, source_target_pairs={{0,14},{2,0},{4,2},{6,4},{8,6},{10,8},{12,10},{14,12},{1,15},{3,1}... | collective-permute-start | bytes 786440 | tf_op jit(solution)/shard_map/ppermute | solution.py:118
  88.8 2.1 %fusion.67 = (f32[32,2048]{1,0:T(8,128)}, f32[32,2048]{1,0:T(8,128)}) fusion(f32[32,2048]{1,0:T(8,128)} %collective-permute-done.17, f32[224,8192]{1,0:T(8,128)} %copy-done.4, f32[224,2048]{1,0:T(8,128)S(1)} %fusion.4, f32[32,2048]{1,0:T(8,128)} %collective-permute-done.16), kind=kLoop, calls=%fused_computation.103 | loop fusion | flops 262144 | bytes 2097152 | tf_op jit(solution)/shard_map/add | solution.py:117
  90.9 2.7 %collective-permute-start.21 = (f32[32,2048]{1,0:T(8,128)}, f32[32,2048]{1,0:T(8,128)}, u32[]{:S(2)}, u32[]{:S(2)}) collective-permute-start(f32[32,2048]{1,0:T(8,128)} %get-tuple-element.80), channel_id=1, source_target_pairs={{0,14},{2,0},{4,2},{6,4},{8,6},{10,8},{12,10},{14,12},{1,15},{3,1}... | collective-permute-start | bytes 786440 | tf_op jit(solution)/shard_map/ppermute | solution.py:118
  93.6 1.4 fusion.65
  95.1 2.7 %collective-permute-start.25 = (f32[32,2048]{1,0:T(8,128)S(1)}, f32[32,2048]{1,0:T(8,128)S(1)}, u32[]{:S(2)}, u32[]{:S(2)}) collective-permute-start(f32[32,2048]{1,0:T(8,128)S(1)} %get-tuple-element.78), channel_id=1, source_target_pairs={{0,14},{2,0},{4,2},{6,4},{8,6},{10,8},{12,10},{14,12},{1,15},{3,1}... | collective-permute-start | bytes 786440 | tf_op jit(solution)/shard_map/ppermute | solution.py:118
  97.8 1.0 collective-permute-done.20
  98.8 1.2 fusion.72
  100.0 4.7 %collective-permute-done.24 = f32[32,2048]{1,0:T(8,128)S(1)} collective-permute-done((f32[32,2048]{1,0:T(8,128)S(1)}, f32[32,2048]{1,0:T(8,128)S(1)}, u32[]{:S(2)}, u32[]{:S(2)}) %collective-permute-start.24) | collective-permute-done | bytes 262176 | tf_op jit(solution)/shard_map/ppermute | solution.py:118
  104.7 1.1 fusion.64
  105.8 1.8 %bitcast_subtract_fusion = f32[32,4096]{1,0:T(8,128)S(1)} fusion(f32[32,8192]{1,0:T(8,128)} %anchor_ref.1, f32[1,32,8192]{2,1,0:T(8,128)} %param.10, f32[1,32,8192]{2,1,0:T(8,128)S(1)} %copy-done.6, f32[32,2048]{1,0:T(8,128)S(1)} %fusion.64, f32[32,2048]{1,0:T(8,128)S(1)} %fusion.72, f32[1,32,8192]{2,1,0:T(8,128)} %param.11), kind=kLoop, calls=%fused_computation.62 | loop fusion | flops 2228224 | bytes 3145728 | tf_op jit(solution)/shard_map/sub | solution.py:156
  107.7 15.3 %all_to_all.20 = f32[16,32,256]{2,1,0:T(8,128)S(1)} all-to-all(f32[16,32,256]{2,1,0:T(8,128)S(1)} %bitcast.81), channel_id=1, replica_groups=mesh['y'=4,'x'=4,'z'=8,'c'=2] {'y','x'}, dimensions={0} | all-to-all | bytes 1048576 | tf_op jit(solution)/shard_map/all_to_all | solution.py:160
  123.2 15.2 %all_to_all.21.pieces_ref = f32[16,32,512]{2,1,0:T(8,128)S(1)} all-to-all(f32[16,32,512]{2,1,0:T(8,128)S(1)} %broadcast_in_dim.31), channel_id=1, replica_groups=mesh['y'=4,'x'=4,'z'=8,'c'=2] {'y','x'}, dimensions={0} | all-to-all | bytes 2097152 | tf_op jit(solution)/shard_map/all_to_all | solution.py:160
  138.5 0.8 broadcast_in_dim.32
  139.3 15.9 %all-to-all-start.3 = ((f32[16,1,128]{2,1,0:T(1,128)}), f32[16,1,128]{2,1,0:T(1,128)S(1)}, u32[]{:S(2)}, u32[]{:S(2)}) async-start(f32[16,1,128]{2,1,0:T(1,128)} %broadcast_in_dim.32), calls=%async_computation.3 | async-start | bytes 16384 | tf_op jit(solution)/shard_map/all_to_all | solution.py:160
  155.1 3.1 %fusion.14 = (f32[1,32,8192]{2,1,0:T(8,128)}, f32[1,32,8192]{2,1,0:T(8,128)}) fusion(f32[1,32,8192]{2,1,0:T(8,128)S(1)} %copy-done.6, f32[1,32,2048]{2,1,0:T(8,128)S(1)} %bitcast.77, f32[1,32,2048]{2,1,0:T(8,128)} %bitcast.76, f32[1,32,4096]{2,1,0:T(8,128)} %bitcast.78, f32[1,32,8192]{2,1,0:T(8,128)} %param.11), kind=kLoop, calls=%fused_computation.25 | loop fusion | flops 2359296 | bytes 5242880 | tf_op jit(solution)/shard_map/add | solution.py:146
  158.2 3.9 %all-to-all-done.3.squares_ref = f32[16,1,128]{2,1,0:T(1,128)S(1)} async-done(((f32[16,1,128]{2,1,0:T(1,128)}), f32[16,1,128]{2,1,0:T(1,128)S(1)}, u32[]{:S(2)}, u32[]{:S(2)}) %all-to-all-start.3) | async-done | bytes 8224 | tf_op jit(solution)/shard_map/all_to_all | solution.py:160
  162.8 3.1 %shard_map.102 = (f32[32,8192]{1,0:T(8,128)}, f32[32,8192]{1,0:T(8,128)}) custom-call(f32[16,1,128]{2,1,0:T(1,128)} %copy-done.11, f32[16,32,512]{2,1,0:T(8,128)} %copy-done.3, f32[32,8192]{1,0:T(8,128)} %anchor_ref.1, f32[32,8192]{1,0:T(8,128)} %momentum_ref.1), custom_call_target="tpu_custom_call" | custom-call | flops 1835008 | bytes 5242880 | tf_op jit(solution)/shard_map/pallas_call | solution.py:67
  (79 shorter events, 5.1 us)
Async XLA Ops:
  0.6 1.1 copy-start
  1.7 3.4 %copy-start.2 = (bf16[1,512,8192]{2,1,0:T(8,128)(2,1)S(1)}, bf16[1,512,8192]{2,1,0:T(8,128)(2,1)}, u32[]{:S(2)}) copy-start(bf16[1,512,8192]{2,1,0:T(8,128)(2,1)} %param.8) | copy-start | bytes 25165828
  6.7 5.6 %collective-permute-start = (f32[32,8192]{1,0:T(8,128)S(1)}, f32[32,8192]{1,0:T(8,128)S(1)}, u32[]{:S(2)}, u32[]{:S(2)}) collective-permute-start(f32[32,8192]{1,0:T(8,128)S(1)} %slice.307), channel_id=1, source_target_pairs={{0,1},{1,0},{2,3},{3,2},{4,5},{5,4},{6,7},{7,6},{8,9},{9,8},{10,11... | collective-permute-start | bytes 3145736 | tf_op jit(solution)/shard_map/ppermute | solution.py:127
  12.3 11.7 %collective-permute-start.1 = (f32[224,8192]{1,0:T(8,128)S(1)}, f32[224,8192]{1,0:T(8,128)S(1)}, u32[]{:S(2)}, u32[]{:S(2)}) collective-permute-start(f32[224,8192]{1,0:T(8,128)S(1)} %fusion.89), channel_id=1, source_target_pairs={{0,1},{1,0},{2,3},{3,2},{4,5},{5,4},{6,7},{7,6},{8,9},{9,8},{10,11... | collective-permute-start | bytes 22020104 | tf_op jit(solution)/shard_map/ppermute | solution.py:129
  12.9 10.5 %collective-permute-start.2 = (f32[32,2048]{1,0:T(8,128)S(1)}, f32[32,2048]{1,0:T(8,128)S(1)}, u32[]{:S(2)}, u32[]{:S(2)}) collective-permute-start(f32[32,2048]{1,0:T(8,128)S(1)} %get-tuple-element.101), channel_id=1, source_target_pairs={{0,2},{2,4},{4,6},{6,8},{8,10},{10,12},{12,14},{14,0},{1,3},{3,5},... | collective-permute-start | bytes 786440 | tf_op jit(solution)/shard_map/ppermute | solution.py:118
  12.9 10.4 %collective-permute-start.3 = (f32[32,2048]{1,0:T(8,128)S(1)}, f32[32,2048]{1,0:T(8,128)S(1)}, u32[]{:S(2)}, u32[]{:S(2)}) collective-permute-start(f32[32,2048]{1,0:T(8,128)S(1)} %get-tuple-element.100), channel_id=1, source_target_pairs={{0,14},{2,0},{4,2},{6,4},{8,6},{10,8},{12,10},{14,12},{1,15},{3,1}... | collective-permute-start | bytes 786440 | tf_op jit(solution)/shard_map/ppermute | solution.py:118
  16.9 11.3 %collective-permute-start.6 = (f32[32,1024]{1,0:T(8,128)S(1)}, f32[32,1024]{1,0:T(8,128)S(1)}, u32[]{:S(2)}, u32[]{:S(2)}) collective-permute-start(f32[32,1024]{1,0:T(8,128)S(1)} %get-tuple-element.99), channel_id=1, source_target_pairs={{0,2},{2,4},{4,6},{6,8},{8,10},{10,12},{12,14},{14,0},{1,3},{3,5},... | collective-permute-start | bytes 393224 | tf_op jit(solution)/shard_map/ppermute | solution.py:118
  17.0 11.3 %collective-permute-start.7 = (f32[32,1024]{1,0:T(8,128)S(1)}, f32[32,1024]{1,0:T(8,128)S(1)}, u32[]{:S(2)}, u32[]{:S(2)}) collective-permute-start(f32[32,1024]{1,0:T(8,128)S(1)} %get-tuple-element.98), channel_id=1, source_target_pairs={{0,14},{2,0},{4,2},{6,4},{8,6},{10,8},{12,10},{14,12},{1,15},{3,1}... | collective-permute-start | bytes 393224 | tf_op jit(solution)/shard_map/ppermute | solution.py:118
  24.0 51.0 %copy-start.4 = (f32[224,8192]{1,0:T(8,128)}, f32[224,8192]{1,0:T(8,128)S(1)}, u32[]{:S(2)}) copy-start(f32[224,8192]{1,0:T(8,128)S(1)} %collective-permute-done.1) | copy-start | bytes 22020100
  24.2 15.9 %collective-permute-start.4 = (f32[32,4096]{1,0:T(8,128)S(1)}, f32[32,4096]{1,0:T(8,128)S(1)}, u32[]{:S(2)}, u32[]{:S(2)}) collective-permute-start(f32[32,4096]{1,0:T(8,128)S(1)} %pad_maximum_fusion.1), channel_id=1, source_target_pairs={{0,2},{2,4},{4,6},{6,8},{8,10},{10,12},{12,14},{14,0},{1,3},{3,5},... | collective-permute-start | bytes 1572872 | tf_op jit(solution)/shard_map/ppermute | solution.py:118
  24.3 15.8 %collective-permute-start.5 = (f32[32,4096]{1,0:T(8,128)S(1)}, f32[32,4096]{1,0:T(8,128)S(1)}, u32[]{:S(2)}, u32[]{:S(2)}) collective-permute-start(f32[32,4096]{1,0:T(8,128)S(1)} %pad_maximum_fusion.2), channel_id=1, source_target_pairs={{0,14},{2,0},{4,2},{6,4},{8,6},{10,8},{12,10},{14,12},{1,15},{3,1}... | collective-permute-start | bytes 1572872 | tf_op jit(solution)/shard_map/ppermute | solution.py:118
  40.3 34.7 %copy-start.6 = (f32[1,32,8192]{2,1,0:T(8,128)S(1)}, f32[1,32,8192]{2,1,0:T(8,128)}, u32[]{:S(2)}) copy-start(f32[1,32,8192]{2,1,0:T(8,128)} %param.12) | copy-start | bytes 3145732
  40.3 34.7 %copy-start.7 = (f32[1,32,8192]{2,1,0:T(8,128)S(1)}, f32[1,32,8192]{2,1,0:T(8,128)}, u32[]{:S(2)}) copy-start(f32[1,32,8192]{2,1,0:T(8,128)} %param.11) | copy-start | bytes 3145732
  40.3 34.7 %copy-start.8 = (f32[32,8192]{1,0:T(8,128)S(1)}, f32[32,8192]{1,0:T(8,128)}, u32[]{:S(2)}) copy-start(f32[32,8192]{1,0:T(8,128)} %anchor_ref.1) | copy-start | bytes 3145732
  40.3 34.7 %copy-start.10 = (f32[1,32,8192]{2,1,0:T(8,128)S(1)}, f32[1,32,8192]{2,1,0:T(8,128)}, u32[]{:S(2)}) copy-start(f32[1,32,8192]{2,1,0:T(8,128)} %param.10) | copy-start | bytes 3145732
  40.3 14.0 %collective-permute-start.8 = (f32[32,4096]{1,0:T(8,128)S(1)}, f32[32,4096]{1,0:T(8,128)S(1)}, u32[]{:S(2)}, u32[]{:S(2)}) collective-permute-start(f32[32,4096]{1,0:T(8,128)S(1)} %get-tuple-element.73), channel_id=1, source_target_pairs={{0,2},{2,4},{4,6},{6,8},{8,10},{10,12},{12,14},{14,0},{1,3},{3,5},... | collective-permute-start | bytes 1572872 | tf_op jit(solution)/shard_map/ppermute | solution.py:118
  40.6 14.7 %collective-permute-start.9 = (f32[32,4096]{1,0:T(8,128)S(1)}, f32[32,4096]{1,0:T(8,128)S(1)}, u32[]{:S(2)}, u32[]{:S(2)}) collective-permute-start(f32[32,4096]{1,0:T(8,128)S(1)} %get-tuple-element.72), channel_id=1, source_target_pairs={{0,14},{2,0},{4,2},{6,4},{8,6},{10,8},{12,10},{14,12},{1,15},{3,1}... | collective-permute-start | bytes 1572872 | tf_op jit(solution)/shard_map/ppermute | solution.py:118
  43.9 19.8 %copy-start.5 = (f32[224,2048]{1,0:T(8,128)}, f32[224,2048]{1,0:T(8,128)S(1)}, u32[]{:S(2)}) copy-start(f32[224,2048]{1,0:T(8,128)S(1)} %fusion.2) | copy-start | bytes 5505028
  43.9 21.9 %collective-permute-start.12 = (f32[32,2048]{1,0:T(8,128)S(1)}, f32[32,2048]{1,0:T(8,128)S(1)}, u32[]{:S(2)}, u32[]{:S(2)}) collective-permute-start(f32[32,2048]{1,0:T(8,128)S(1)} %pad_maximum_fusion.4), channel_id=1, source_target_pairs={{0,2},{2,4},{4,6},{6,8},{8,10},{10,12},{12,14},{14,0},{1,3},{3,5},... | collective-permute-start | bytes 786440 | tf_op jit(solution)/shard_map/ppermute | solution.py:118
  44.0 23.9 %collective-permute-start.13 = (f32[32,2048]{1,0:T(8,128)S(1)}, f32[32,2048]{1,0:T(8,128)S(1)}, u32[]{:S(2)}, u32[]{:S(2)}) collective-permute-start(f32[32,2048]{1,0:T(8,128)S(1)} %pad_maximum_fusion.5), channel_id=1, source_target_pairs={{0,14},{2,0},{4,2},{6,4},{8,6},{10,8},{12,10},{14,12},{1,15},{3,1}... | collective-permute-start | bytes 786440 | tf_op jit(solution)/shard_map/ppermute | solution.py:118
  46.7 16.1 %collective-permute-start.14 = (f32[32,1024]{1,0:T(8,128)S(1)}, f32[32,1024]{1,0:T(8,128)S(1)}, u32[]{:S(2)}, u32[]{:S(2)}) collective-permute-start(f32[32,1024]{1,0:T(8,128)S(1)} %get-tuple-element.97), channel_id=1, source_target_pairs={{0,2},{2,4},{4,6},{6,8},{8,10},{10,12},{12,14},{14,0},{1,3},{3,5},... | collective-permute-start | bytes 393224 | tf_op jit(solution)/shard_map/ppermute | solution.py:118
  54.4 9.4 %collective-permute-start.15 = (f32[32,1024]{1,0:T(8,128)S(1)}, f32[32,1024]{1,0:T(8,128)S(1)}, u32[]{:S(2)}, u32[]{:S(2)}) collective-permute-start(f32[32,1024]{1,0:T(8,128)S(1)} %get-tuple-element.96), channel_id=1, source_target_pairs={{0,14},{2,0},{4,2},{6,4},{8,6},{10,8},{12,10},{14,12},{1,15},{3,1}... | collective-permute-start | bytes 393224 | tf_op jit(solution)/shard_map/ppermute | solution.py:118
  55.5 18.5 %collective-permute-start.10 = (f32[32,4096]{1,0:T(8,128)S(1)}, f32[32,4096]{1,0:T(8,128)S(1)}, u32[]{:S(2)}, u32[]{:S(2)}) collective-permute-start(f32[32,4096]{1,0:T(8,128)S(1)} %get-tuple-element.71), channel_id=1, source_target_pairs={{0,2},{2,4},{4,6},{6,8},{8,10},{10,12},{12,14},{14,0},{1,3},{3,5},... | collective-permute-start | bytes 1572872 | tf_op jit(solution)/shard_map/ppermute | solution.py:118
  62.8 12.2 %collective-permute-start.11 = (f32[32,4096]{1,0:T(8,128)S(1)}, f32[32,4096]{1,0:T(8,128)S(1)}, u32[]{:S(2)}, u32[]{:S(2)}) collective-permute-start(f32[32,4096]{1,0:T(8,128)S(1)} %get-tuple-element.70), channel_id=1, source_target_pairs={{0,14},{2,0},{4,2},{6,4},{8,6},{10,8},{12,10},{14,12},{1,15},{3,1}... | collective-permute-start | bytes 1572872 | tf_op jit(solution)/shard_map/ppermute | solution.py:118
  64.5 19.3 %collective-permute-start.18 = (f32[32,2048]{1,0:T(8,128)}, f32[32,2048]{1,0:T(8,128)}, u32[]{:S(2)}, u32[]{:S(2)}) collective-permute-start(f32[32,2048]{1,0:T(8,128)} %pad_maximum_fusion.6), channel_id=1, source_target_pairs={{0,2},{2,4},{4,6},{6,8},{8,10},{10,12},{12,14},{14,0},{1,3},{3,5},... | collective-permute-start | bytes 786440 | tf_op jit(solution)/shard_map/ppermute | solution.py:118
  65.8 18.1 %collective-permute-start.19 = (f32[32,2048]{1,0:T(8,128)}, f32[32,2048]{1,0:T(8,128)}, u32[]{:S(2)}, u32[]{:S(2)}) collective-permute-start(f32[32,2048]{1,0:T(8,128)} %pad_maximum_fusion.7), channel_id=1, source_target_pairs={{0,14},{2,0},{4,2},{6,4},{8,6},{10,8},{12,10},{14,12},{1,15},{3,1}... | collective-permute-start | bytes 786440 | tf_op jit(solution)/shard_map/ppermute | solution.py:118
  68.8 19.9 %collective-permute-start.16 = (f32[32,2048]{1,0:T(8,128)}, f32[32,2048]{1,0:T(8,128)}, u32[]{:S(2)}, u32[]{:S(2)}) collective-permute-start(f32[32,2048]{1,0:T(8,128)} %get-tuple-element.85), channel_id=1, source_target_pairs={{0,2},{2,4},{4,6},{6,8},{8,10},{10,12},{12,14},{14,0},{1,3},{3,5},... | collective-permute-start | bytes 786440 | tf_op jit(solution)/shard_map/ppermute | solution.py:118
  74.0 14.8 %collective-permute-start.17 = (f32[32,2048]{1,0:T(8,128)}, f32[32,2048]{1,0:T(8,128)}, u32[]{:S(2)}, u32[]{:S(2)}) collective-permute-start(f32[32,2048]{1,0:T(8,128)} %get-tuple-element.84), channel_id=1, source_target_pairs={{0,14},{2,0},{4,2},{6,4},{8,6},{10,8},{12,10},{14,12},{1,15},{3,1}... | collective-permute-start | bytes 786440 | tf_op jit(solution)/shard_map/ppermute | solution.py:118
  77.1 16.4 %all-to-all-start = ((f32[16,32,256]{2,1,0:T(8,128)}), f32[16,32,256]{2,1,0:T(8,128)S(1)}, u32[]{:S(2)}, u32[]{:S(2)}) async-start(f32[16,32,256]{2,1,0:T(8,128)} %bitcast.80), calls=%async_computation | async-start | bytes 1048576 | tf_op jit(solution)/shard_map/all_to_all | solution.py:160
  86.1 7.5 %collective-permute-start.22 = (f32[32,2048]{1,0:T(8,128)}, f32[32,2048]{1,0:T(8,128)}, u32[]{:S(2)}, u32[]{:S(2)}) collective-permute-start(f32[32,2048]{1,0:T(8,128)} %get-tuple-element.83), channel_id=1, source_target_pairs={{0,2},{2,4},{4,6},{6,8},{8,10},{10,12},{12,14},{14,0},{1,3},{3,5},... | collective-permute-start | bytes 786440 | tf_op jit(solution)/shard_map/ppermute | solution.py:118
  86.6 6.9 %collective-permute-start.23 = (f32[32,2048]{1,0:T(8,128)}, f32[32,2048]{1,0:T(8,128)}, u32[]{:S(2)}, u32[]{:S(2)}) collective-permute-start(f32[32,2048]{1,0:T(8,128)} %get-tuple-element.82), channel_id=1, source_target_pairs={{0,14},{2,0},{4,2},{6,4},{8,6},{10,8},{12,10},{14,12},{1,15},{3,1}... | collective-permute-start | bytes 786440 | tf_op jit(solution)/shard_map/ppermute | solution.py:118
  90.9 7.9 %collective-permute-start.20 = (f32[32,2048]{1,0:T(8,128)}, f32[32,2048]{1,0:T(8,128)}, u32[]{:S(2)}, u32[]{:S(2)}) collective-permute-start(f32[32,2048]{1,0:T(8,128)} %get-tuple-element.81), channel_id=1, source_target_pairs={{0,2},{2,4},{4,6},{6,8},{8,10},{10,12},{12,14},{14,0},{1,3},{3,5},... | collective-permute-start | bytes 786440 | tf_op jit(solution)/shard_map/ppermute | solution.py:118
  90.9 7.9 %collective-permute-start.21 = (f32[32,2048]{1,0:T(8,128)}, f32[32,2048]{1,0:T(8,128)}, u32[]{:S(2)}, u32[]{:S(2)}) collective-permute-start(f32[32,2048]{1,0:T(8,128)} %get-tuple-element.80), channel_id=1, source_target_pairs={{0,14},{2,0},{4,2},{6,4},{8,6},{10,8},{12,10},{14,12},{1,15},{3,1}... | collective-permute-start | bytes 786440 | tf_op jit(solution)/shard_map/ppermute | solution.py:118
  95.0 9.7 %collective-permute-start.24 = (f32[32,2048]{1,0:T(8,128)S(1)}, f32[32,2048]{1,0:T(8,128)S(1)}, u32[]{:S(2)}, u32[]{:S(2)}) collective-permute-start(f32[32,2048]{1,0:T(8,128)S(1)} %get-tuple-element.79), channel_id=1, source_target_pairs={{0,2},{2,4},{4,6},{6,8},{8,10},{10,12},{12,14},{14,0},{1,3},{3,5},... | collective-permute-start | bytes 786440 | tf_op jit(solution)/shard_map/ppermute | solution.py:118
  95.1 9.6 %collective-permute-start.25 = (f32[32,2048]{1,0:T(8,128)S(1)}, f32[32,2048]{1,0:T(8,128)S(1)}, u32[]{:S(2)}, u32[]{:S(2)}) collective-permute-start(f32[32,2048]{1,0:T(8,128)S(1)} %get-tuple-element.78), channel_id=1, source_target_pairs={{0,14},{2,0},{4,2},{6,4},{8,6},{10,8},{12,10},{14,12},{1,15},{3,1}... | collective-permute-start | bytes 786440 | tf_op jit(solution)/shard_map/ppermute | solution.py:118
  100.0 5.9 %copy-start.9 = (f32[32,2048]{1,0:T(8,128)}, f32[32,2048]{1,0:T(8,128)S(1)}, u32[]{:S(2)}) copy-start(f32[32,2048]{1,0:T(8,128)S(1)} %fusion.72) | copy-start | bytes 786436
  107.6 58.2 %copy-start.1 = (bf16[1,512,512]{2,1,0:T(8,128)(2,1)S(1)}, bf16[1,512,512]{2,1,0:T(8,128)(2,1)}, u32[]{:S(2)}) copy-start(bf16[1,512,512]{2,1,0:T(8,128)(2,1)} %param.7) | copy-start | bytes 1572868
  138.4 23.8 %copy-start.3 = (f32[16,32,512]{2,1,0:T(8,128)}, f32[16,32,512]{2,1,0:T(8,128)S(1)}, u32[]{:S(2)}) copy-start(f32[16,32,512]{2,1,0:T(8,128)S(1)} %all_to_all.21.pieces_ref) | copy-start | bytes 3145732
  139.3 22.9 %all-to-all-start.3 = ((f32[16,1,128]{2,1,0:T(1,128)}), f32[16,1,128]{2,1,0:T(1,128)S(1)}, u32[]{:S(2)}, u32[]{:S(2)}) async-start(f32[16,1,128]{2,1,0:T(1,128)} %broadcast_in_dim.32), calls=%async_computation.3 | async-start | bytes 16384 | tf_op jit(solution)/shard_map/all_to_all | solution.py:160
  162.2 0.6 copy-start.11

commit v8 on v5

--- a/solution.py
+++ b/solution.py
@@ -61,16 +61,16 @@
 
 
 def finish(squares, pieces, anchor, outer_momentum):
-    replicas, _, piece = pieces.shape
-    parts = 2
-    part = pl.BlockSpec((ROWS_DEV, D // parts), lambda h: (0, h))
+    replicas, _, both = pieces.shape
+    blocks = 2
+    part = pl.BlockSpec((ROWS_DEV, WIDTH // blocks), lambda h, q: (0, h * blocks + q))
     shape = jax.ShapeDtypeStruct(anchor.shape, jnp.float32)
     return pl.pallas_call(
         finish_kernel,
-        grid=(parts,),
+        grid=(CHUNKS, blocks),
         in_specs=[
-            pl.BlockSpec(squares.shape, lambda h: (0, 0, 0)),
-            pl.BlockSpec((replicas // parts, ROWS_DEV, piece), lambda h: (h, 0, 0)),
+            pl.BlockSpec(squares.shape, lambda h, q: (0, 0, 0)),
+            pl.BlockSpec((replicas // blocks, ROWS_DEV, both // CHUNKS), lambda h, q: (q, 0, h)),
             part,
             part,
         ],
@@ -117,37 +117,50 @@
     last = (up[-1], down[-1])
     lhs = after(ordered[stay:], sent, last)
     kept = [product(lhs, cols[k]) for k in chunks]
-    for t in range(1, 5):
+    for t in range(1, 4):
         for k in chunks:
             moved = (lax.ppermute(up[k], "z", UP), lax.ppermute(down[k], "z", DOWN))
             u, d = after(moved, last)
             if t == 1:
                 up[k] = jnp.concatenate([own(k, 3, 0, HALF), own(k, 3, HALF, WIDTH) + u], axis=1)
                 down[k] = jnp.concatenate([own(k, 5, 0, HALF) + d, own(k, 5, HALF, WIDTH)], axis=1)
-            elif t < 4:
+            else:
                 up[k] = own(k, 4 - t) + u
                 down[k] = own(k, 4 + t) + d
-            else:
-                up[k] = down[k] = own(k, 0) + u + d
             last = (up[k], down[k])
 
-    gradient = jnp.concatenate(up, axis=1)
     correction_one = 1.0 - beta_first**INNER_STEP
     correction_two = 1.0 - beta_second**INNER_STEP
-    own_drift = drift[0]
-    moment_one = beta_first * adam_first[0] + (1.0 - beta_first) * gradient
-    moment_two = beta_second * adam_second[0] + (1.0 - beta_second) * gradient * gradient
-    update = moment_one / correction_one / (
-        jnp.sqrt(moment_two / correction_two) + 1e-08
-    ) + decay_weight * (anchor + own_drift)
-    pseudo = inner_rate * update - own_drift
+    replicas = Y * X
+    piece = WIDTH // replicas
 
-    replicas = Y * X
-    piece = D // replicas
-    spread = pseudo.reshape(ROWS_DEV, replicas, piece).transpose(1, 0, 2)
+    def moments(first_old, second_old, gradient):
+        moment_one = beta_first * first_old + (1.0 - beta_first) * gradient
+        moment_two = beta_second * second_old + (1.0 - beta_second) * gradient * gradient
+        return moment_one, moment_two
+
+    def pseudo_of(k, gradient):
+        at = slice(k * WIDTH, (k + 1) * WIDTH)
+        own_drift = drift[0, :, at]
+        moment_one, moment_two = moments(adam_first[0, :, at], adam_second[0, :, at], gradient)
+        update = moment_one / correction_one / (
+            jnp.sqrt(moment_two / correction_two) + 1e-08
+        ) + decay_weight * (anchor[:, at] + own_drift)
+        pseudo = inner_rate * update - own_drift
+        return pseudo.reshape(ROWS_DEV, replicas, piece).transpose(1, 0, 2)
+
+    gradients = []
+    spread = []
+    for k in chunks:
+        moved = (lax.ppermute(up[k], "z", UP), lax.ppermute(down[k], "z", DOWN))
+        u, d = after(moved, last, spread)
+        gradients.append(own(k, 0) + u + d)
+        spread.append(pseudo_of(k, gradients[k]))
+    moment_one, moment_two = moments(adam_first[0], adam_second[0], jnp.concatenate(gradients, axis=1))
+    spread = jnp.concatenate(spread, axis=2)
     met = lax.all_to_all(spread, ("y", "x"), split_axis=0, concat_axis=0, tiled=True)
     part = jnp.sum(met, axis=0) / replicas
-    copies = jnp.broadcast_to(part[None], (replicas, ROWS_DEV, piece))
+    copies = jnp.broadcast_to(part[None], (replicas,) + part.shape)
     pieces = lax.all_to_all(copies, ("y", "x"), split_axis=0, concat_axis=0, tiled=True)
     squares = jnp.sum(jnp.sum(pieces * pieces, axis=(0, 1)).reshape(-1, 128), axis=0)
     squares = jnp.broadcast_to(squares, (PARTS, 1, 128))

time: 159 us -> 160 us (level)
    add x3 -> x1, other arithmetic: 3.43 us -> 3 us  [moments(): beta_second * second_old + (1.0 - beta_second) * gradient * gradient]
where the time goes in v8:
time: 160 us
  waiting for transfers between devices  58.6 us (37%)
  blocking collectives  41 us (26%)
  starting transfers between devices  36.6 us (23%)
  matrix products  6.39 us (4%)
  other arithmetic  6.35 us (4%)
  local copies, waits for them, and re-layouts  5.64 us (4%)
  Pallas kernels  4.28 us (3%)
    ppermute x16, waiting for transfers between devices, per_device(): moved = (lax.ppermute(up[k], 'z', UP), lax.ppermute(down[k], 'z', DOWN))  53.8 us
    ppermute x16, starting transfers between devices, per_device(): moved = (lax.ppermute(up[k], 'z', UP), lax.ppermute(down[k], 'z', DOWN))  24.7 us
    all_to_all x1, blocking collectives, per_device(): lax.all_to_all(spread, ('y', 'x'), split_axis=0, concat_axis=0, tiled=True)  22.8 us
    all_to_all x1, blocking collectives, per_device(): lax.all_to_all(copies, ('y', 'x'), split_axis=0, concat_axis=0, tiled=True)  18.3 us
    all_to_all x1, starting transfers between devices, per_device(): lax.all_to_all(squares, ('z', 'c'), split_axis=0, concat_axis=0, tiled=True)  8.2 us
    dot_general x4, matrix products, product(): lax.dot_general(lhs, rhs, (((1,), (0,)), ((), ())), preferred_element_typ...  5.88 us
    unnamed x18, local copies, waits for them, and re-layouts  4.49 us
    pallas_call x1, Pallas kernels, finish(): pl.pallas_call(finish_kernel, grid=(CHUNKS, blocks), in_specs=[pl.BlockSp...  4.28 us
  transfers between devices with their start and end apart: 19, of which 11 were waited for; matrix products, arithmetic and copies ran while one was open for 6% of the time, Pallas kernels for 0%

profile of v8, /device:TPU:1, one launch (start us, length us, event | category | flops | bytes accessed | tf_op | source)
XLA Modules:
  0.0 159.9 jit_solution(11857812157112075228)
XLA Ops:
  0.7 1.0 copy-done
  1.7 0.5 convolution_convert_fusion
  2.2 2.9 %copy-done.2 = bf16[1,512,8192]{2,1,0:T(8,128)(2,1)S(1)} copy-done((bf16[1,512,8192]{2,1,0:T(8,128)(2,1)S(1)}, bf16[1,512,8192]{2,1,0:T(8,128)(2,1)}, u32[]{:S(2)}) %copy-start.2) | copy-done | bytes 8388632
  5.1 1.6 fusion.71
  6.7 3.3 %collective-permute-start = (f32[32,8192]{1,0:T(8,128)S(1)}, f32[32,8192]{1,0:T(8,128)S(1)}, u32[]{:S(2)}, u32[]{:S(2)}) collective-permute-start(f32[32,8192]{1,0:T(8,128)S(1)} %slice.223), channel_id=1, source_target_pairs={{0,1},{1,0},{2,3},{3,2},{4,5},{5,4},{6,7},{7,6},{8,9},{9,8},{10,11... | collective-permute-start | bytes 3145736 | tf_op jit(solution)/shard_map/ppermute | solution.py:109
  10.1 2.1 %fusion.79 = f32[224,8192]{1,0:T(8,128)S(1)} fusion(bf16[224,512]{1,0:T(8,128)(2,1)S(1)} %get-tuple-element.26, bf16[1,512,8192]{2,1,0:T(8,128)(2,1)S(1)} %copy-done.2), kind=kOutput, calls=%fused_computation.132 | convolution fusion | flops 1879048192 | bytes 15958016 | tf_op jit(solution)/shard_map/dot_general | solution.py:92
  12.2 0.2 collective-permute-done
  12.3 0.4 collective-permute-start.1
  12.7 0.1 slice_add_fusion
  12.9 3.9 %collective-permute-start.3 = (f32[32,2048]{1,0:T(8,128)S(1)}, f32[32,2048]{1,0:T(8,128)S(1)}, u32[]{:S(2)}, u32[]{:S(2)}) collective-permute-start(f32[32,2048]{1,0:T(8,128)S(1)} %get-tuple-element.72), channel_id=1, source_target_pairs={{0,14},{2,0},{4,2},{6,4},{8,6},{10,8},{12,10},{14,12},{1,15},{3,1}... | collective-permute-start | bytes 786440 | tf_op jit(solution)/shard_map/ppermute | solution.py:122
  17.0 2.7 %collective-permute-start.7 = (f32[32,2048]{1,0:T(8,128)S(1)}, f32[32,2048]{1,0:T(8,128)S(1)}, u32[]{:S(2)}, u32[]{:S(2)}) collective-permute-start(f32[32,2048]{1,0:T(8,128)S(1)} %get-tuple-element.70), channel_id=1, source_target_pairs={{0,14},{2,0},{4,2},{6,4},{8,6},{10,8},{12,10},{14,12},{1,15},{3,1}... | collective-permute-start | bytes 786440 | tf_op jit(solution)/shard_map/ppermute | solution.py:122
  19.7 1.1 fusion.2
  20.8 1.1 fusion
  21.9 1.4 collective-permute-done.2
  23.3 0.7 collective-permute-done.1
  24.0 0.1 fusion.69
  24.3 3.9 %collective-permute-start.5 = (f32[32,4096]{1,0:T(8,128)S(1)}, f32[32,4096]{1,0:T(8,128)S(1)}, u32[]{:S(2)}, u32[]{:S(2)}) collective-permute-start(f32[32,4096]{1,0:T(8,128)S(1)} %pad_maximum_fusion.3), channel_id=1, source_target_pairs={{0,14},{2,0},{4,2},{6,4},{8,6},{10,8},{12,10},{14,12},{1,15},{3,1}... | collective-permute-start | bytes 1572872 | tf_op jit(solution)/shard_map/ppermute | solution.py:122
  28.2 0.7 collective-permute-done.6
  28.9 0.1 fusion.67
  29.1 0.3 collective-permute-start.10
  29.4 2.7 %collective-permute-start.11 = (f32[32,4096]{1,0:T(8,128)S(1)}, f32[32,4096]{1,0:T(8,128)S(1)}, u32[]{:S(2)}, u32[]{:S(2)}) collective-permute-start(f32[32,4096]{1,0:T(8,128)S(1)} %pad_maximum_fusion.5), channel_id=1, source_target_pairs={{0,14},{2,0},{4,2},{6,4},{8,6},{10,8},{12,10},{14,12},{1,15},{3,1}... | collective-permute-start | bytes 1572872 | tf_op jit(solution)/shard_map/ppermute | solution.py:122
  32.2 7.9 %collective-permute-done.4 = f32[32,4096]{1,0:T(8,128)S(1)} collective-permute-done((f32[32,4096]{1,0:T(8,128)S(1)}, f32[32,4096]{1,0:T(8,128)S(1)}, u32[]{:S(2)}, u32[]{:S(2)}) %collective-permute-start.4) | collective-permute-done | bytes 524320 | tf_op jit(solution)/shard_map/ppermute | solution.py:122
  40.1 0.2 fusion.35
  40.4 2.7 %collective-permute-start.9 = (f32[32,4096]{1,0:T(8,128)S(1)}, f32[32,4096]{1,0:T(8,128)S(1)}, u32[]{:S(2)}, u32[]{:S(2)}) collective-permute-start(f32[32,4096]{1,0:T(8,128)S(1)} %get-tuple-element.58), channel_id=1, source_target_pairs={{0,14},{2,0},{4,2},{6,4},{8,6},{10,8},{12,10},{14,12},{1,15},{3,1}... | collective-permute-start | bytes 1572872 | tf_op jit(solution)/shard_map/ppermute | solution.py:122
  43.1 8.2 %collective-permute-done.10 = f32[32,4096]{1,0:T(8,128)S(1)} collective-permute-done((f32[32,4096]{1,0:T(8,128)S(1)}, f32[32,4096]{1,0:T(8,128)S(1)}, u32[]{:S(2)}, u32[]{:S(2)}) %collective-permute-start.10) | collective-permute-done | bytes 524320 | tf_op jit(solution)/shard_map/ppermute | solution.py:122
  51.3 0.2 fusion.33
  51.6 2.7 %collective-permute-start.15 = (f32[32,4096]{1,0:T(8,128)S(1)}, f32[32,4096]{1,0:T(8,128)S(1)}, u32[]{:S(2)}, u32[]{:S(2)}) collective-permute-start(f32[32,4096]{1,0:T(8,128)S(1)} %get-tuple-element.56), channel_id=1, source_target_pairs={{0,14},{2,0},{4,2},{6,4},{8,6},{10,8},{12,10},{14,12},{1,15},{3,1}... | collective-permute-start | bytes 1572872 | tf_op jit(solution)/shard_map/ppermute | solution.py:122
  54.2 8.3 %collective-permute-done.8 = f32[32,4096]{1,0:T(8,128)S(1)} collective-permute-done((f32[32,4096]{1,0:T(8,128)S(1)}, f32[32,4096]{1,0:T(8,128)S(1)}, u32[]{:S(2)}, u32[]{:S(2)}) %collective-permute-start.8) | collective-permute-done | bytes 524320 | tf_op jit(solution)/shard_map/ppermute | solution.py:122
  62.6 0.2 fusion.32
  62.8 2.7 %collective-permute-start.13 = (f32[32,4096]{1,0:T(8,128)S(1)}, f32[32,4096]{1,0:T(8,128)S(1)}, u32[]{:S(2)}, u32[]{:S(2)}) collective-permute-start(f32[32,4096]{1,0:T(8,128)S(1)} %get-tuple-element.54), channel_id=1, source_target_pairs={{0,14},{2,0},{4,2},{6,4},{8,6},{10,8},{12,10},{14,12},{1,15},{3,1}... | collective-permute-start | bytes 1572872 | tf_op jit(solution)/shard_map/ppermute | solution.py:155
  65.5 8.3 %collective-permute-done.14 = f32[32,4096]{1,0:T(8,128)S(1)} collective-permute-done((f32[32,4096]{1,0:T(8,128)S(1)}, f32[32,4096]{1,0:T(8,128)S(1)}, u32[]{:S(2)}, u32[]{:S(2)}) %collective-permute-start.14) | collective-permute-done | bytes 524320 | tf_op jit(solution)/shard_map/ppermute | solution.py:122
  73.8 0.2 fusion.30
  74.1 2.7 %collective-permute-start.17 = (f32[32,4096]{1,0:T(8,128)S(1)}, f32[32,4096]{1,0:T(8,128)S(1)}, u32[]{:S(2)}, u32[]{:S(2)}) collective-permute-start(f32[32,4096]{1,0:T(8,128)S(1)} %get-tuple-element.52), channel_id=1, source_target_pairs={{0,14},{2,0},{4,2},{6,4},{8,6},{10,8},{12,10},{14,12},{1,15},{3,1}... | collective-permute-start | bytes 1572872 | tf_op jit(solution)/shard_map/ppermute | solution.py:155
  76.7 8.3 %collective-permute-done.12 = f32[32,4096]{1,0:T(8,128)S(1)} collective-permute-done((f32[32,4096]{1,0:T(8,128)S(1)}, f32[32,4096]{1,0:T(8,128)S(1)}, u32[]{:S(2)}, u32[]{:S(2)}) %collective-permute-start.12) | collective-permute-done | bytes 524320 | tf_op jit(solution)/shard_map/ppermute | solution.py:155
  85.1 0.5 bitcast_subtract_fusion.1
  85.6 10.7 %collective-permute-done.16 = f32[32,4096]{1,0:T(8,128)S(1)} collective-permute-done((f32[32,4096]{1,0:T(8,128)S(1)}, f32[32,4096]{1,0:T(8,128)S(1)}, u32[]{:S(2)}, u32[]{:S(2)}) %collective-permute-start.16) | collective-permute-done | bytes 524320 | tf_op jit(solution)/shard_map/ppermute | solution.py:155
  96.3 1.2 bitcast_subtract_fusion
  97.6 0.1 pad_maximum_fusion.1
  97.7 22.8 %all_to_all.15 = f32[16,32,512]{2,1,0:T(8,128)S(1)} all-to-all(f32[16,32,512]{2,1,0:T(8,128)S(1)} %pad_maximum_fusion.1), channel_id=1, replica_groups=mesh['y'=4,'x'=4,'z'=8,'c'=2] {'y','x'}, dimensions={0} | all-to-all | bytes 2097152 | tf_op jit(solution)/shard_map/all_to_all | solution.py:161
  120.5 0.1 broadcast_in_dim.31
  120.7 18.3 %all_to_all.16.pieces_ref = f32[16,32,512]{2,1,0:T(8,128)S(1)} all-to-all(f32[16,32,512]{2,1,0:T(8,128)S(1)} %broadcast_in_dim.31), channel_id=1, replica_groups=mesh['y'=4,'x'=4,'z'=8,'c'=2] {'y','x'}, dimensions={0} | all-to-all | bytes 2097152 | tf_op jit(solution)/shard_map/all_to_all | solution.py:164
  139.0 0.1 multiply_reduce_fusion
  139.1 0.8 broadcast_in_dim.32
  139.9 8.2 %all-to-all-start.2 = ((f32[16,1,128]{2,1,0:T(1,128)}), f32[16,1,128]{2,1,0:T(1,128)S(1)}, u32[]{:S(2)}, u32[]{:S(2)}) async-start(f32[16,1,128]{2,1,0:T(1,128)} %broadcast_in_dim.32), calls=%async_computation.2 | async-start | bytes 16384 | tf_op jit(solution)/shard_map/all_to_all | solution.py:167
  148.1 3.0 %fusion.12 = (f32[1,32,8192]{2,1,0:T(8,128)}, f32[1,32,8192]{2,1,0:T(8,128)}) fusion(f32[1,32,8192]{2,1,0:T(8,128)S(1)} %copy-done.4, f32[1,32,4096]{2,1,0:T(8,128)} %bitcast.74, f32[1,32,4096]{2,1,0:T(8,128)S(1)} %bitcast.73, f32[1,32,8192]{2,1,0:T(8,128)} %param.11), kind=kLoop, calls=%fused_computation.23 | loop fusion | flops 2097152 | bytes 5242880 | tf_op jit(solution)/shard_map/add | solution.py:139
  151.1 3.9 %all-to-all-done.2.squares_ref = f32[16,1,128]{2,1,0:T(1,128)S(1)} async-done(((f32[16,1,128]{2,1,0:T(1,128)}), f32[16,1,128]{2,1,0:T(1,128)S(1)}, u32[]{:S(2)}, u32[]{:S(2)}) %all-to-all-start.2) | async-done | bytes 8224 | tf_op jit(solution)/shard_map/all_to_all | solution.py:167
  155.0 0.6 copy-done.8
  155.6 4.3 %shard_map.102 = (f32[32,8192]{1,0:T(8,128)}, f32[32,8192]{1,0:T(8,128)}) custom-call(f32[16,1,128]{2,1,0:T(1,128)} %copy-done.8, f32[16,32,512]{2,1,0:T(8,128)} %copy-done.3, f32[32,8192]{1,0:T(8,128)} %anchor_ref.1, f32[32,8192]{1,0:T(8,128)} %momentum_ref.1), custom_call_target="tpu_custom_call" | custom-call | flops 1835008 | bytes 5242880 | tf_op jit(solution)/shard_map/pallas_call | solution.py:68
  (46 shorter events, 1.2 us)
Async XLA Ops:
  0.6 1.1 copy-start
  1.7 3.4 %copy-start.2 = (bf16[1,512,8192]{2,1,0:T(8,128)(2,1)S(1)}, bf16[1,512,8192]{2,1,0:T(8,128)(2,1)}, u32[]{:S(2)}) copy-start(bf16[1,512,8192]{2,1,0:T(8,128)(2,1)} %param.8) | copy-start | bytes 25165828
  6.7 5.6 %collective-permute-start = (f32[32,8192]{1,0:T(8,128)S(1)}, f32[32,8192]{1,0:T(8,128)S(1)}, u32[]{:S(2)}, u32[]{:S(2)}) collective-permute-start(f32[32,8192]{1,0:T(8,128)S(1)} %slice.223), channel_id=1, source_target_pairs={{0,1},{1,0},{2,3},{3,2},{4,5},{5,4},{6,7},{7,6},{8,9},{9,8},{10,11... | collective-permute-start | bytes 3145736 | tf_op jit(solution)/shard_map/ppermute | solution.py:109
  12.3 11.7 %collective-permute-start.1 = (f32[224,8192]{1,0:T(8,128)S(1)}, f32[224,8192]{1,0:T(8,128)S(1)}, u32[]{:S(2)}, u32[]{:S(2)}) collective-permute-start(f32[224,8192]{1,0:T(8,128)S(1)} %fusion.79), channel_id=1, source_target_pairs={{0,1},{1,0},{2,3},{3,2},{4,5},{5,4},{6,7},{7,6},{8,9},{9,8},{10,11... | collective-permute-start | bytes 22020104 | tf_op jit(solution)/shard_map/ppermute | solution.py:111
  12.9 10.5 %collective-permute-start.2 = (f32[32,2048]{1,0:T(8,128)S(1)}, f32[32,2048]{1,0:T(8,128)S(1)}, u32[]{:S(2)}, u32[]{:S(2)}) collective-permute-start(f32[32,2048]{1,0:T(8,128)S(1)} %get-tuple-element.73), channel_id=1, source_target_pairs={{0,2},{2,4},{4,6},{6,8},{8,10},{10,12},{12,14},{14,0},{1,3},{3,5},... | collective-permute-start | bytes 786440 | tf_op jit(solution)/shard_map/ppermute | solution.py:122
  12.9 10.4 %collective-permute-start.3 = (f32[32,2048]{1,0:T(8,128)S(1)}, f32[32,2048]{1,0:T(8,128)S(1)}, u32[]{:S(2)}, u32[]{:S(2)}) collective-permute-start(f32[32,2048]{1,0:T(8,128)S(1)} %get-tuple-element.72), channel_id=1, source_target_pairs={{0,14},{2,0},{4,2},{6,4},{8,6},{10,8},{12,10},{14,12},{1,15},{3,1}... | collective-permute-start | bytes 786440 | tf_op jit(solution)/shard_map/ppermute | solution.py:122
  16.9 12.0 %collective-permute-start.6 = (f32[32,2048]{1,0:T(8,128)S(1)}, f32[32,2048]{1,0:T(8,128)S(1)}, u32[]{:S(2)}, u32[]{:S(2)}) collective-permute-start(f32[32,2048]{1,0:T(8,128)S(1)} %get-tuple-element.71), channel_id=1, source_target_pairs={{0,2},{2,4},{4,6},{6,8},{8,10},{10,12},{12,14},{14,0},{1,3},{3,5},... | collective-permute-start | bytes 786440 | tf_op jit(solution)/shard_map/ppermute | solution.py:122
  17.0 11.9 %collective-permute-start.7 = (f32[32,2048]{1,0:T(8,128)S(1)}, f32[32,2048]{1,0:T(8,128)S(1)}, u32[]{:S(2)}, u32[]{:S(2)}) collective-permute-start(f32[32,2048]{1,0:T(8,128)S(1)} %get-tuple-element.70), channel_id=1, source_target_pairs={{0,14},{2,0},{4,2},{6,4},{8,6},{10,8},{12,10},{14,12},{1,15},{3,1}... | collective-permute-start | bytes 786440 | tf_op jit(solution)/shard_map/ppermute | solution.py:122
  24.2 15.9 %collective-permute-start.4 = (f32[32,4096]{1,0:T(8,128)S(1)}, f32[32,4096]{1,0:T(8,128)S(1)}, u32[]{:S(2)}, u32[]{:S(2)}) collective-permute-start(f32[32,4096]{1,0:T(8,128)S(1)} %pad_maximum_fusion.2), channel_id=1, source_target_pairs={{0,2},{2,4},{4,6},{6,8},{8,10},{10,12},{12,14},{14,0},{1,3},{3,5},... | collective-permute-start | bytes 1572872 | tf_op jit(solution)/shard_map/ppermute | solution.py:122
  24.3 15.8 %collective-permute-start.5 = (f32[32,4096]{1,0:T(8,128)S(1)}, f32[32,4096]{1,0:T(8,128)S(1)}, u32[]{:S(2)}, u32[]{:S(2)}) collective-permute-start(f32[32,4096]{1,0:T(8,128)S(1)} %pad_maximum_fusion.3), channel_id=1, source_target_pairs={{0,14},{2,0},{4,2},{6,4},{8,6},{10,8},{12,10},{14,12},{1,15},{3,1}... | collective-permute-start | bytes 1572872 | tf_op jit(solution)/shard_map/ppermute | solution.py:122
  29.1 22.2 %collective-permute-start.10 = (f32[32,4096]{1,0:T(8,128)S(1)}, f32[32,4096]{1,0:T(8,128)S(1)}, u32[]{:S(2)}, u32[]{:S(2)}) collective-permute-start(f32[32,4096]{1,0:T(8,128)S(1)} %pad_maximum_fusion.4), channel_id=1, source_target_pairs={{0,2},{2,4},{4,6},{6,8},{8,10},{10,12},{12,14},{14,0},{1,3},{3,5},... | collective-permute-start | bytes 1572872 | tf_op jit(solution)/shard_map/ppermute | solution.py:122
  29.4 21.9 %collective-permute-start.11 = (f32[32,4096]{1,0:T(8,128)S(1)}, f32[32,4096]{1,0:T(8,128)S(1)}, u32[]{:S(2)}, u32[]{:S(2)}) collective-permute-start(f32[32,4096]{1,0:T(8,128)S(1)} %pad_maximum_fusion.5), channel_id=1, source_target_pairs={{0,14},{2,0},{4,2},{6,4},{8,6},{10,8},{12,10},{14,12},{1,15},{3,1}... | collective-permute-start | bytes 1572872 | tf_op jit(solution)/shard_map/ppermute | solution.py:122
  40.3 44.7 %copy-start.4 = (f32[1,32,8192]{2,1,0:T(8,128)S(1)}, f32[1,32,8192]{2,1,0:T(8,128)}, u32[]{:S(2)}) copy-start(f32[1,32,8192]{2,1,0:T(8,128)} %param.12) | copy-start | bytes 3145732
  40.3 44.7 %copy-start.5 = (f32[1,32,8192]{2,1,0:T(8,128)S(1)}, f32[1,32,8192]{2,1,0:T(8,128)}, u32[]{:S(2)}) copy-start(f32[1,32,8192]{2,1,0:T(8,128)} %param.11) | copy-start | bytes 3145732
  40.3 44.7 %copy-start.6 = (f32[32,8192]{1,0:T(8,128)S(1)}, f32[32,8192]{1,0:T(8,128)}, u32[]{:S(2)}) copy-start(f32[32,8192]{1,0:T(8,128)} %anchor_ref.1) | copy-start | bytes 3145732
  40.3 44.7 %copy-start.7 = (f32[1,32,8192]{2,1,0:T(8,128)S(1)}, f32[1,32,8192]{2,1,0:T(8,128)}, u32[]{:S(2)}) copy-start(f32[1,32,8192]{2,1,0:T(8,128)} %param.10) | copy-start | bytes 3145732
  40.3 22.2 %collective-permute-start.8 = (f32[32,4096]{1,0:T(8,128)S(1)}, f32[32,4096]{1,0:T(8,128)S(1)}, u32[]{:S(2)}, u32[]{:S(2)}) collective-permute-start(f32[32,4096]{1,0:T(8,128)S(1)} %get-tuple-element.59), channel_id=1, source_target_pairs={{0,2},{2,4},{4,6},{6,8},{8,10},{10,12},{12,14},{14,0},{1,3},{3,5},... | collective-permute-start | bytes 1572872 | tf_op jit(solution)/shard_map/ppermute | solution.py:122
  40.4 22.1 %collective-permute-start.9 = (f32[32,4096]{1,0:T(8,128)S(1)}, f32[32,4096]{1,0:T(8,128)S(1)}, u32[]{:S(2)}, u32[]{:S(2)}) collective-permute-start(f32[32,4096]{1,0:T(8,128)S(1)} %get-tuple-element.58), channel_id=1, source_target_pairs={{0,14},{2,0},{4,2},{6,4},{8,6},{10,8},{12,10},{14,12},{1,15},{3,1}... | collective-permute-start | bytes 1572872 | tf_op jit(solution)/shard_map/ppermute | solution.py:122
  51.5 22.3 %collective-permute-start.14 = (f32[32,4096]{1,0:T(8,128)S(1)}, f32[32,4096]{1,0:T(8,128)S(1)}, u32[]{:S(2)}, u32[]{:S(2)}) collective-permute-start(f32[32,4096]{1,0:T(8,128)S(1)} %get-tuple-element.57), channel_id=1, source_target_pairs={{0,2},{2,4},{4,6},{6,8},{8,10},{10,12},{12,14},{14,0},{1,3},{3,5},... | collective-permute-start | bytes 1572872 | tf_op jit(solution)/shard_map/ppermute | solution.py:122
  51.6 22.2 %collective-permute-start.15 = (f32[32,4096]{1,0:T(8,128)S(1)}, f32[32,4096]{1,0:T(8,128)S(1)}, u32[]{:S(2)}, u32[]{:S(2)}) collective-permute-start(f32[32,4096]{1,0:T(8,128)S(1)} %get-tuple-element.56), channel_id=1, source_target_pairs={{0,14},{2,0},{4,2},{6,4},{8,6},{10,8},{12,10},{14,12},{1,15},{3,1}... | collective-permute-start | bytes 1572872 | tf_op jit(solution)/shard_map/ppermute | solution.py:122
  62.7 22.3 %collective-permute-start.12 = (f32[32,4096]{1,0:T(8,128)S(1)}, f32[32,4096]{1,0:T(8,128)S(1)}, u32[]{:S(2)}, u32[]{:S(2)}) collective-permute-start(f32[32,4096]{1,0:T(8,128)S(1)} %get-tuple-element.55), channel_id=1, source_target_pairs={{0,2},{2,4},{4,6},{6,8},{8,10},{10,12},{12,14},{14,0},{1,3},{3,5},... | collective-permute-start | bytes 1572872 | tf_op jit(solution)/shard_map/ppermute | solution.py:155
  62.8 22.2 %collective-permute-start.13 = (f32[32,4096]{1,0:T(8,128)S(1)}, f32[32,4096]{1,0:T(8,128)S(1)}, u32[]{:S(2)}, u32[]{:S(2)}) collective-permute-start(f32[32,4096]{1,0:T(8,128)S(1)} %get-tuple-element.54), channel_id=1, source_target_pairs={{0,14},{2,0},{4,2},{6,4},{8,6},{10,8},{12,10},{14,12},{1,15},{3,1}... | collective-permute-start | bytes 1572872 | tf_op jit(solution)/shard_map/ppermute | solution.py:155
  74.0 22.3 %collective-permute-start.16 = (f32[32,4096]{1,0:T(8,128)S(1)}, f32[32,4096]{1,0:T(8,128)S(1)}, u32[]{:S(2)}, u32[]{:S(2)}) collective-permute-start(f32[32,4096]{1,0:T(8,128)S(1)} %get-tuple-element.53), channel_id=1, source_target_pairs={{0,2},{2,4},{4,6},{6,8},{8,10},{10,12},{12,14},{14,0},{1,3},{3,5},... | collective-permute-start | bytes 1572872 | tf_op jit(solution)/shard_map/ppermute | solution.py:155
  74.1 22.2 %collective-permute-start.17 = (f32[32,4096]{1,0:T(8,128)S(1)}, f32[32,4096]{1,0:T(8,128)S(1)}, u32[]{:S(2)}, u32[]{:S(2)}) collective-permute-start(f32[32,4096]{1,0:T(8,128)S(1)} %get-tuple-element.52), channel_id=1, source_target_pairs={{0,14},{2,0},{4,2},{6,4},{8,6},{10,8},{12,10},{14,12},{1,15},{3,1}... | collective-permute-start | bytes 1572872 | tf_op jit(solution)/shard_map/ppermute | solution.py:155
  97.7 62.2 %copy-start.1 = (bf16[1,512,512]{2,1,0:T(8,128)(2,1)S(1)}, bf16[1,512,512]{2,1,0:T(8,128)(2,1)}, u32[]{:S(2)}) copy-start(bf16[1,512,512]{2,1,0:T(8,128)(2,1)} %param.7) | copy-start | bytes 1572868
  139.0 16.0 %copy-start.3 = (f32[16,32,512]{2,1,0:T(8,128)}, f32[16,32,512]{2,1,0:T(8,128)S(1)}, u32[]{:S(2)}) copy-start(f32[16,32,512]{2,1,0:T(8,128)S(1)} %all_to_all.16.pieces_ref) | copy-start | bytes 3145732
  139.9 15.1 %all-to-all-start.2 = ((f32[16,1,128]{2,1,0:T(1,128)}), f32[16,1,128]{2,1,0:T(1,128)S(1)}, u32[]{:S(2)}, u32[]{:S(2)}) async-start(f32[16,1,128]{2,1,0:T(1,128)} %broadcast_in_dim.32), calls=%async_computation.2 | async-start | bytes 16384 | tf_op jit(solution)/shard_map/all_to_all | solution.py:167
  155.0 0.6 copy-start.8

commit v9 on v5

--- a/solution.py
+++ b/solution.py
@@ -146,6 +146,10 @@
     piece = D // replicas
     spread = pseudo.reshape(ROWS_DEV, replicas, piece).transpose(1, 0, 2)
     met = lax.all_to_all(spread, ("y", "x"), split_axis=0, concat_axis=0, tiled=True)
+    gradient = after(gradient, spread)
+    moment_one = beta_first * adam_first[0] + (1.0 - beta_first) * gradient
+    moment_two = beta_second * adam_second[0] + (1.0 - beta_second) * gradient * gradient
+    moment_one, moment_two, met = lax.optimization_barrier((moment_one, moment_two, met))
     part = jnp.sum(met, axis=0) / replicas
     copies = jnp.broadcast_to(part[None], (replicas, ROWS_DEV, piece))
     pieces = lax.all_to_all(copies, ("y", "x"), split_axis=0, concat_axis=0, tiled=True)

time: 159 us -> 162 us (1.019)
  waiting for transfers between devices: 58.8 us -> 67.9 us
  blocking collectives: 41 us -> 34.5 us
  other arithmetic: 5.81 us -> 7.77 us
    all_to_all x1, waiting for transfers between devices: 3.79 us -> 12.9 us  [per_device(): lax.all_to_all(spread, ('y', 'x'), split_axis=0, concat_axis=0, tiled=True)]
    all_to_all x1, blocking collectives: 22.8 us -> 14.6 us  [per_device(): lax.all_to_all(squares, ('z', 'c'), split_axis=0, concat_axis=0, tiled=True)]
    unnamed x18 -> x16, local copies, waits for them, and re-layouts: 4.49 us -> 3.9 us
  transfers between devices with their start and end apart: 19 -> 19, of which waited for: 11 -> 11; matrix products, arithmetic and copies ran while one was open for 6% -> 5% of each run, Pallas kernels for 0% -> 0%
where the time goes in v9:
time: 162 us; the launch traced here: 161 us
  waiting for transfers between devices  67.9 us (42%)
  starting transfers between devices  35.2 us (22%)
  blocking collectives  34.5 us (21%)
  other arithmetic  7.77 us (5%)
  matrix products  6.46 us (4%)
  local copies, waits for them, and re-layouts  5.23 us (3%)
  Pallas kernels  3.11 us (2%)
    ppermute x16, waiting for transfers between devices, per_device(): moved = (lax.ppermute(up[k], 'z', UP), lax.ppermute(down[k], 'z', DOWN))  54.1 us
    ppermute x16, starting transfers between devices, per_device(): moved = (lax.ppermute(up[k], 'z', UP), lax.ppermute(down[k], 'z', DOWN))  24.7 us
    all_to_all x1, blocking collectives, per_device(): lax.all_to_all(copies, ('y', 'x'), split_axis=0, concat_axis=0, tiled=True)  19.8 us
    all_to_all x1, blocking collectives, per_device(): lax.all_to_all(squares, ('z', 'c'), split_axis=0, concat_axis=0, tiled=True)  14.6 us
    all_to_all x1, waiting for transfers between devices, per_device(): lax.all_to_all(spread, ('y', 'x'), split_axis=0, concat_axis=0, tiled=True)  12.9 us
    all_to_all x1, starting transfers between devices, per_device(): lax.all_to_all(spread, ('y', 'x'), split_axis=0, concat_axis=0, tiled=True)  6.8 us
    dot_general x4, matrix products, product(): lax.dot_general(lhs, rhs, (((1,), (0,)), ((), ())), preferred_element_typ...  5.95 us
    unnamed x16, local copies, waits for them, and re-layouts  3.9 us
  transfers between devices with their start and end apart: 19, of which 11 were waited for; matrix products, arithmetic and copies ran while one was open for 5% of the time, Pallas kernels for 0%

profile of v9, /device:TPU:1, one launch (start us, length us, event | category | flops | bytes accessed | tf_op | source)
XLA Modules:
  0.0 161.1 jit_solution(11779076306874913412)
XLA Ops:
  0.7 1.0 copy-done
  1.7 0.5 convolution_convert_fusion
  2.2 2.9 %copy-done.2 = bf16[1,512,8192]{2,1,0:T(8,128)(2,1)S(1)} copy-done((bf16[1,512,8192]{2,1,0:T(8,128)(2,1)S(1)}, bf16[1,512,8192]{2,1,0:T(8,128)(2,1)}, u32[]{:S(2)}) %copy-start.2) | copy-done | bytes 8388632
  5.1 1.6 %fusion.63 = f32[64,8192]{1,0:T(8,128)S(1)} fusion(bf16[512,512]{1,0:T(8,128)(2,1)S(1)} %convolution_convert_fusion, bf16[1,512,8192]{2,1,0:T(8,128)(2,1)S(1)} %copy-done.2), kind=kOutput, calls=%fused_computation.104 | convolution fusion | flops 536870912 | bytes 10551296 | tf_op jit(solution)/shard_map/dot_general | solution.py:92
  6.8 3.3 %collective-permute-start = (f32[32,8192]{1,0:T(8,128)S(1)}, f32[32,8192]{1,0:T(8,128)S(1)}, u32[]{:S(2)}, u32[]{:S(2)}) collective-permute-start(f32[32,8192]{1,0:T(8,128)S(1)} %slice.191), channel_id=1, source_target_pairs={{0,1},{1,0},{2,3},{3,2},{4,5},{5,4},{6,7},{7,6},{8,9},{9,8},{10,11... | collective-permute-start | bytes 3145736 | tf_op jit(solution)/shard_map/ppermute | solution.py:109
  10.1 2.1 %fusion.71 = f32[224,8192]{1,0:T(8,128)S(1)} fusion(bf16[224,512]{1,0:T(8,128)(2,1)S(1)} %get-tuple-element.30, bf16[1,512,8192]{2,1,0:T(8,128)(2,1)S(1)} %copy-done.2), kind=kOutput, calls=%fused_computation.118 | convolution fusion | flops 1879048192 | bytes 15958016 | tf_op jit(solution)/shard_map/dot_general | solution.py:92
  12.2 0.2 collective-permute-done
  12.4 0.4 collective-permute-start.1
  12.8 0.1 slice_add_fusion
  13.0 3.9 %collective-permute-start.3 = (f32[32,2048]{1,0:T(8,128)S(1)}, f32[32,2048]{1,0:T(8,128)S(1)}, u32[]{:S(2)}, u32[]{:S(2)}) collective-permute-start(f32[32,2048]{1,0:T(8,128)S(1)} %get-tuple-element.78), channel_id=1, source_target_pairs={{0,14},{2,0},{4,2},{6,4},{8,6},{10,8},{12,10},{14,12},{1,15},{3,1}... | collective-permute-start | bytes 786440 | tf_op jit(solution)/shard_map/ppermute | solution.py:122
  17.1 2.7 %collective-permute-start.7 = (f32[32,2048]{1,0:T(8,128)S(1)}, f32[32,2048]{1,0:T(8,128)S(1)}, u32[]{:S(2)}, u32[]{:S(2)}) collective-permute-start(f32[32,2048]{1,0:T(8,128)S(1)} %get-tuple-element.76), channel_id=1, source_target_pairs={{0,14},{2,0},{4,2},{6,4},{8,6},{10,8},{12,10},{14,12},{1,15},{3,1}... | collective-permute-start | bytes 786440 | tf_op jit(solution)/shard_map/ppermute | solution.py:122
  19.7 1.1 fusion.2
  20.8 1.1 fusion
  22.0 1.4 collective-permute-done.2
  23.4 0.7 collective-permute-done.1
  24.1 0.2 fusion.61
  24.4 3.9 %collective-permute-start.5 = (f32[32,4096]{1,0:T(8,128)S(1)}, f32[32,4096]{1,0:T(8,128)S(1)}, u32[]{:S(2)}, u32[]{:S(2)}) collective-permute-start(f32[32,4096]{1,0:T(8,128)S(1)} %pad_maximum_fusion.2), channel_id=1, source_target_pairs={{0,14},{2,0},{4,2},{6,4},{8,6},{10,8},{12,10},{14,12},{1,15},{3,1}... | collective-permute-start | bytes 1572872 | tf_op jit(solution)/shard_map/ppermute | solution.py:122
  28.3 0.7 collective-permute-done.6
  29.0 0.2 fusion.59
  29.2 0.3 collective-permute-start.10
  29.5 2.7 %collective-permute-start.11 = (f32[32,4096]{1,0:T(8,128)S(1)}, f32[32,4096]{1,0:T(8,128)S(1)}, u32[]{:S(2)}, u32[]{:S(2)}) collective-permute-start(f32[32,4096]{1,0:T(8,128)S(1)} %pad_maximum_fusion.4), channel_id=1, source_target_pairs={{0,14},{2,0},{4,2},{6,4},{8,6},{10,8},{12,10},{14,12},{1,15},{3,1}... | collective-permute-start | bytes 1572872 | tf_op jit(solution)/shard_map/ppermute | solution.py:122
  32.3 7.9 %collective-permute-done.4 = f32[32,4096]{1,0:T(8,128)S(1)} collective-permute-done((f32[32,4096]{1,0:T(8,128)S(1)}, f32[32,4096]{1,0:T(8,128)S(1)}, u32[]{:S(2)}, u32[]{:S(2)}) %collective-permute-start.4) | collective-permute-done | bytes 524320 | tf_op jit(solution)/shard_map/ppermute | solution.py:122
  40.2 0.2 fusion.31
  40.5 2.7 %collective-permute-start.9 = (f32[32,4096]{1,0:T(8,128)S(1)}, f32[32,4096]{1,0:T(8,128)S(1)}, u32[]{:S(2)}, u32[]{:S(2)}) collective-permute-start(f32[32,4096]{1,0:T(8,128)S(1)} %get-tuple-element.62), channel_id=1, source_target_pairs={{0,14},{2,0},{4,2},{6,4},{8,6},{10,8},{12,10},{14,12},{1,15},{3,1}... | collective-permute-start | bytes 1572872 | tf_op jit(solution)/shard_map/ppermute | solution.py:122
  43.1 8.3 %collective-permute-done.10 = f32[32,4096]{1,0:T(8,128)S(1)} collective-permute-done((f32[32,4096]{1,0:T(8,128)S(1)}, f32[32,4096]{1,0:T(8,128)S(1)}, u32[]{:S(2)}, u32[]{:S(2)}) %collective-permute-start.10) | collective-permute-done | bytes 524320 | tf_op jit(solution)/shard_map/ppermute | solution.py:122
  51.4 0.2 fusion.29
  51.7 2.7 %collective-permute-start.15 = (f32[32,4096]{1,0:T(8,128)S(1)}, f32[32,4096]{1,0:T(8,128)S(1)}, u32[]{:S(2)}, u32[]{:S(2)}) collective-permute-start(f32[32,4096]{1,0:T(8,128)S(1)} %get-tuple-element.60), channel_id=1, source_target_pairs={{0,14},{2,0},{4,2},{6,4},{8,6},{10,8},{12,10},{14,12},{1,15},{3,1}... | collective-permute-start | bytes 1572872 | tf_op jit(solution)/shard_map/ppermute | solution.py:122
  54.4 8.2 %collective-permute-done.8 = f32[32,4096]{1,0:T(8,128)S(1)} collective-permute-done((f32[32,4096]{1,0:T(8,128)S(1)}, f32[32,4096]{1,0:T(8,128)S(1)}, u32[]{:S(2)}, u32[]{:S(2)}) %collective-permute-start.8) | collective-permute-done | bytes 524320 | tf_op jit(solution)/shard_map/ppermute | solution.py:122
  62.6 0.2 fusion.28
  63.0 2.7 %collective-permute-start.13 = (f32[32,4096]{1,0:T(8,128)S(1)}, f32[32,4096]{1,0:T(8,128)S(1)}, u32[]{:S(2)}, u32[]{:S(2)}) collective-permute-start(f32[32,4096]{1,0:T(8,128)S(1)} %get-tuple-element.58), channel_id=1, source_target_pairs={{0,14},{2,0},{4,2},{6,4},{8,6},{10,8},{12,10},{14,12},{1,15},{3,1}... | collective-permute-start | bytes 1572872 | tf_op jit(solution)/shard_map/ppermute | solution.py:122
  65.6 8.3 %collective-permute-done.14 = f32[32,4096]{1,0:T(8,128)S(1)} collective-permute-done((f32[32,4096]{1,0:T(8,128)S(1)}, f32[32,4096]{1,0:T(8,128)S(1)}, u32[]{:S(2)}, u32[]{:S(2)}) %collective-permute-start.14) | collective-permute-done | bytes 524320 | tf_op jit(solution)/shard_map/ppermute | solution.py:122
  73.9 0.2 fusion.26
  74.2 2.7 %collective-permute-start.17 = (f32[32,4096]{1,0:T(8,128)S(1)}, f32[32,4096]{1,0:T(8,128)S(1)}, u32[]{:S(2)}, u32[]{:S(2)}) collective-permute-start(f32[32,4096]{1,0:T(8,128)S(1)} %get-tuple-element.56), channel_id=1, source_target_pairs={{0,14},{2,0},{4,2},{6,4},{8,6},{10,8},{12,10},{14,12},{1,15},{3,1}... | collective-permute-start | bytes 1572872 | tf_op jit(solution)/shard_map/ppermute | solution.py:122
  76.9 8.2 %collective-permute-done.12 = f32[32,4096]{1,0:T(8,128)S(1)} collective-permute-done((f32[32,4096]{1,0:T(8,128)S(1)}, f32[32,4096]{1,0:T(8,128)S(1)}, u32[]{:S(2)}, u32[]{:S(2)}) %collective-permute-start.12) | collective-permute-done | bytes 524320 | tf_op jit(solution)/shard_map/ppermute | solution.py:122
  85.1 0.1 fusion.35
  85.2 11.1 %collective-permute-done.16 = f32[32,4096]{1,0:T(8,128)S(1)} collective-permute-done((f32[32,4096]{1,0:T(8,128)S(1)}, f32[32,4096]{1,0:T(8,128)S(1)}, u32[]{:S(2)}, u32[]{:S(2)}) %collective-permute-start.16) | collective-permute-done | bytes 524320 | tf_op jit(solution)/shard_map/ppermute | solution.py:122
  96.4 0.1 fusion.25
  96.5 1.7 %bitcast_subtract_fusion = (f32[32,8192]{1,0:T(8,128)S(1)}, f32[32,8192]{1,0:T(8,128)}) fusion(f32[1,32,8192]{2,1,0:T(8,128)S(1)} %copy-done.7, f32[32,8192]{1,0:T(8,128)S(1)} %copy-done.6, f32[1,32,8192]{2,1,0:T(8,128)S(1)} %copy-done.4, f32[1,32,8192]{2,1,0:T(8,128)S(1)} %copy-done.5, f32[32,4096]{1,0:T(8,128)S(1)} %fusion.25, f32[32,4096]{1,0:T(8,128)S(1)} %fusion.35), kind=kLoop, calls=%fused_computation.35 | loop fusion | flops 4456448 | bytes 7340032 | tf_op jit(solution)/shard_map/sub | solution.py:143
  98.3 1.0 copy.15
  99.3 6.8 %all-to-all-start = ((f32[16,32,512]{2,1,0:T(8,128)}), f32[16,32,512]{2,1,0:T(8,128)}, u32[]{:S(2)}, u32[]{:S(2)}) async-start(f32[16,32,512]{2,1,0:T(8,128)} %bitcast.48), calls=%async_computation | async-start | bytes 2097152 | tf_op jit(solution)/shard_map/all_to_all | solution.py:148
  106.1 2.9 %fusion.18 = (f32[32,8192]{1,0:T(8,128)}, f32[32,8192]{1,0:T(8,128)}) fusion(f32[32,8192]{1,0:T(8,128)} %get-tuple-element.50, f32[1,32,8192]{2,1,0:T(8,128)S(1)} %copy-done.4, f32[1,32,8192]{2,1,0:T(8,128)S(1)} %copy-done.5), kind=kLoop, calls=%fused_computation.30 | loop fusion | flops 1835008 | bytes 5242880 | tf_op jit(solution)/shard_map/add | solution.py:151
  109.0 12.9 %all-to-all-done = f32[16,32,512]{2,1,0:T(8,128)} async-done(((f32[16,32,512]{2,1,0:T(8,128)}), f32[16,32,512]{2,1,0:T(8,128)}, u32[]{:S(2)}, u32[]{:S(2)}) %all-to-all-start) | async-done | bytes 1048608 | tf_op jit(solution)/shard_map/all_to_all | solution.py:148
  122.0 1.3 reduce_sum.27
  123.3 0.1 broadcast_in_dim.37
  123.4 19.8 %all_to_all.15.pieces_ref = f32[16,32,512]{2,1,0:T(8,128)S(1)} all-to-all(f32[16,32,512]{2,1,0:T(8,128)S(1)} %broadcast_in_dim.37), channel_id=1, replica_groups=mesh['y'=4,'x'=4,'z'=8,'c'=2] {'y','x'}, dimensions={0} | all-to-all | bytes 2097152 | tf_op jit(solution)/shard_map/all_to_all | solution.py:155
  143.2 0.1 multiply_reduce_fusion
  143.4 14.6 %all_to_all.16.squares_ref = f32[16,1,128]{2,1,0:T(1,128)} all-to-all(f32[16,1,128]{2,1,0:T(1,128)S(1)} %broadcast_in_dim.38), channel_id=1, replica_groups=mesh['y'=4,'x'=4,'z'=8,'c'=2] {'z','c'}, dimensions={0} | all-to-all | bytes 16384 | tf_op jit(solution)/shard_map/all_to_all | solution.py:158
  158.0 3.1 %shard_map.102 = (f32[32,8192]{1,0:T(8,128)}, f32[32,8192]{1,0:T(8,128)}) custom-call(f32[16,1,128]{2,1,0:T(1,128)} %all_to_all.16.squares_ref, f32[16,32,512]{2,1,0:T(8,128)} %copy-done.3, f32[32,8192]{1,0:T(8,128)} %anchor_ref.1, f32[32,8192]{1,0:T(8,128)} %momentum_ref.1), custom_call_target="tpu_custom_call" | custom-call | flops 1835008 | bytes 5242880 | tf_op jit(solution)/shard_map/pallas_call | solution.py:68
  (43 shorter events, 1.0 us)
Async XLA Ops:
  0.6 1.1 copy-start
  1.7 3.4 %copy-start.2 = (bf16[1,512,8192]{2,1,0:T(8,128)(2,1)S(1)}, bf16[1,512,8192]{2,1,0:T(8,128)(2,1)}, u32[]{:S(2)}) copy-start(bf16[1,512,8192]{2,1,0:T(8,128)(2,1)} %param.8) | copy-start | bytes 25165828
  6.8 5.6 %collective-permute-start = (f32[32,8192]{1,0:T(8,128)S(1)}, f32[32,8192]{1,0:T(8,128)S(1)}, u32[]{:S(2)}, u32[]{:S(2)}) collective-permute-start(f32[32,8192]{1,0:T(8,128)S(1)} %slice.191), channel_id=1, source_target_pairs={{0,1},{1,0},{2,3},{3,2},{4,5},{5,4},{6,7},{7,6},{8,9},{9,8},{10,11... | collective-permute-start | bytes 3145736 | tf_op jit(solution)/shard_map/ppermute | solution.py:109
  12.4 11.7 %collective-permute-start.1 = (f32[224,8192]{1,0:T(8,128)S(1)}, f32[224,8192]{1,0:T(8,128)S(1)}, u32[]{:S(2)}, u32[]{:S(2)}) collective-permute-start(f32[224,8192]{1,0:T(8,128)S(1)} %fusion.71), channel_id=1, source_target_pairs={{0,1},{1,0},{2,3},{3,2},{4,5},{5,4},{6,7},{7,6},{8,9},{9,8},{10,11... | collective-permute-start | bytes 22020104 | tf_op jit(solution)/shard_map/ppermute | solution.py:111
  12.9 10.5 %collective-permute-start.2 = (f32[32,2048]{1,0:T(8,128)S(1)}, f32[32,2048]{1,0:T(8,128)S(1)}, u32[]{:S(2)}, u32[]{:S(2)}) collective-permute-start(f32[32,2048]{1,0:T(8,128)S(1)} %get-tuple-element.79), channel_id=1, source_target_pairs={{0,2},{2,4},{4,6},{6,8},{8,10},{10,12},{12,14},{14,0},{1,3},{3,5},... | collective-permute-start | bytes 786440 | tf_op jit(solution)/shard_map/ppermute | solution.py:122
  13.0 10.4 %collective-permute-start.3 = (f32[32,2048]{1,0:T(8,128)S(1)}, f32[32,2048]{1,0:T(8,128)S(1)}, u32[]{:S(2)}, u32[]{:S(2)}) collective-permute-start(f32[32,2048]{1,0:T(8,128)S(1)} %get-tuple-element.78), channel_id=1, source_target_pairs={{0,14},{2,0},{4,2},{6,4},{8,6},{10,8},{12,10},{14,12},{1,15},{3,1}... | collective-permute-start | bytes 786440 | tf_op jit(solution)/shard_map/ppermute | solution.py:122
  17.0 12.0 %collective-permute-start.6 = (f32[32,2048]{1,0:T(8,128)S(1)}, f32[32,2048]{1,0:T(8,128)S(1)}, u32[]{:S(2)}, u32[]{:S(2)}) collective-permute-start(f32[32,2048]{1,0:T(8,128)S(1)} %get-tuple-element.77), channel_id=1, source_target_pairs={{0,2},{2,4},{4,6},{6,8},{8,10},{10,12},{12,14},{14,0},{1,3},{3,5},... | collective-permute-start | bytes 786440 | tf_op jit(solution)/shard_map/ppermute | solution.py:122
  17.1 11.9 %collective-permute-start.7 = (f32[32,2048]{1,0:T(8,128)S(1)}, f32[32,2048]{1,0:T(8,128)S(1)}, u32[]{:S(2)}, u32[]{:S(2)}) collective-permute-start(f32[32,2048]{1,0:T(8,128)S(1)} %get-tuple-element.76), channel_id=1, source_target_pairs={{0,14},{2,0},{4,2},{6,4},{8,6},{10,8},{12,10},{14,12},{1,15},{3,1}... | collective-permute-start | bytes 786440 | tf_op jit(solution)/shard_map/ppermute | solution.py:122
  24.3 15.9 %collective-permute-start.4 = (f32[32,4096]{1,0:T(8,128)S(1)}, f32[32,4096]{1,0:T(8,128)S(1)}, u32[]{:S(2)}, u32[]{:S(2)}) collective-permute-start(f32[32,4096]{1,0:T(8,128)S(1)} %pad_maximum_fusion.1), channel_id=1, source_target_pairs={{0,2},{2,4},{4,6},{6,8},{8,10},{10,12},{12,14},{14,0},{1,3},{3,5},... | collective-permute-start | bytes 1572872 | tf_op jit(solution)/shard_map/ppermute | solution.py:122
  24.4 15.8 %collective-permute-start.5 = (f32[32,4096]{1,0:T(8,128)S(1)}, f32[32,4096]{1,0:T(8,128)S(1)}, u32[]{:S(2)}, u32[]{:S(2)}) collective-permute-start(f32[32,4096]{1,0:T(8,128)S(1)} %pad_maximum_fusion.2), channel_id=1, source_target_pairs={{0,14},{2,0},{4,2},{6,4},{8,6},{10,8},{12,10},{14,12},{1,15},{3,1}... | collective-permute-start | bytes 1572872 | tf_op jit(solution)/shard_map/ppermute | solution.py:122
  29.2 22.2 %collective-permute-start.10 = (f32[32,4096]{1,0:T(8,128)S(1)}, f32[32,4096]{1,0:T(8,128)S(1)}, u32[]{:S(2)}, u32[]{:S(2)}) collective-permute-start(f32[32,4096]{1,0:T(8,128)S(1)} %pad_maximum_fusion.3), channel_id=1, source_target_pairs={{0,2},{2,4},{4,6},{6,8},{8,10},{10,12},{12,14},{14,0},{1,3},{3,5},... | collective-permute-start | bytes 1572872 | tf_op jit(solution)/shard_map/ppermute | solution.py:122
  29.5 21.9 %collective-permute-start.11 = (f32[32,4096]{1,0:T(8,128)S(1)}, f32[32,4096]{1,0:T(8,128)S(1)}, u32[]{:S(2)}, u32[]{:S(2)}) collective-permute-start(f32[32,4096]{1,0:T(8,128)S(1)} %pad_maximum_fusion.4), channel_id=1, source_target_pairs={{0,14},{2,0},{4,2},{6,4},{8,6},{10,8},{12,10},{14,12},{1,15},{3,1}... | collective-permute-start | bytes 1572872 | tf_op jit(solution)/shard_map/ppermute | solution.py:122
  40.4 22.3 %collective-permute-start.8 = (f32[32,4096]{1,0:T(8,128)S(1)}, f32[32,4096]{1,0:T(8,128)S(1)}, u32[]{:S(2)}, u32[]{:S(2)}) collective-permute-start(f32[32,4096]{1,0:T(8,128)S(1)} %get-tuple-element.63), channel_id=1, source_target_pairs={{0,2},{2,4},{4,6},{6,8},{8,10},{10,12},{12,14},{14,0},{1,3},{3,5},... | collective-permute-start | bytes 1572872 | tf_op jit(solution)/shard_map/ppermute | solution.py:122
  40.5 22.2 %collective-permute-start.9 = (f32[32,4096]{1,0:T(8,128)S(1)}, f32[32,4096]{1,0:T(8,128)S(1)}, u32[]{:S(2)}, u32[]{:S(2)}) collective-permute-start(f32[32,4096]{1,0:T(8,128)S(1)} %get-tuple-element.62), channel_id=1, source_target_pairs={{0,14},{2,0},{4,2},{6,4},{8,6},{10,8},{12,10},{14,12},{1,15},{3,1}... | collective-permute-start | bytes 1572872 | tf_op jit(solution)/shard_map/ppermute | solution.py:122
  51.6 44.9 %copy-start.4 = (f32[1,32,8192]{2,1,0:T(8,128)S(1)}, f32[1,32,8192]{2,1,0:T(8,128)}, u32[]{:S(2)}) copy-start(f32[1,32,8192]{2,1,0:T(8,128)} %param.12) | copy-start | bytes 3145732
  51.6 44.9 %copy-start.5 = (f32[1,32,8192]{2,1,0:T(8,128)S(1)}, f32[1,32,8192]{2,1,0:T(8,128)}, u32[]{:S(2)}) copy-start(f32[1,32,8192]{2,1,0:T(8,128)} %param.11) | copy-start | bytes 3145732
  51.6 44.9 %copy-start.6 = (f32[32,8192]{1,0:T(8,128)S(1)}, f32[32,8192]{1,0:T(8,128)}, u32[]{:S(2)}) copy-start(f32[32,8192]{1,0:T(8,128)} %anchor_ref.1) | copy-start | bytes 3145732
  51.6 44.9 %copy-start.7 = (f32[1,32,8192]{2,1,0:T(8,128)S(1)}, f32[1,32,8192]{2,1,0:T(8,128)}, u32[]{:S(2)}) copy-start(f32[1,32,8192]{2,1,0:T(8,128)} %param.10) | copy-start | bytes 3145732
  51.7 22.2 %collective-permute-start.14 = (f32[32,4096]{1,0:T(8,128)S(1)}, f32[32,4096]{1,0:T(8,128)S(1)}, u32[]{:S(2)}, u32[]{:S(2)}) collective-permute-start(f32[32,4096]{1,0:T(8,128)S(1)} %get-tuple-element.61), channel_id=1, source_target_pairs={{0,2},{2,4},{4,6},{6,8},{8,10},{10,12},{12,14},{14,0},{1,3},{3,5},... | collective-permute-start | bytes 1572872 | tf_op jit(solution)/shard_map/ppermute | solution.py:122
  51.7 22.1 %collective-permute-start.15 = (f32[32,4096]{1,0:T(8,128)S(1)}, f32[32,4096]{1,0:T(8,128)S(1)}, u32[]{:S(2)}, u32[]{:S(2)}) collective-permute-start(f32[32,4096]{1,0:T(8,128)S(1)} %get-tuple-element.60), channel_id=1, source_target_pairs={{0,14},{2,0},{4,2},{6,4},{8,6},{10,8},{12,10},{14,12},{1,15},{3,1}... | collective-permute-start | bytes 1572872 | tf_op jit(solution)/shard_map/ppermute | solution.py:122
  62.9 22.2 %collective-permute-start.12 = (f32[32,4096]{1,0:T(8,128)S(1)}, f32[32,4096]{1,0:T(8,128)S(1)}, u32[]{:S(2)}, u32[]{:S(2)}) collective-permute-start(f32[32,4096]{1,0:T(8,128)S(1)} %get-tuple-element.59), channel_id=1, source_target_pairs={{0,2},{2,4},{4,6},{6,8},{8,10},{10,12},{12,14},{14,0},{1,3},{3,5},... | collective-permute-start | bytes 1572872 | tf_op jit(solution)/shard_map/ppermute | solution.py:122
  63.0 22.2 %collective-permute-start.13 = (f32[32,4096]{1,0:T(8,128)S(1)}, f32[32,4096]{1,0:T(8,128)S(1)}, u32[]{:S(2)}, u32[]{:S(2)}) collective-permute-start(f32[32,4096]{1,0:T(8,128)S(1)} %get-tuple-element.58), channel_id=1, source_target_pairs={{0,14},{2,0},{4,2},{6,4},{8,6},{10,8},{12,10},{14,12},{1,15},{3,1}... | collective-permute-start | bytes 1572872 | tf_op jit(solution)/shard_map/ppermute | solution.py:122
  74.1 22.2 %collective-permute-start.16 = (f32[32,4096]{1,0:T(8,128)S(1)}, f32[32,4096]{1,0:T(8,128)S(1)}, u32[]{:S(2)}, u32[]{:S(2)}) collective-permute-start(f32[32,4096]{1,0:T(8,128)S(1)} %get-tuple-element.57), channel_id=1, source_target_pairs={{0,2},{2,4},{4,6},{6,8},{8,10},{10,12},{12,14},{14,0},{1,3},{3,5},... | collective-permute-start | bytes 1572872 | tf_op jit(solution)/shard_map/ppermute | solution.py:122
  74.2 22.1 %collective-permute-start.17 = (f32[32,4096]{1,0:T(8,128)S(1)}, f32[32,4096]{1,0:T(8,128)S(1)}, u32[]{:S(2)}, u32[]{:S(2)}) collective-permute-start(f32[32,4096]{1,0:T(8,128)S(1)} %get-tuple-element.56), channel_id=1, source_target_pairs={{0,14},{2,0},{4,2},{6,4},{8,6},{10,8},{12,10},{14,12},{1,15},{3,1}... | collective-permute-start | bytes 1572872 | tf_op jit(solution)/shard_map/ppermute | solution.py:122
  99.3 22.6 %all-to-all-start = ((f32[16,32,512]{2,1,0:T(8,128)}), f32[16,32,512]{2,1,0:T(8,128)}, u32[]{:S(2)}, u32[]{:S(2)}) async-start(f32[16,32,512]{2,1,0:T(8,128)} %bitcast.48), calls=%async_computation | async-start | bytes 2097152 | tf_op jit(solution)/shard_map/all_to_all | solution.py:148
  106.1 55.0 %copy-start.1 = (bf16[1,512,512]{2,1,0:T(8,128)(2,1)S(1)}, bf16[1,512,512]{2,1,0:T(8,128)(2,1)}, u32[]{:S(2)}) copy-start(bf16[1,512,512]{2,1,0:T(8,128)(2,1)} %param.7) | copy-start | bytes 1572868
  143.2 14.8 %copy-start.3 = (f32[16,32,512]{2,1,0:T(8,128)}, f32[16,32,512]{2,1,0:T(8,128)S(1)}, u32[]{:S(2)}) copy-start(f32[16,32,512]{2,1,0:T(8,128)S(1)} %all_to_all.15.pieces_ref) | copy-start | bytes 3145732

commit v10 on v5

--- a/solution.py
+++ b/solution.py
@@ -62,7 +62,7 @@
 
 def finish(squares, pieces, anchor, outer_momentum):
     replicas, _, piece = pieces.shape
-    parts = 2
+    parts = 1
     part = pl.BlockSpec((ROWS_DEV, D // parts), lambda h: (0, h))
     shape = jax.ShapeDtypeStruct(anchor.shape, jnp.float32)
     return pl.pallas_call(

time: 159 us -> 159 us (level)
  no operation moved by 1% of the time
where the time goes in v10:
time: 159 us
  waiting for transfers between devices  58.8 us (37%)
  blocking collectives  41 us (26%)
  starting transfers between devices  36.6 us (23%)
  matrix products  6.39 us (4%)
  other arithmetic  5.81 us (4%)
  local copies, waits for them, and re-layouts  5.62 us (4%)
  Pallas kernels  3.61 us (2%)
    ppermute x16, waiting for transfers between devices, per_device(): moved = (lax.ppermute(up[k], 'z', UP), lax.ppermute(down[k], 'z', DOWN))  54.2 us
    ppermute x16, starting transfers between devices, per_device(): moved = (lax.ppermute(up[k], 'z', UP), lax.ppermute(down[k], 'z', DOWN))  24.7 us
    all_to_all x1, blocking collectives, per_device(): lax.all_to_all(spread, ('y', 'x'), split_axis=0, concat_axis=0, tiled=True)  22.8 us
    all_to_all x1, blocking collectives, per_device(): lax.all_to_all(copies, ('y', 'x'), split_axis=0, concat_axis=0, tiled=True)  18.3 us
    all_to_all x1, starting transfers between devices, per_device(): lax.all_to_all(squares, ('z', 'c'), split_axis=0, concat_axis=0, tiled=True)  8.2 us
    dot_general x4, matrix products, product(): lax.dot_general(lhs, rhs, (((1,), (0,)), ((), ())), preferred_element_typ...  5.88 us
    unnamed x18, local copies, waits for them, and re-layouts  4.49 us
    all_to_all x1, waiting for transfers between devices, per_device(): lax.all_to_all(squares, ('z', 'c'), split_axis=0, concat_axis=0, tiled=True)  3.79 us
  transfers between devices with their start and end apart: 19, of which 11 were waited for; matrix products, arithmetic and copies ran while one was open for 6% of the time, Pallas kernels for 0%

profile of v10, /device:TPU:1, one launch (start us, length us, event | category | flops | bytes accessed | tf_op | source)
XLA Modules:
  0.0 158.9 jit_solution(2877233223763685447)
XLA Ops:
  0.7 1.0 copy-done
  1.7 0.5 convolution_convert_fusion
  2.2 2.9 %copy-done.2 = bf16[1,512,8192]{2,1,0:T(8,128)(2,1)S(1)} copy-done((bf16[1,512,8192]{2,1,0:T(8,128)(2,1)S(1)}, bf16[1,512,8192]{2,1,0:T(8,128)(2,1)}, u32[]{:S(2)}) %copy-start.2) | copy-done | bytes 8388632
  5.1 1.6 fusion.63
  6.7 3.3 %collective-permute-start = (f32[32,8192]{1,0:T(8,128)S(1)}, f32[32,8192]{1,0:T(8,128)S(1)}, u32[]{:S(2)}, u32[]{:S(2)}) collective-permute-start(f32[32,8192]{1,0:T(8,128)S(1)} %slice.191), channel_id=1, source_target_pairs={{0,1},{1,0},{2,3},{3,2},{4,5},{5,4},{6,7},{7,6},{8,9},{9,8},{10,11... | collective-permute-start | bytes 3145736 | tf_op jit(solution)/shard_map/ppermute | solution.py:109
  10.1 2.1 %fusion.71 = f32[224,8192]{1,0:T(8,128)S(1)} fusion(bf16[224,512]{1,0:T(8,128)(2,1)S(1)} %get-tuple-element.26, bf16[1,512,8192]{2,1,0:T(8,128)(2,1)S(1)} %copy-done.2), kind=kOutput, calls=%fused_computation.119 | convolution fusion | flops 1879048192 | bytes 15958016 | tf_op jit(solution)/shard_map/dot_general | solution.py:92
  12.2 0.2 collective-permute-done
  12.3 0.4 collective-permute-start.1
  12.7 0.1 slice_add_fusion
  12.9 3.9 %collective-permute-start.3 = (f32[32,2048]{1,0:T(8,128)S(1)}, f32[32,2048]{1,0:T(8,128)S(1)}, u32[]{:S(2)}, u32[]{:S(2)}) collective-permute-start(f32[32,2048]{1,0:T(8,128)S(1)} %get-tuple-element.68), channel_id=1, source_target_pairs={{0,14},{2,0},{4,2},{6,4},{8,6},{10,8},{12,10},{14,12},{1,15},{3,1}... | collective-permute-start | bytes 786440 | tf_op jit(solution)/shard_map/ppermute | solution.py:122
  17.0 2.7 %collective-permute-start.7 = (f32[32,2048]{1,0:T(8,128)S(1)}, f32[32,2048]{1,0:T(8,128)S(1)}, u32[]{:S(2)}, u32[]{:S(2)}) collective-permute-start(f32[32,2048]{1,0:T(8,128)S(1)} %get-tuple-element.66), channel_id=1, source_target_pairs={{0,14},{2,0},{4,2},{6,4},{8,6},{10,8},{12,10},{14,12},{1,15},{3,1}... | collective-permute-start | bytes 786440 | tf_op jit(solution)/shard_map/ppermute | solution.py:122
  19.7 1.1 fusion.2
  20.8 1.1 fusion
  21.9 1.4 collective-permute-done.2
  23.3 0.7 collective-permute-done.1
  24.0 0.1 fusion.61
  24.3 3.9 %collective-permute-start.5 = (f32[32,4096]{1,0:T(8,128)S(1)}, f32[32,4096]{1,0:T(8,128)S(1)}, u32[]{:S(2)}, u32[]{:S(2)}) collective-permute-start(f32[32,4096]{1,0:T(8,128)S(1)} %pad_maximum_fusion.3), channel_id=1, source_target_pairs={{0,14},{2,0},{4,2},{6,4},{8,6},{10,8},{12,10},{14,12},{1,15},{3,1}... | collective-permute-start | bytes 1572872 | tf_op jit(solution)/shard_map/ppermute | solution.py:122
  28.2 0.7 collective-permute-done.6
  28.9 0.1 fusion.59
  29.1 0.3 collective-permute-start.10
  29.4 2.7 %collective-permute-start.11 = (f32[32,4096]{1,0:T(8,128)S(1)}, f32[32,4096]{1,0:T(8,128)S(1)}, u32[]{:S(2)}, u32[]{:S(2)}) collective-permute-start(f32[32,4096]{1,0:T(8,128)S(1)} %pad_maximum_fusion.5), channel_id=1, source_target_pairs={{0,14},{2,0},{4,2},{6,4},{8,6},{10,8},{12,10},{14,12},{1,15},{3,1}... | collective-permute-start | bytes 1572872 | tf_op jit(solution)/shard_map/ppermute | solution.py:122
  32.2 7.9 %collective-permute-done.4 = f32[32,4096]{1,0:T(8,128)S(1)} collective-permute-done((f32[32,4096]{1,0:T(8,128)S(1)}, f32[32,4096]{1,0:T(8,128)S(1)}, u32[]{:S(2)}, u32[]{:S(2)}) %collective-permute-start.4) | collective-permute-done | bytes 524320 | tf_op jit(solution)/shard_map/ppermute | solution.py:122
  40.1 0.2 fusion.31
  40.4 2.7 %collective-permute-start.9 = (f32[32,4096]{1,0:T(8,128)S(1)}, f32[32,4096]{1,0:T(8,128)S(1)}, u32[]{:S(2)}, u32[]{:S(2)}) collective-permute-start(f32[32,4096]{1,0:T(8,128)S(1)} %get-tuple-element.54), channel_id=1, source_target_pairs={{0,14},{2,0},{4,2},{6,4},{8,6},{10,8},{12,10},{14,12},{1,15},{3,1}... | collective-permute-start | bytes 1572872 | tf_op jit(solution)/shard_map/ppermute | solution.py:122
  43.1 8.3 %collective-permute-done.10 = f32[32,4096]{1,0:T(8,128)S(1)} collective-permute-done((f32[32,4096]{1,0:T(8,128)S(1)}, f32[32,4096]{1,0:T(8,128)S(1)}, u32[]{:S(2)}, u32[]{:S(2)}) %collective-permute-start.10) | collective-permute-done | bytes 524320 | tf_op jit(solution)/shard_map/ppermute | solution.py:122
  51.3 0.2 fusion.29
  51.7 2.7 %collective-permute-start.15 = (f32[32,4096]{1,0:T(8,128)S(1)}, f32[32,4096]{1,0:T(8,128)S(1)}, u32[]{:S(2)}, u32[]{:S(2)}) collective-permute-start(f32[32,4096]{1,0:T(8,128)S(1)} %get-tuple-element.52), channel_id=1, source_target_pairs={{0,14},{2,0},{4,2},{6,4},{8,6},{10,8},{12,10},{14,12},{1,15},{3,1}... | collective-permute-start | bytes 1572872 | tf_op jit(solution)/shard_map/ppermute | solution.py:122
  54.3 8.2 %collective-permute-done.8 = f32[32,4096]{1,0:T(8,128)S(1)} collective-permute-done((f32[32,4096]{1,0:T(8,128)S(1)}, f32[32,4096]{1,0:T(8,128)S(1)}, u32[]{:S(2)}, u32[]{:S(2)}) %collective-permute-start.8) | collective-permute-done | bytes 524320 | tf_op jit(solution)/shard_map/ppermute | solution.py:122
  62.6 0.2 fusion.28
  62.8 2.7 %collective-permute-start.13 = (f32[32,4096]{1,0:T(8,128)S(1)}, f32[32,4096]{1,0:T(8,128)S(1)}, u32[]{:S(2)}, u32[]{:S(2)}) collective-permute-start(f32[32,4096]{1,0:T(8,128)S(1)} %get-tuple-element.50), channel_id=1, source_target_pairs={{0,14},{2,0},{4,2},{6,4},{8,6},{10,8},{12,10},{14,12},{1,15},{3,1}... | collective-permute-start | bytes 1572872 | tf_op jit(solution)/shard_map/ppermute | solution.py:122
  65.5 8.3 %collective-permute-done.14 = f32[32,4096]{1,0:T(8,128)S(1)} collective-permute-done((f32[32,4096]{1,0:T(8,128)S(1)}, f32[32,4096]{1,0:T(8,128)S(1)}, u32[]{:S(2)}, u32[]{:S(2)}) %collective-permute-start.14) | collective-permute-done | bytes 524320 | tf_op jit(solution)/shard_map/ppermute | solution.py:122
  73.8 0.2 fusion.26
  74.1 2.7 %collective-permute-start.17 = (f32[32,4096]{1,0:T(8,128)S(1)}, f32[32,4096]{1,0:T(8,128)S(1)}, u32[]{:S(2)}, u32[]{:S(2)}) collective-permute-start(f32[32,4096]{1,0:T(8,128)S(1)} %get-tuple-element.48), channel_id=1, source_target_pairs={{0,14},{2,0},{4,2},{6,4},{8,6},{10,8},{12,10},{14,12},{1,15},{3,1}... | collective-permute-start | bytes 1572872 | tf_op jit(solution)/shard_map/ppermute | solution.py:122
  76.8 8.3 %collective-permute-done.12 = f32[32,4096]{1,0:T(8,128)S(1)} collective-permute-done((f32[32,4096]{1,0:T(8,128)S(1)}, f32[32,4096]{1,0:T(8,128)S(1)}, u32[]{:S(2)}, u32[]{:S(2)}) %collective-permute-start.12) | collective-permute-done | bytes 524320 | tf_op jit(solution)/shard_map/ppermute | solution.py:122
  85.0 0.1 fusion.35
  85.2 11.1 %collective-permute-done.16 = f32[32,4096]{1,0:T(8,128)S(1)} collective-permute-done((f32[32,4096]{1,0:T(8,128)S(1)}, f32[32,4096]{1,0:T(8,128)S(1)}, u32[]{:S(2)}, u32[]{:S(2)}) %collective-permute-start.16) | collective-permute-done | bytes 524320 | tf_op jit(solution)/shard_map/ppermute | solution.py:122
  96.3 0.1 fusion.25
  96.4 0.8 bitcast_subtract_fusion
  97.4 22.8 %all_to_all.15 = f32[16,32,512]{2,1,0:T(8,128)S(1)} all-to-all(f32[16,32,512]{2,1,0:T(8,128)S(1)} %bitcast.47), channel_id=1, replica_groups=mesh['y'=4,'x'=4,'z'=8,'c'=2] {'y','x'}, dimensions={0} | all-to-all | bytes 2097152 | tf_op jit(solution)/shard_map/all_to_all | solution.py:148
  120.2 0.1 broadcast_in_dim.31
  120.3 18.3 %all_to_all.16.pieces_ref = f32[16,32,512]{2,1,0:T(8,128)S(1)} all-to-all(f32[16,32,512]{2,1,0:T(8,128)S(1)} %broadcast_in_dim.31), channel_id=1, replica_groups=mesh['y'=4,'x'=4,'z'=8,'c'=2] {'y','x'}, dimensions={0} | all-to-all | bytes 2097152 | tf_op jit(solution)/shard_map/all_to_all | solution.py:151
  138.6 0.1 multiply_reduce_fusion
  138.8 0.8 broadcast_in_dim.32
  139.5 8.2 %all-to-all-start.2 = ((f32[16,1,128]{2,1,0:T(1,128)}), f32[16,1,128]{2,1,0:T(1,128)S(1)}, u32[]{:S(2)}, u32[]{:S(2)}) async-start(f32[16,1,128]{2,1,0:T(1,128)} %broadcast_in_dim.32), calls=%async_computation.2 | async-start | bytes 16384 | tf_op jit(solution)/shard_map/all_to_all | solution.py:154
  147.7 3.2 %fusion.12 = (f32[1,32,8192]{2,1,0:T(8,128)}, f32[1,32,8192]{2,1,0:T(8,128)}) fusion(f32[1,32,8192]{2,1,0:T(8,128)} %param.12, f32[1,32,4096]{2,1,0:T(8,128)S(1)} %bitcast.46, f32[1,32,4096]{2,1,0:T(8,128)S(1)} %bitcast.45, f32[1,32,8192]{2,1,0:T(8,128)} %param.11), kind=kLoop, calls=%fused_computation.24 | loop fusion | flops 2097152 | bytes 5242880 | tf_op jit(solution)/shard_map/add | solution.py:139
  150.9 3.8 %all-to-all-done.2.squares_ref = f32[16,1,128]{2,1,0:T(1,128)S(1)} async-done(((f32[16,1,128]{2,1,0:T(1,128)}), f32[16,1,128]{2,1,0:T(1,128)S(1)}, u32[]{:S(2)}, u32[]{:S(2)}) %all-to-all-start.2) | async-done | bytes 8224 | tf_op jit(solution)/shard_map/all_to_all | solution.py:154
  154.7 0.6 copy-done.8
  155.3 3.6 %shard_map.102 = (f32[32,8192]{1,0:T(8,128)}, f32[32,8192]{1,0:T(8,128)}) custom-call(f32[16,1,128]{2,1,0:T(1,128)} %copy-done.8, f32[16,32,512]{2,1,0:T(8,128)} %copy-done.3, f32[32,8192]{1,0:T(8,128)} %anchor_ref.1, f32[32,8192]{1,0:T(8,128)} %momentum_ref.1), custom_call_target="tpu_custom_call" | custom-call | flops 1835008 | bytes 5242880 | tf_op jit(solution)/shard_map/pallas_call | solution.py:68
  (45 shorter events, 1.2 us)
Async XLA Ops:
  0.6 1.1 copy-start
  1.7 3.4 %copy-start.2 = (bf16[1,512,8192]{2,1,0:T(8,128)(2,1)S(1)}, bf16[1,512,8192]{2,1,0:T(8,128)(2,1)}, u32[]{:S(2)}) copy-start(bf16[1,512,8192]{2,1,0:T(8,128)(2,1)} %param.8) | copy-start | bytes 25165828
  6.7 5.6 %collective-permute-start = (f32[32,8192]{1,0:T(8,128)S(1)}, f32[32,8192]{1,0:T(8,128)S(1)}, u32[]{:S(2)}, u32[]{:S(2)}) collective-permute-start(f32[32,8192]{1,0:T(8,128)S(1)} %slice.191), channel_id=1, source_target_pairs={{0,1},{1,0},{2,3},{3,2},{4,5},{5,4},{6,7},{7,6},{8,9},{9,8},{10,11... | collective-permute-start | bytes 3145736 | tf_op jit(solution)/shard_map/ppermute | solution.py:109
  12.3 11.7 %collective-permute-start.1 = (f32[224,8192]{1,0:T(8,128)S(1)}, f32[224,8192]{1,0:T(8,128)S(1)}, u32[]{:S(2)}, u32[]{:S(2)}) collective-permute-start(f32[224,8192]{1,0:T(8,128)S(1)} %fusion.71), channel_id=1, source_target_pairs={{0,1},{1,0},{2,3},{3,2},{4,5},{5,4},{6,7},{7,6},{8,9},{9,8},{10,11... | collective-permute-start | bytes 22020104 | tf_op jit(solution)/shard_map/ppermute | solution.py:111
  12.9 10.5 %collective-permute-start.2 = (f32[32,2048]{1,0:T(8,128)S(1)}, f32[32,2048]{1,0:T(8,128)S(1)}, u32[]{:S(2)}, u32[]{:S(2)}) collective-permute-start(f32[32,2048]{1,0:T(8,128)S(1)} %get-tuple-element.69), channel_id=1, source_target_pairs={{0,2},{2,4},{4,6},{6,8},{8,10},{10,12},{12,14},{14,0},{1,3},{3,5},... | collective-permute-start | bytes 786440 | tf_op jit(solution)/shard_map/ppermute | solution.py:122
  12.9 10.4 %collective-permute-start.3 = (f32[32,2048]{1,0:T(8,128)S(1)}, f32[32,2048]{1,0:T(8,128)S(1)}, u32[]{:S(2)}, u32[]{:S(2)}) collective-permute-start(f32[32,2048]{1,0:T(8,128)S(1)} %get-tuple-element.68), channel_id=1, source_target_pairs={{0,14},{2,0},{4,2},{6,4},{8,6},{10,8},{12,10},{14,12},{1,15},{3,1}... | collective-permute-start | bytes 786440 | tf_op jit(solution)/shard_map/ppermute | solution.py:122
  16.9 12.0 %collective-permute-start.6 = (f32[32,2048]{1,0:T(8,128)S(1)}, f32[32,2048]{1,0:T(8,128)S(1)}, u32[]{:S(2)}, u32[]{:S(2)}) collective-permute-start(f32[32,2048]{1,0:T(8,128)S(1)} %get-tuple-element.67), channel_id=1, source_target_pairs={{0,2},{2,4},{4,6},{6,8},{8,10},{10,12},{12,14},{14,0},{1,3},{3,5},... | collective-permute-start | bytes 786440 | tf_op jit(solution)/shard_map/ppermute | solution.py:122
  17.0 11.9 %collective-permute-start.7 = (f32[32,2048]{1,0:T(8,128)S(1)}, f32[32,2048]{1,0:T(8,128)S(1)}, u32[]{:S(2)}, u32[]{:S(2)}) collective-permute-start(f32[32,2048]{1,0:T(8,128)S(1)} %get-tuple-element.66), channel_id=1, source_target_pairs={{0,14},{2,0},{4,2},{6,4},{8,6},{10,8},{12,10},{14,12},{1,15},{3,1}... | collective-permute-start | bytes 786440 | tf_op jit(solution)/shard_map/ppermute | solution.py:122
  24.2 15.9 %collective-permute-start.4 = (f32[32,4096]{1,0:T(8,128)S(1)}, f32[32,4096]{1,0:T(8,128)S(1)}, u32[]{:S(2)}, u32[]{:S(2)}) collective-permute-start(f32[32,4096]{1,0:T(8,128)S(1)} %pad_maximum_fusion.2), channel_id=1, source_target_pairs={{0,2},{2,4},{4,6},{6,8},{8,10},{10,12},{12,14},{14,0},{1,3},{3,5},... | collective-permute-start | bytes 1572872 | tf_op jit(solution)/shard_map/ppermute | solution.py:122
  24.3 15.8 %collective-permute-start.5 = (f32[32,4096]{1,0:T(8,128)S(1)}, f32[32,4096]{1,0:T(8,128)S(1)}, u32[]{:S(2)}, u32[]{:S(2)}) collective-permute-start(f32[32,4096]{1,0:T(8,128)S(1)} %pad_maximum_fusion.3), channel_id=1, source_target_pairs={{0,14},{2,0},{4,2},{6,4},{8,6},{10,8},{12,10},{14,12},{1,15},{3,1}... | collective-permute-start | bytes 1572872 | tf_op jit(solution)/shard_map/ppermute | solution.py:122
  29.1 22.2 %collective-permute-start.10 = (f32[32,4096]{1,0:T(8,128)S(1)}, f32[32,4096]{1,0:T(8,128)S(1)}, u32[]{:S(2)}, u32[]{:S(2)}) collective-permute-start(f32[32,4096]{1,0:T(8,128)S(1)} %pad_maximum_fusion.4), channel_id=1, source_target_pairs={{0,2},{2,4},{4,6},{6,8},{8,10},{10,12},{12,14},{14,0},{1,3},{3,5},... | collective-permute-start | bytes 1572872 | tf_op jit(solution)/shard_map/ppermute | solution.py:122
  29.4 21.9 %collective-permute-start.11 = (f32[32,4096]{1,0:T(8,128)S(1)}, f32[32,4096]{1,0:T(8,128)S(1)}, u32[]{:S(2)}, u32[]{:S(2)}) collective-permute-start(f32[32,4096]{1,0:T(8,128)S(1)} %pad_maximum_fusion.5), channel_id=1, source_target_pairs={{0,14},{2,0},{4,2},{6,4},{8,6},{10,8},{12,10},{14,12},{1,15},{3,1}... | collective-permute-start | bytes 1572872 | tf_op jit(solution)/shard_map/ppermute | solution.py:122
  40.3 22.3 %collective-permute-start.8 = (f32[32,4096]{1,0:T(8,128)S(1)}, f32[32,4096]{1,0:T(8,128)S(1)}, u32[]{:S(2)}, u32[]{:S(2)}) collective-permute-start(f32[32,4096]{1,0:T(8,128)S(1)} %get-tuple-element.55), channel_id=1, source_target_pairs={{0,2},{2,4},{4,6},{6,8},{8,10},{10,12},{12,14},{14,0},{1,3},{3,5},... | collective-permute-start | bytes 1572872 | tf_op jit(solution)/shard_map/ppermute | solution.py:122
  40.4 22.2 %collective-permute-start.9 = (f32[32,4096]{1,0:T(8,128)S(1)}, f32[32,4096]{1,0:T(8,128)S(1)}, u32[]{:S(2)}, u32[]{:S(2)}) collective-permute-start(f32[32,4096]{1,0:T(8,128)S(1)} %get-tuple-element.54), channel_id=1, source_target_pairs={{0,14},{2,0},{4,2},{6,4},{8,6},{10,8},{12,10},{14,12},{1,15},{3,1}... | collective-permute-start | bytes 1572872 | tf_op jit(solution)/shard_map/ppermute | solution.py:122
  51.5 44.9 %copy-start.4 = (f32[1,32,8192]{2,1,0:T(8,128)S(1)}, f32[1,32,8192]{2,1,0:T(8,128)}, u32[]{:S(2)}) copy-start(f32[1,32,8192]{2,1,0:T(8,128)} %param.12) | copy-start | bytes 3145732
  51.5 44.9 %copy-start.5 = (f32[1,32,8192]{2,1,0:T(8,128)S(1)}, f32[1,32,8192]{2,1,0:T(8,128)}, u32[]{:S(2)}) copy-start(f32[1,32,8192]{2,1,0:T(8,128)} %param.11) | copy-start | bytes 3145732
  51.5 44.9 %copy-start.6 = (f32[32,8192]{1,0:T(8,128)S(1)}, f32[32,8192]{1,0:T(8,128)}, u32[]{:S(2)}) copy-start(f32[32,8192]{1,0:T(8,128)} %anchor_ref.1) | copy-start | bytes 3145732
  51.6 44.9 %copy-start.7 = (f32[1,32,8192]{2,1,0:T(8,128)S(1)}, f32[1,32,8192]{2,1,0:T(8,128)}, u32[]{:S(2)}) copy-start(f32[1,32,8192]{2,1,0:T(8,128)} %param.10) | copy-start | bytes 3145732
  51.6 22.2 %collective-permute-start.14 = (f32[32,4096]{1,0:T(8,128)S(1)}, f32[32,4096]{1,0:T(8,128)S(1)}, u32[]{:S(2)}, u32[]{:S(2)}) collective-permute-start(f32[32,4096]{1,0:T(8,128)S(1)} %get-tuple-element.53), channel_id=1, source_target_pairs={{0,2},{2,4},{4,6},{6,8},{8,10},{10,12},{12,14},{14,0},{1,3},{3,5},... | collective-permute-start | bytes 1572872 | tf_op jit(solution)/shard_map/ppermute | solution.py:122
  51.7 22.1 %collective-permute-start.15 = (f32[32,4096]{1,0:T(8,128)S(1)}, f32[32,4096]{1,0:T(8,128)S(1)}, u32[]{:S(2)}, u32[]{:S(2)}) collective-permute-start(f32[32,4096]{1,0:T(8,128)S(1)} %get-tuple-element.52), channel_id=1, source_target_pairs={{0,14},{2,0},{4,2},{6,4},{8,6},{10,8},{12,10},{14,12},{1,15},{3,1}... | collective-permute-start | bytes 1572872 | tf_op jit(solution)/shard_map/ppermute | solution.py:122
  62.7 22.3 %collective-permute-start.12 = (f32[32,4096]{1,0:T(8,128)S(1)}, f32[32,4096]{1,0:T(8,128)S(1)}, u32[]{:S(2)}, u32[]{:S(2)}) collective-permute-start(f32[32,4096]{1,0:T(8,128)S(1)} %get-tuple-element.51), channel_id=1, source_target_pairs={{0,2},{2,4},{4,6},{6,8},{8,10},{10,12},{12,14},{14,0},{1,3},{3,5},... | collective-permute-start | bytes 1572872 | tf_op jit(solution)/shard_map/ppermute | solution.py:122
  62.8 22.2 %collective-permute-start.13 = (f32[32,4096]{1,0:T(8,128)S(1)}, f32[32,4096]{1,0:T(8,128)S(1)}, u32[]{:S(2)}, u32[]{:S(2)}) collective-permute-start(f32[32,4096]{1,0:T(8,128)S(1)} %get-tuple-element.50), channel_id=1, source_target_pairs={{0,14},{2,0},{4,2},{6,4},{8,6},{10,8},{12,10},{14,12},{1,15},{3,1}... | collective-permute-start | bytes 1572872 | tf_op jit(solution)/shard_map/ppermute | solution.py:122
  74.0 22.3 %collective-permute-start.16 = (f32[32,4096]{1,0:T(8,128)S(1)}, f32[32,4096]{1,0:T(8,128)S(1)}, u32[]{:S(2)}, u32[]{:S(2)}) collective-permute-start(f32[32,4096]{1,0:T(8,128)S(1)} %get-tuple-element.49), channel_id=1, source_target_pairs={{0,2},{2,4},{4,6},{6,8},{8,10},{10,12},{12,14},{14,0},{1,3},{3,5},... | collective-permute-start | bytes 1572872 | tf_op jit(solution)/shard_map/ppermute | solution.py:122
  74.1 22.2 %collective-permute-start.17 = (f32[32,4096]{1,0:T(8,128)S(1)}, f32[32,4096]{1,0:T(8,128)S(1)}, u32[]{:S(2)}, u32[]{:S(2)}) collective-permute-start(f32[32,4096]{1,0:T(8,128)S(1)} %get-tuple-element.48), channel_id=1, source_target_pairs={{0,14},{2,0},{4,2},{6,4},{8,6},{10,8},{12,10},{14,12},{1,15},{3,1}... | collective-permute-start | bytes 1572872 | tf_op jit(solution)/shard_map/ppermute | solution.py:122
  97.4 61.5 %copy-start.1 = (bf16[1,512,512]{2,1,0:T(8,128)(2,1)S(1)}, bf16[1,512,512]{2,1,0:T(8,128)(2,1)}, u32[]{:S(2)}) copy-start(bf16[1,512,512]{2,1,0:T(8,128)(2,1)} %param.7) | copy-start | bytes 1572868
  138.6 16.0 %copy-start.3 = (f32[16,32,512]{2,1,0:T(8,128)}, f32[16,32,512]{2,1,0:T(8,128)S(1)}, u32[]{:S(2)}) copy-start(f32[16,32,512]{2,1,0:T(8,128)S(1)} %all_to_all.16.pieces_ref) | copy-start | bytes 3145732
  139.5 15.1 %all-to-all-start.2 = ((f32[16,1,128]{2,1,0:T(1,128)}), f32[16,1,128]{2,1,0:T(1,128)S(1)}, u32[]{:S(2)}, u32[]{:S(2)}) async-start(f32[16,1,128]{2,1,0:T(1,128)} %broadcast_in_dim.32), calls=%async_computation.2 | async-start | bytes 16384 | tf_op jit(solution)/shard_map/all_to_all | solution.py:154
  154.7 0.6 copy-start.8
